TPU v7x, 256 devices: a whole 4x4x8 slice. The times are simulated.
256 devices in a mesh: seq: 8 (over z_lo, x), tensor: 32 (over z_hi, y, core).
Axes of the slice: x: 4, y: 4, z: 8 (z_hi: 4, z_lo: 2; z = z_hi * 2 + z_lo), core: 2. Of those that a mesh axis runs over, the one named last changes fastest.
Arguments:
- tokens: bfloat16 [768, 8192], P('tensor', 'seq'), may hold values from -6 to 6
- w_gate: bfloat16 [8192, 28672], P('seq', 'tensor'), may hold values from -0.109375 to 0.109375
- w_up: bfloat16 [8192, 28672], P('seq', 'tensor'), may hold values from -0.109375 to 0.109375
- w_down: bfloat16 [28672, 8192], P('tensor', 'seq'), may hold values from -0.0546875 to 0.0546875
- mask_gate: int32 [64, 224], P('seq', 'tensor'), may hold values 0 or 1
- mask_up: int32 [64, 224], P('seq', 'tensor'), may hold values 0 or 1
- mask_down: int32 [224, 64], P('tensor', 'seq'), may hold values 0 or 1
- cotangent: bfloat16 [768, 8192], P('tensor', 'seq'), may hold values from -6 to 6
Outputs:
- output: bfloat16 [768, 8192], P('tensor', 'seq')
- grad_tokens: bfloat16 [768, 8192], P('tensor', 'seq')
- grad_gate: bfloat16 [8192, 28672], P('seq', 'tensor')
- grad_up: bfloat16 [8192, 28672], P('seq', 'tensor')
- grad_down: bfloat16 [28672, 8192], P('tensor', 'seq')
All inputs are finite; a program needn't handle non-finite values. No bound on the sum of `mask_gate` or of `mask_up` or of `mask_down` on one device may be relied on, other than what follows from the above.
Results may differ from a plain program's by a relative error of at most 0.0049.
Values may be sent and summed in bfloat16 or wider, within the bound.
A program may use at most 128 MiB of HBM per device.

v0:
```python
import jax
import jax.numpy as jnp
from jax import lax
from jax.sharding import PartitionSpec as P


def widen(mask, rows):
    block = rows // mask.shape[0]
    full = jnp.repeat(jnp.repeat(mask, block, axis=0), block, axis=1)
    return full.astype(jnp.bfloat16)


def gating(summed, width):
    gate = summed[:, :width]
    up = summed[:, width:]
    sig = jax.nn.sigmoid(gate)
    act = gate * sig
    return (gate, up, sig, act)


def gate_up_grads(gate, up, sig, act, grad_hidden):
    dgate = (grad_hidden * up * sig * (1.0 + gate * (1.0 - sig))).astype(jnp.bfloat16)
    dup = (grad_hidden * act).astype(jnp.bfloat16)
    return jnp.concatenate([dgate, dup], axis=1)


def per_device(tokens, w_gate, w_up, w_down, mask_gate, mask_up, mask_down, cotangent):
    width = w_gate.shape[1]
    gate_mask = widen(mask_gate, w_gate.shape[0])
    up_mask = widen(mask_up, w_up.shape[0])
    down_mask = widen(mask_down, w_down.shape[0])
    joined = jnp.concatenate([w_gate * gate_mask, w_up * up_mask], axis=1)
    down_w = w_down * down_mask
    contract_first = (((0,), (0,)), ((), ()))
    contract_last = (((1,), (1,)), ((), ()))
    gathered = lax.all_gather(tokens, "tensor", axis=0, tiled=True)
    partial_value = jnp.dot(gathered, joined, preferred_element_type=jnp.float32)
    summed = lax.psum(partial_value, "seq")
    gate, up, sig, act = gating(summed, width)
    hidden = (act * up).astype(jnp.bfloat16)
    rows_here = hidden
    output = lax.psum_scatter(
        jnp.dot(rows_here, down_w, preferred_element_type=jnp.float32),
        "tensor",
        scatter_dimension=0,
        tiled=True,
    ).astype(jnp.bfloat16)
    cot_rows = lax.all_gather(cotangent, "tensor", axis=0, tiled=True)
    grad_part = lax.dot_general(cot_rows, down_w, contract_last, preferred_element_type=jnp.float32)
    grad_hidden = lax.psum(grad_part, "seq")
    grads = gate_up_grads(gate, up, sig, act, grad_hidden)
    rows_here = grads
    grad_tokens = lax.psum_scatter(
        lax.dot_general(rows_here, joined, contract_last, preferred_element_type=jnp.float32),
        "tensor",
        scatter_dimension=0,
        tiled=True,
    ).astype(jnp.bfloat16)
    weight_grad = lax.dot_general(
        gathered, grads, contract_first, preferred_element_type=jnp.float32
    )
    grad_gate = (weight_grad[:, :width] * gate_mask).astype(jnp.bfloat16)
    grad_up = (weight_grad[:, width:] * up_mask).astype(jnp.bfloat16)
    down_grad = lax.dot_general(
        hidden, cot_rows, contract_first, preferred_element_type=jnp.float32
    )
    grad_down = (down_grad * down_mask).astype(jnp.bfloat16)
    return (output, grad_tokens, grad_gate, grad_up, grad_down)


def solution(mesh):
    return jax.shard_map(
        per_device,
        mesh=mesh,
        in_specs=(
            P("tensor", "seq"),
            P("seq", "tensor"),
            P("seq", "tensor"),
            P("tensor", "seq"),
            P("seq", "tensor"),
            P("seq", "tensor"),
            P("tensor", "seq"),
            P("tensor", "seq"),
        ),
        out_specs=(
            P("tensor", "seq"),
            P("tensor", "seq"),
            P("seq", "tensor"),
            P("seq", "tensor"),
            P("tensor", "seq"),
        ),
        check_vma=False,
    )
```

profile of v0, /device:TPU:1, one launch (start us, length us, event | category | flops | bytes accessed | tf_op | source)
XLA Modules:
  0.0 521.2 jit_solution(15795633586915568263)
XLA Ops:
  7.2 0.0 all-gather.5.cloned.1.call-start
  7.2 0.7 all-gather.5.cloned.1.call-update
  7.9 0.0 all-gather.3.cloned.1.call-start
  7.9 0.7 all-gather.3.cloned.1.call-update
  8.6 0.0 all-reduce.3.cloned.1.call-start
  8.7 0.7 convert_element_type.66
  9.4 0.1 copy.13
  9.5 0.7 convert_element_type.69
  10.2 0.1 copy.15
  10.3 0.7 convert_element_type.73
  11.0 0.1 broadcast_bitcast_fusion
  11.0 0.1 broadcast_bitcast_fusion.1
  11.1 2.9 copy.14
  14.0 3.8 copy.16
  17.8 3.6 bitcast_multiply_fusion
  21.4 46.6 %all-gather.5.cloned.1.call-done = bf16[768,1024]{1,0:T(8,128)(2,1)} async-done(((bf16[24,1024]{1,0:T(8,128)(2,1)}), bf16[768,1024]{1,0:T(8,128)(2,1)}) %all-gather.5.cloned.1.call-update) | async-done | bytes 1572880 | tf_op jit(solution)/shard_map/all_gather | solution.py:48
  68.0 0.0 copy-start.7
  68.0 1.1 broadcast_in_dim.23
  69.2 0.0 copy-start.2
  69.2 1.3 copy-done.2
  70.4 0.0 copy-done.7
  70.4 0.0 copy-start
  70.4 4.7 convolution_bitcast_fusion.2
  75.1 45.8 %all-gather.3.cloned.1.call-done = bf16[768,1024]{1,0:T(8,128)(2,1)} async-done(((bf16[24,1024]{1,0:T(8,128)(2,1)}), bf16[768,1024]{1,0:T(8,128)(2,1)}) %all-gather.3.cloned.1.call-update) | async-done | bytes 1572880 | tf_op jit(solution)/shard_map/all_gather | solution.py:36
  120.9 0.0 copy-done
  120.9 7.5 %convolution_bitcast_fusion.1 = f32[768,1792]{0,1:T(8,128)} fusion(bf16[768,1024]{1,0:T(8,128)(2,1)} %all-gather.3.cloned.1.call-done, bf16[1024,896]{0,1:T(8,128)(2,1)S(1)} %copy-done, bf16[1024,896]{0,1:T(8,128)(2,1)} %get-tuple-element.18), kind=kOutput, calls=%fused_computation.1 | convolution fusion | flops 2825912320 | bytes 10747904 | tf_op jit(solution)/shard_map/dot_general | solution.py:37
  128.4 0.0 all-reduce.3.cloned.1.call-update
  128.4 0.0 reduce-scatter.5.cloned.1.call-start
  128.5 184.2 %all-reduce.3.cloned.1.call-done = (f32[768,1792]{0,1:T(8,128)}, f32[768,896]{0,1:T(8,128)}) async-done(((f32[768,1792]{0,1:T(8,128)}, f32[768,896]{0,1:T(8,128)}), (f32[768,1792]{0,1:T(8,128)}, f32[768,896]{0,1:T(8,128)})) %all-reduce.3.cloned.1.call-update) | async-done | bytes 8257552 | tf_op jit(solution)/shard_map/psum | solution.py:38
  312.7 0.0 copy-start.1
  312.7 4.3 multiply_convert_fusion.2
  317.0 0.0 copy-start.4
  317.0 0.0 copy-start.6
  317.0 1.1 copy-done.4
  318.1 0.5 copy-done.6
  318.5 0.0 copy-done.1
  318.5 4.8 fusion.3
  323.3 0.0 copy-start.3
  323.3 0.0 reduce-scatter.5.cloned.1.call-update
  323.3 0.2 reduce-scatter.3.cloned.1.call-start
  323.5 1.2 copy-done.3
  324.8 5.0 fusion.4
  329.8 0.0 copy-start.5
  329.8 0.0 reduce-scatter.3.cloned.1.call-update
  329.8 1.3 copy-done.5
  331.1 4.9 convolution_bitcast_fusion
  336.1 2.4 fusion
  338.5 3.8 copy.18
  342.3 2.4 copy.17
  344.7 4.9 multiply_convert_fusion
  349.6 66.6 %reduce-scatter.5.cloned.1.call-done = f32[24,1024]{1,0:T(8,128)} async-done(((f32[768,1024]{1,0:T(8,128)}), f32[24,1024]{1,0:T(8,128)}) %reduce-scatter.5.cloned.1.call-update) | async-done | bytes 98320 | tf_op jit(solution)/shard_map/reduce_scatter | solution.py:53
  416.2 1.5 convert_element_type.79
  417.7 95.4 %reduce-scatter.3.cloned.1.call-done = f32[24,1024]{1,0:T(8,128)} async-done(((f32[768,1024]{1,0:T(8,128)}), f32[24,1024]{1,0:T(8,128)}) %reduce-scatter.3.cloned.1.call-update) | async-done | bytes 98320 | tf_op jit(solution)/shard_map/reduce_scatter | solution.py:42
  513.1 1.5 convert_element_type.76
  (3 shorter events, 0.0 us)
Async XLA Ops:
  7.2 60.8 %all-gather.5.cloned.1.call-start = ((), (), s32[]{:S(2)}) async-start(), calls=%async_computation.4 | async-start | bytes 1622016 | tf_op jit(solution)/shard_map/all_gather | solution.py:48
  7.9 113.0 %all-gather.3.cloned.1.call-start = ((), (), s32[]{:S(2)}) async-start(), calls=%async_computation.2 | async-start | bytes 1622016 | tf_op jit(solution)/shard_map/all_gather | solution.py:36
  8.6 304.0 %all-reduce.3.cloned.1.call-start = ((), (), s32[]{:S(2)}) async-start(), calls=%async_computation.6 | async-start | bytes 16515072 | tf_op jit(solution)/shard_map/psum | solution.py:38
  68.0 2.4 copy-start.7
  69.2 1.3 copy-start.2
  70.4 50.5 %copy-start = (bf16[1024,896]{0,1:T(8,128)(2,1)S(1)}, bf16[1024,896]{0,1:T(8,128)(2,1)}, u32[]{:S(2)}) copy-start(bf16[1024,896]{0,1:T(8,128)(2,1)} %get-tuple-element.17) | copy-start | bytes 5505028
  128.4 287.7 %reduce-scatter.5.cloned.1.call-start = ((), (), s32[]{:S(2)}) async-start(), calls=%async_computation.5 | async-start | bytes 3244032 | tf_op jit(solution)/shard_map/reduce_scatter | solution.py:53
  312.7 5.8 %copy-start.1 = (bf16[1024,896]{0,1:T(8,128)(2,1)S(1)}, bf16[1024,896]{0,1:T(8,128)(2,1)}, u32[]{:S(2)}) copy-start(bf16[1024,896]{0,1:T(8,128)(2,1)} %get-tuple-element.18) | copy-start | bytes 5505028
  317.0 1.1 copy-start.4
  317.0 1.5 copy-start.6
  323.3 1.5 copy-start.3
  323.3 189.8 %reduce-scatter.3.cloned.1.call-start = ((), (), s32[]{:S(2)}) async-start(), calls=%async_computation.3 | async-start | bytes 3244032 | tf_op jit(solution)/shard_map/reduce_scatter | solution.py:42
  329.8 1.3 copy-start.5
Sparse Core Ops, SparseCore 0:
  10.5 57.4 all-gather.4
  70.5 50.3 all-gather.2
  128.5 184.0 all-reduce.2
  323.4 92.6 reduce-scatter.4
  419.9 93.1 reduce-scatter.2
where the time goes:
time: 523 us; the launch traced here: 521 us
  waiting for transfers between devices  440 us (84%)
  matrix products  31.8 us (6%)
  local copies, waits for them, and re-layouts  19.8 us (4%)
  other arithmetic  15.4 us (3%)
  between operations  13.9 us (3%)
    psum x1, waiting for transfers between devices, per_device(): summed = lax.psum(partial_value, 'seq')  184 us
    reduce_scatter x1, waiting for transfers between devices, per_device(): lax.psum_scatter(jnp.dot(rows_here, down_w, preferred_element_type=jnp.fl...  95.4 us
    reduce_scatter x1, waiting for transfers between devices, per_device(): lax.psum_scatter(lax.dot_general(rows_here, joined, contract_last, prefer...  66.6 us
    all_gather x1, waiting for transfers between devices, per_device(): cot_rows = lax.all_gather(cotangent, 'tensor', axis=0, tiled=True)  46.6 us
    all_gather x1, waiting for transfers between devices, per_device(): gathered = lax.all_gather(tokens, 'tensor', axis=0, tiled=True)  45.8 us
    unnamed x24, local copies, waits for them, and re-layouts  18.5 us
  transfers between devices with their start and end apart: 5, of which 5 were waited for; matrix products, arithmetic and copies ran while one was open for 8% of the time, Pallas kernels for 0%

commit v1 on v0

--- a/solution.py
+++ b/solution.py
@@ -26,6 +26,7 @@
 
 def per_device(tokens, w_gate, w_up, w_down, mask_gate, mask_up, mask_down, cotangent):
     width = w_gate.shape[1]
+    feat = tokens.shape[1]
     gate_mask = widen(mask_gate, w_gate.shape[0])
     up_mask = widen(mask_up, w_up.shape[0])
     down_mask = widen(mask_down, w_down.shape[0])
@@ -33,25 +34,28 @@
     down_w = w_down * down_mask
     contract_first = (((0,), (0,)), ((), ()))
     contract_last = (((1,), (1,)), ((), ()))
-    gathered = lax.all_gather(tokens, "tensor", axis=0, tiled=True)
+    both = lax.all_gather(
+        jnp.concatenate([tokens, cotangent], axis=1), "tensor", axis=0, tiled=True
+    )
+    gathered = both[:, :feat]
+    cot_rows = both[:, feat:]
     partial_value = jnp.dot(gathered, joined, preferred_element_type=jnp.float32)
-    summed = lax.psum(partial_value, "seq")
+    summed = lax.psum_scatter(partial_value, "seq", scatter_dimension=0, tiled=True)
     gate, up, sig, act = gating(summed, width)
-    hidden = (act * up).astype(jnp.bfloat16)
-    rows_here = hidden
+    hidden_part = (act * up).astype(jnp.bfloat16)
+    hidden = lax.all_gather(hidden_part, "seq", axis=0, tiled=True)
     output = lax.psum_scatter(
-        jnp.dot(rows_here, down_w, preferred_element_type=jnp.float32),
+        jnp.dot(hidden, down_w, preferred_element_type=jnp.float32),
         "tensor",
         scatter_dimension=0,
         tiled=True,
     ).astype(jnp.bfloat16)
-    cot_rows = lax.all_gather(cotangent, "tensor", axis=0, tiled=True)
     grad_part = lax.dot_general(cot_rows, down_w, contract_last, preferred_element_type=jnp.float32)
-    grad_hidden = lax.psum(grad_part, "seq")
-    grads = gate_up_grads(gate, up, sig, act, grad_hidden)
-    rows_here = grads
+    grad_hidden = lax.psum_scatter(grad_part, "seq", scatter_dimension=0, tiled=True)
+    grads_part = gate_up_grads(gate, up, sig, act, grad_hidden)
+    grads = lax.all_gather(grads_part, "seq", axis=0, tiled=True)
     grad_tokens = lax.psum_scatter(
-        lax.dot_general(rows_here, joined, contract_last, preferred_element_type=jnp.float32),
+        lax.dot_general(grads, joined, contract_last, preferred_element_type=jnp.float32),
         "tensor",
         scatter_dimension=0,
         tiled=True,

time: 523 us -> 489 us (0.935)
  waiting for transfers between devices: 440 us -> 408 us
    psum x1 -> x0, waiting for transfers between devices: 184 us -> none  [per_device(): summed = lax.psum(partial_value, 'seq')]
    reduce_scatter x2 -> x4, waiting for transfers between devices: 162 us -> 266 us  [the longest x1 95.6 us: per_device(): lax.psum_scatter(lax.dot_general(grads, joined, contract_last, preferred_...]
    all_gather x2 -> x3, waiting for transfers between devices: 92.4 us -> 141 us  [the longest x1 62.8 us: per_device(): lax.all_gather(jnp.concatenate([tokens, cotangent], axis=1), 'tensor', ax...]
    unnamed x24 -> x32, local copies, waits for them, and re-layouts: 18.5 us -> 10.5 us
    convert_element_type x2 -> x4, local copies, waits for them, and re-layouts: 0.19 us -> 7.15 us  [widen(): return full.astype(jnp.bfloat16)]
  transfers between devices with their start and end apart: 5 -> 7, of which waited for: 5 -> 7; matrix products, arithmetic and copies ran while one was open for 8% -> 10% of each run, Pallas kernels for 0% -> 0%
where the time goes in v1:
time: 489 us; the launch traced here: 487 us
  waiting for transfers between devices  408 us (83%)
  matrix products  30.3 us (6%)
  local copies, waits for them, and re-layouts  21.8 us (4%)
  between operations  14.3 us (3%)
  other arithmetic  13 us (3%)
    reduce_scatter x1, waiting for transfers between devices, per_device(): lax.psum_scatter(lax.dot_general(grads, joined, contract_last, preferred_...  95.6 us
    reduce_scatter x1, waiting for transfers between devices, per_device(): lax.psum_scatter(partial_value, 'seq', scatter_dimension=0, tiled=True)  74.2 us
    reduce_scatter x1, waiting for transfers between devices, per_device(): lax.psum_scatter(jnp.dot(hidden, down_w, preferred_element_type=jnp.float...  72.6 us
    all_gather x1, waiting for transfers between devices, per_device(): lax.all_gather(jnp.concatenate([tokens, cotangent], axis=1), 'tensor', ax...  62.8 us
    all_gather x1, waiting for transfers between devices, per_device(): grads = lax.all_gather(grads_part, 'seq', axis=0, tiled=True)  42.9 us
    all_gather x1, waiting for transfers between devices, per_device(): hidden = lax.all_gather(hidden_part, 'seq', axis=0, tiled=True)  35.4 us
    reduce_scatter x1, waiting for transfers between devices, per_device(): lax.psum_scatter(grad_part, 'seq', scatter_dimension=0, tiled=True)  24 us
    unnamed x32, local copies, waits for them, and re-layouts  10.5 us
  transfers between devices with their start and end apart: 7, of which 7 were waited for; matrix products, arithmetic and copies ran while one was open for 10% of the time, Pallas kernels for 0%

profile of v1, /device:TPU:1, one launch (start us, length us, event | category | flops | bytes accessed | tf_op | source)
XLA Modules:
  0.0 487.4 jit_solution(1921421634901228654)
XLA Ops:
  7.2 0.0 copy-start.11
  7.2 0.0 all-gather.4.cloned.1.call-start
  7.2 1.6 pad_maximum_fusion.4
  8.8 0.0 all-gather.4.cloned.1.call-update
  8.8 0.0 reduce-scatter.9.cloned.1.call-start
  8.9 0.7 convert_element_type.73
  9.6 62.8 %all-gather.4.cloned.1.call-done = bf16[768,2048]{1,0:T(8,128)(2,1)} async-done(((bf16[24,2048]{1,0:T(8,128)(2,1)}), bf16[768,2048]{1,0:T(8,128)(2,1)}) %all-gather.4.cloned.1.call-update) | async-done | bytes 3145744 | tf_op jit(solution)/shard_map/all_gather | solution.py:37
  72.5 1.1 broadcast_in_dim.23
  73.6 0.0 copy-start.4
  73.6 1.2 copy-done.4
  74.8 0.0 copy-done.11
  74.8 4.8 fusion.5
  79.6 0.0 reduce-scatter.9.cloned.1.call-update
  79.7 0.0 reduce-scatter.5.cloned.1.call-start
  79.7 0.6 copy-done.6
  80.3 0.1 copy.15
  80.4 0.1 broadcast_bitcast_fusion
  80.5 0.0 copy-done.7
  80.5 0.1 copy.13
  80.6 0.1 broadcast_bitcast_fusion.1
  80.7 2.9 copy.14
  83.6 3.8 copy.16
  87.4 2.1 bitcast_multiply_fusion.1
  89.5 0.0 copy-start.1
  89.5 0.0 copy-start.3
  89.5 1.2 copy-done.1
  90.7 0.6 copy-done.3
  91.3 0.0 copy-done.8
  91.3 4.8 fusion.3
  96.2 0.0 reduce-scatter.5.cloned.1.call-update
  96.2 0.0 copy-start.5
  96.2 0.0 all-gather.6.cloned.1.call-start
  96.3 24.0 %reduce-scatter.9.cloned.1.call-done = f32[96,896]{1,0:T(8,128)} async-done(((f32[768,896]{1,0:T(8,128)}), f32[96,896]{1,0:T(8,128)}) %reduce-scatter.9.cloned.1.call-update) | async-done | bytes 344080 | tf_op jit(solution)/shard_map/reduce_scatter | solution.py:54
  120.3 74.2 %reduce-scatter.5.cloned.1.call-done = f32[96,1792]{1,0:T(8,128)} async-done(((f32[768,1792]{1,0:T(8,128)}), f32[96,1792]{1,0:T(8,128)}) %reduce-scatter.5.cloned.1.call-update) | async-done | bytes 688144 | tf_op jit(solution)/shard_map/reduce_scatter | solution.py:43
  194.5 2.0 multiply_convert_fusion.2
  196.5 0.0 all-gather.6.cloned.1.call-update
  196.6 0.0 all-gather.8.cloned.1.call-start
  196.6 0.8 pad_maximum_fusion.3
  197.4 0.0 all-gather.8.cloned.1.call-update
  197.4 0.0 reduce-scatter.7.cloned.1.call-start
  197.5 35.4 %all-gather.6.cloned.1.call-done = bf16[768,896]{1,0:T(8,128)(2,1)} async-done(((bf16[96,896]{1,0:T(8,128)(2,1)}), bf16[768,896]{1,0:T(8,128)(2,1)}) %all-gather.6.cloned.1.call-update) | async-done | bytes 1376272 | tf_op jit(solution)/shard_map/all_gather | solution.py:46
  232.8 0.0 copy-done.5
  232.8 5.5 %fusion.10 = f32[768,1024]{1,0:T(8,128)} fusion(bf16[768,896]{1,0:T(8,128)(2,1)} %all-gather.6.cloned.1.call-done, bf16[896,1024]{1,0:T(8,128)(2,1)} %param.11, bf16[112,8,8,128]{3,2,1,0:T(8,128)(2,1)S(1)} %bitcast.33), kind=kOutput, calls=%fused_computation.17 | convolution fusion | flops 1410203648 | bytes 8192000 | tf_op jit(solution)/shard_map/dot_general | solution.py:48
  238.3 0.0 reduce-scatter.7.cloned.1.call-update
  238.3 0.2 reduce-scatter.11.cloned.1.call-start
  238.5 42.9 %all-gather.8.cloned.1.call-done = bf16[768,1792]{1,0:T(8,128)(2,1)} async-done(((bf16[96,1792]{1,0:T(8,128)(2,1)}), bf16[768,1792]{1,0:T(8,128)(2,1)}) %all-gather.8.cloned.1.call-update) | async-done | bytes 2752528 | tf_op jit(solution)/shard_map/all_gather | solution.py:56
  281.5 0.0 copy-done.2
  281.5 7.1 %fusion.2 = f32[768,1024]{1,0:T(8,128)} fusion(bf16[768,1792]{1,0:T(8,128)(2,1)} %all-gather.8.cloned.1.call-done, bf16[1024,896]{0,1:T(8,128)(2,1)S(1)} %copy-done.2, bf16[1024,896]{0,1:T(8,128)(2,1)} %copy-done.3), kind=kOutput, calls=%fused_computation.6 | convolution fusion | flops 2825912320 | bytes 9568256 | tf_op jit(solution)/shard_map/dot_general | solution.py:58
  288.6 0.0 reduce-scatter.11.cloned.1.call-update
  288.6 1.5 broadcast_in_dim.19
  290.1 3.1 copy.17
  293.1 1.5 broadcast_in_dim.21
  294.6 3.9 copy.18
  298.5 0.0 copy-done.12
  298.5 5.0 %multiply_convert_fusion = bf16[896,1024]{1,0:T(8,128)(2,1)} fusion(bf16[768,896]{1,0:T(8,128)(2,1)S(1)} %copy-done.12, bf16[112,8,8,128]{3,2,1,0:T(8,128)(2,1)} %bitcast.32, bf16[768,2048]{1,0:T(8,128)(2,1)} %all-gather.4.cloned.1.call-done), kind=kOutput, calls=%fused_computation.5 | convolution fusion | flops 1412038656 | bytes 6619136 | tf_op jit(solution)/shard_map/dot_general | solution.py:68
  303.5 0.0 copy-done.9
  303.5 0.0 copy-done.10
  303.5 3.1 fusion.7
  306.6 0.0 copy-done
  306.6 2.8 fusion
  309.4 72.6 %reduce-scatter.7.cloned.1.call-done = f32[24,1024]{1,0:T(8,128)} async-done(((f32[768,1024]{1,0:T(8,128)}), f32[24,1024]{1,0:T(8,128)}) %reduce-scatter.7.cloned.1.call-update) | async-done | bytes 98320 | tf_op jit(solution)/shard_map/reduce_scatter | solution.py:47
  381.9 1.5 convert_element_type.76
  383.5 95.6 %reduce-scatter.11.cloned.1.call-done = f32[24,1024]{1,0:T(8,128)} async-done(((f32[768,1024]{1,0:T(8,128)}), f32[24,1024]{1,0:T(8,128)}) %reduce-scatter.11.cloned.1.call-update) | async-done | bytes 98320 | tf_op jit(solution)/shard_map/reduce_scatter | solution.py:57
  479.1 1.5 convert_element_type.79
  (13 shorter events, 0.1 us)
Async XLA Ops:
  7.2 67.7 %copy-start.11 = (bf16[896,1024]{1,0:T(8,128)(2,1)S(1)}, bf16[896,1024]{1,0:T(8,128)(2,1)}, u32[]{:S(2)}) copy-start(bf16[896,1024]{1,0:T(8,128)(2,1)} %param.11) | copy-start | bytes 5505028
  7.2 65.2 %all-gather.4.cloned.1.call-start = ((), (), s32[]{:S(2)}) async-start(), calls=%async_computation.4 | async-start | bytes 3244032 | tf_op jit(solution)/shard_map/all_gather | solution.py:37
  8.8 111.4 %reduce-scatter.9.cloned.1.call-start = ((), (), s32[]{:S(2)}) async-start(), calls=%async_computation.8 | async-start | bytes 3096576 | tf_op jit(solution)/shard_map/reduce_scatter | solution.py:54
  73.6 1.2 copy-start.4
  79.6 0.7 copy-start.6
  79.6 0.9 copy-start.7
  79.7 114.9 %reduce-scatter.5.cloned.1.call-start = ((), (), s32[]{:S(2)}) async-start(), calls=%async_computation.5 | async-start | bytes 6193152 | tf_op jit(solution)/shard_map/reduce_scatter | solution.py:43
  87.4 3.9 copy-start.8
  89.5 1.2 copy-start.1
  89.5 1.8 copy-start.3
  96.2 136.6 %copy-start.5 = (bf16[896,8,128]{2,1,0:T(8,128)(2,1)S(1)}, bf16[896,8,128]{2,1,0:T(8,128)(2,1)}, u32[]{:S(2)}) copy-start(bf16[896,8,128]{2,1,0:T(8,128)(2,1)} %copy-done.4) | copy-start | bytes 5505028
  96.2 136.6 %all-gather.6.cloned.1.call-start = ((), (), s32[]{:S(2)}) async-start(), calls=%async_computation.6 | async-start | bytes 1548288 | tf_op jit(solution)/shard_map/all_gather | solution.py:46
  196.6 84.9 %all-gather.8.cloned.1.call-start = ((), (), s32[]{:S(2)}) async-start(), calls=%async_computation.9 | async-start | bytes 3096576 | tf_op jit(solution)/shard_map/all_gather | solution.py:56
  197.4 184.5 %reduce-scatter.7.cloned.1.call-start = ((), (), s32[]{:S(2)}) async-start(), calls=%async_computation.7 | async-start | bytes 3244032 | tf_op jit(solution)/shard_map/reduce_scatter | solution.py:47
  238.3 43.2 %copy-start.2 = (bf16[1024,896]{0,1:T(8,128)(2,1)S(1)}, bf16[1024,896]{0,1:T(8,128)(2,1)}, u32[]{:S(2)}) copy-start(bf16[1024,896]{0,1:T(8,128)(2,1)} %copy-done.1) | copy-start | bytes 5505028
  238.3 240.8 %reduce-scatter.11.cloned.1.call-start = ((), (), s32[]{:S(2)}) async-start(), calls=%async_computation.10 | async-start | bytes 3244032 | tf_op jit(solution)/shard_map/reduce_scatter | solution.py:57
  294.6 3.9 copy-start.12
  298.5 5.0 %copy-start.9 = (bf16[768,2048]{1,0:T(8,128)(2,1)S(1)}, bf16[768,2048]{1,0:T(8,128)(2,1)}, u32[]{:S(2)}) copy-start(bf16[768,2048]{1,0:T(8,128)(2,1)} %all-gather.4.cloned.1.call-done) | copy-start | bytes 9437188
  298.5 5.0 %copy-start.10 = (bf16[768,1792]{1,0:T(8,128)(2,1)S(1)}, bf16[768,1792]{1,0:T(8,128)(2,1)}, u32[]{:S(2)}) copy-start(bf16[768,1792]{1,0:T(8,128)(2,1)} %all-gather.8.cloned.1.call-done) | copy-start | bytes 8257540
  303.5 3.1 copy-start
Sparse Core Ops, SparseCore 0:
  11.1 61.2 all-gather.3
  79.8 40.4 reduce-scatter.8
  123.0 71.4 reduce-scatter.4
  196.7 36.0 all-gather.5
  234.6 46.8 all-gather.7
  285.8 96.1 reduce-scatter.6
  385.9 93.1 reduce-scatter.10

commit v2 on v1

--- a/solution.py
+++ b/solution.py
@@ -1,7 +1,89 @@
+import functools
+
 import jax
 import jax.numpy as jnp
 from jax import lax
+from jax.experimental import pallas as pl
+from jax.experimental.pallas import tpu as pltpu
 from jax.sharding import PartitionSpec as P
+
+MESH = pl.DeviceIdType.MESH
+AXES = ("seq", "tensor")
+
+
+def peer(axis, j):
+    return tuple(j if a == axis else lax.axis_index(a) for a in AXES)
+
+
+def exchange_kernel(axis, n, gather, x_ref, y_ref, send_sem, recv_sem, own_sem):
+    me = lax.axis_index(axis)
+    barrier = pltpu.get_barrier_semaphore()
+
+    def greet(k, carry):
+        j = lax.rem(me + k, n)
+        pl.semaphore_signal(barrier, inc=1, device_id=peer(axis, j), device_id_type=MESH)
+        return carry
+
+    lax.fori_loop(1, n, greet, 0)
+    pl.semaphore_wait(barrier, n - 1)
+
+    def src(j):
+        return x_ref if gather else x_ref.at[j]
+
+    def remote(j, slot):
+        return pltpu.make_async_remote_copy(
+            src_ref=src(j),
+            dst_ref=y_ref.at[slot],
+            send_sem=send_sem.at[j],
+            recv_sem=recv_sem.at[slot],
+            device_id=peer(axis, j),
+            device_id_type=MESH,
+        )
+
+    own = pltpu.make_async_copy(src(me), y_ref.at[me], own_sem)
+    own.start()
+
+    def send(k, carry):
+        remote(lax.rem(me + k, n), me).start()
+        return carry
+
+    lax.fori_loop(1, n, send, 0)
+
+    def finish(k, carry):
+        remote(lax.rem(me + k, n), me).wait_send()
+        i = lax.rem(me + n - k, n)
+        remote(i, i).wait_recv()
+        return carry
+
+    lax.fori_loop(1, n, finish, 0)
+    own.wait()
+
+
+def exchange(x, axis, n, gather, cid):
+    shape = (n,) + x.shape if gather else x.shape
+    return pl.pallas_call(
+        functools.partial(exchange_kernel, axis, n, gather),
+        out_shape=jax.ShapeDtypeStruct(shape, x.dtype),
+        in_specs=[pl.BlockSpec(memory_space=pl.ANY)],
+        out_specs=pl.BlockSpec(memory_space=pl.ANY),
+        scratch_shapes=[
+            pltpu.SemaphoreType.DMA((n,)),
+            pltpu.SemaphoreType.DMA((n,)),
+            pltpu.SemaphoreType.DMA,
+        ],
+        compiler_params=pltpu.CompilerParams(collective_id=cid, has_side_effects=True),
+    )(x)
+
+
+def gather_rows(x, axis, n, cid):
+    y = exchange(x, axis, n, True, cid)
+    return y.reshape((n * x.shape[0],) + x.shape[1:])
+
+
+def sum_scatter_rows(x, axis, n, cid):
+    rows = x.shape[0] // n
+    y = exchange(x.reshape((n, rows) + x.shape[1:]), axis, n, False, cid)
+    return jnp.sum(y, axis=0)
 
 
 def widen(mask, rows):
@@ -24,7 +106,7 @@
     return jnp.concatenate([dgate, dup], axis=1)
 
 
-def per_device(tokens, w_gate, w_up, w_down, mask_gate, mask_up, mask_down, cotangent):
+def per_device(nseq, ntensor, tokens, w_gate, w_up, w_down, mask_gate, mask_up, mask_down, cotangent):
     width = w_gate.shape[1]
     feat = tokens.shape[1]
     gate_mask = widen(mask_gate, w_gate.shape[0])
@@ -34,9 +116,7 @@
     down_w = w_down * down_mask
     contract_first = (((0,), (0,)), ((), ()))
     contract_last = (((1,), (1,)), ((), ()))
-    both = lax.all_gather(
-        jnp.concatenate([tokens, cotangent], axis=1), "tensor", axis=0, tiled=True
-    )
+    both = gather_rows(jnp.concatenate([tokens, cotangent], axis=1), "tensor", ntensor, 0)
     gathered = both[:, :feat]
     cot_rows = both[:, feat:]
     partial_value = jnp.dot(gathered, joined, preferred_element_type=jnp.float32)
@@ -44,21 +124,18 @@
     gate, up, sig, act = gating(summed, width)
     hidden_part = (act * up).astype(jnp.bfloat16)
     hidden = lax.all_gather(hidden_part, "seq", axis=0, tiled=True)
-    output = lax.psum_scatter(
-        jnp.dot(hidden, down_w, preferred_element_type=jnp.float32),
-        "tensor",
-        scatter_dimension=0,
-        tiled=True,
+    output = sum_scatter_rows(
+        jnp.dot(hidden, down_w, preferred_element_type=jnp.float32), "tensor", ntensor, 1
     ).astype(jnp.bfloat16)
     grad_part = lax.dot_general(cot_rows, down_w, contract_last, preferred_element_type=jnp.float32)
     grad_hidden = lax.psum_scatter(grad_part, "seq", scatter_dimension=0, tiled=True)
     grads_part = gate_up_grads(gate, up, sig, act, grad_hidden)
     grads = lax.all_gather(grads_part, "seq", axis=0, tiled=True)
-    grad_tokens = lax.psum_scatter(
+    grad_tokens = sum_scatter_rows(
         lax.dot_general(grads, joined, contract_last, preferred_element_type=jnp.float32),
         "tensor",
-        scatter_dimension=0,
-        tiled=True,
+        ntensor,
+        2,
     ).astype(jnp.bfloat16)
     weight_grad = lax.dot_general(
         gathered, grads, contract_first, preferred_element_type=jnp.float32
@@ -74,7 +151,7 @@
 
 def solution(mesh):
     return jax.shard_map(
-        per_device,
+        functools.partial(per_device, mesh.shape["seq"], mesh.shape["tensor"]),
         mesh=mesh,
         in_specs=(
             P("tensor", "seq"),

time: 489 us -> 496 us (1.014)
  waiting for transfers between devices: 408 us -> 135 us
  Pallas kernels: 0 us -> 271 us
    pallas_call x0 -> x3, Pallas kernels: none -> 271 us  [exchange(): pl.pallas_call(functools.partial(exchange_kernel, axis, n, gather), out_s...]
    reduce_scatter x2 -> x0, waiting for transfers between devices: 168 us -> none  [the longest x1 95.6 us: per_device(): lax.psum_scatter(lax.dot_general(grads, joined, contract_last, preferred_...]
    all_gather x1 -> x0, waiting for transfers between devices: 62.8 us -> none  [per_device(): lax.all_gather(jnp.concatenate([tokens, cotangent], axis=1), 'tensor', ax...]
    all_gather x1, waiting for transfers between devices: 42.9 us -> 0.01 us  [per_device(): grads = lax.all_gather(grads_part, 'seq', axis=0, tiled=True)]
    reduce_scatter x1, waiting for transfers between devices: 24 us -> 35 us  [per_device(): lax.psum_scatter(grad_part, 'seq', scatter_dimension=0, tiled=True)]
    all_gather x1, waiting for transfers between devices: 35.4 us -> 25.4 us  [per_device(): hidden = lax.all_gather(hidden_part, 'seq', axis=0, tiled=True)]
    reduce_sum x0 -> x2, other arithmetic: none -> 5.48 us  [sum_scatter_rows(): return jnp.sum(y, axis=0)]
    unnamed x32 -> x26, local copies, waits for them, and re-layouts: 10.5 us -> 10.6 us
  transfers between devices with their start and end apart: 7 -> 4, of which waited for: 7 -> 3; matrix products, arithmetic and copies ran while one was open for 10% -> 8% of each run, Pallas kernels for 0% -> 21%
where the time goes in v2:
time: 496 us; the launch traced here: 490 us
  Pallas kernels  271 us (55%)
  waiting for transfers between devices  135 us (27%)
  matrix products  33.6 us (7%)
  local copies, waits for them, and re-layouts  21.7 us (4%)
  other arithmetic  14.4 us (3%)
  between operations  13.9 us (3%)
    pallas_call x3, Pallas kernels, exchange(): pl.pallas_call(functools.partial(exchange_kernel, axis, n, gather), out_s...  271 us
    reduce_scatter x1, waiting for transfers between devices, per_device(): lax.psum_scatter(partial_value, 'seq', scatter_dimension=0, tiled=True)  74.3 us
    reduce_scatter x1, waiting for transfers between devices, per_device(): lax.psum_scatter(grad_part, 'seq', scatter_dimension=0, tiled=True)  35 us
    all_gather x1, waiting for transfers between devices, per_device(): hidden = lax.all_gather(hidden_part, 'seq', axis=0, tiled=True)  25.4 us
    unnamed x26, local copies, waits for them, and re-layouts  10.6 us
  transfers between devices with their start and end apart: 4, of which 3 were waited for; matrix products, arithmetic and copies ran while one was open for 8% of the time, Pallas kernels for 21%

profile of v2, /device:TPU:1, one launch (start us, length us, event | category | flops | bytes accessed | tf_op | source)
XLA Modules:
  0.0 490.3 jit_solution(15126199191833409659)
XLA Ops:
  7.2 0.0 copy-start.5
  7.2 0.0 reduce-scatter.5.cloned.1.call-start
  7.2 1.5 pad_maximum_fusion.4.x_ref
  8.7 84.0 %shard_map.119 = bf16[32,24,2048]{2,1,0:T(8,128)(2,1)} custom-call(bf16[24,2048]{1,0:T(8,128)(2,1)} %pad_maximum_fusion.4.x_ref), custom_call_target="tpu_custom_call" | custom-call | tf_op jit(solution)/shard_map/pallas_call | solution.py:64
  92.7 0.0 copy-done.5
  92.7 0.0 copy-start.8
  92.8 1.1 broadcast_in_dim.23
  93.9 0.0 copy-start.4
  93.9 1.2 copy-done.4
  95.1 0.0 copy-done.8
  95.2 4.8 fusion.5
  99.9 0.0 copy-start.6
  99.9 0.0 copy-start.7
  99.9 0.0 reduce-scatter.5.cloned.1.call-update
  100.0 0.0 reduce-scatter.3.cloned.1.call-start
  100.0 0.6 copy-done.6
  100.6 0.1 copy.15
  100.7 0.1 broadcast_bitcast_fusion
  100.8 0.0 copy-done.7
  100.8 0.1 copy.13
  100.9 0.1 broadcast_bitcast_fusion.1
  101.0 2.9 copy.14
  103.9 3.8 copy.16
  107.7 0.0 copy-start.1
  107.7 1.9 bitcast_multiply_fusion.1
  109.6 0.0 copy-start.2
  109.6 0.0 copy-start.3
  109.6 1.2 copy-done.2
  110.8 0.7 copy-done.3
  111.5 0.0 copy-done.1
  111.5 4.9 %fusion.3 = f32[768,1792]{1,0:T(8,128)} fusion(bf16[1024,896]{0,1:T(8,128)(2,1)S(1)} %get-tuple-element.10, bf16[1024,896]{0,1:T(8,128)(2,1)S(1)} %get-tuple-element.11, bf16[768,2048]{1,0:T(8,128)(2,1)S(1)} %bitcast.37), kind=kOutput, calls=%fused_computation.7 | convolution fusion | flops 2825912320 | bytes 10747904 | tf_op jit(solution)/shard_map/dot_general | solution.py:122
  116.4 0.0 reduce-scatter.3.cloned.1.call-update
  116.4 0.0 all-gather.3.cloned.1.call-start
  116.5 35.0 %reduce-scatter.5.cloned.1.call-done = f32[96,896]{1,0:T(8,128)} async-done(((f32[768,896]{1,0:T(8,128)}), f32[96,896]{1,0:T(8,128)}) %reduce-scatter.5.cloned.1.call-update) | async-done | bytes 344080 | tf_op jit(solution)/shard_map/reduce_scatter | solution.py:131
  151.5 74.3 %reduce-scatter.3.cloned.1.call-done = f32[96,1792]{1,0:T(8,128)} async-done(((f32[768,1792]{1,0:T(8,128)}), f32[96,1792]{1,0:T(8,128)}) %reduce-scatter.3.cloned.1.call-update) | async-done | bytes 688144 | tf_op jit(solution)/shard_map/reduce_scatter | solution.py:123
  225.9 2.0 multiply_convert_fusion.2
  227.9 0.0 all-gather.3.cloned.1.call-update
  227.9 0.2 all-gather.5.cloned.1.call-start
  228.2 0.8 pad_maximum_fusion.3
  228.9 0.0 all-gather.5.cloned.1.call-update
  229.0 1.5 broadcast_in_dim.19
  230.4 3.1 copy.17
  233.5 1.5 broadcast_in_dim.21
  234.9 3.8 copy.18
  238.7 25.4 %all-gather.3.cloned.1.call-done = bf16[768,896]{1,0:T(8,128)(2,1)} async-done(((bf16[96,896]{1,0:T(8,128)(2,1)}), bf16[768,896]{1,0:T(8,128)(2,1)}) %all-gather.3.cloned.1.call-update) | async-done | bytes 1376272 | tf_op jit(solution)/shard_map/all_gather | solution.py:126
  264.2 6.0 %fusion.10 = f32[768,1024]{1,0:T(8,128)} fusion(bf16[768,896]{1,0:T(8,128)(2,1)} %all-gather.3.cloned.1.call-done, bf16[896,1024]{1,0:T(8,128)(2,1)} %param.11, bf16[112,8,8,128]{3,2,1,0:T(8,128)(2,1)} %bitcast.41), kind=kOutput, calls=%fused_computation.17 | convolution fusion | flops 1410203648 | bytes 8192000 | tf_op jit(solution)/shard_map/dot_general | solution.py:128
  270.2 101.1 %shard_map.120 = f32[32,24,1024]{2,1,0:T(8,128)} custom-call(f32[32,24,1024]{2,1,0:T(8,128)} %bitcast.39), custom_call_target="tpu_custom_call" | custom-call | tf_op jit(solution)/shard_map/pallas_call | solution.py:64
  371.3 0.0 copy-start.9
  371.3 2.8 reduce_sum.18
  374.1 0.0 copy-done.9
  374.1 4.8 multiply_convert_fusion
  379.0 0.0 all-gather.5.cloned.1.call-done
  379.0 7.5 %fusion.2 = f32[768,1024]{1,0:T(8,128)} fusion(bf16[768,1792]{1,0:T(8,128)(2,1)} %all-gather.5.cloned.1.call-done, bf16[1024,896]{0,1:T(8,128)(2,1)} %copy-done.2, bf16[1024,896]{0,1:T(8,128)(2,1)} %copy-done.3), kind=kOutput, calls=%fused_computation.6 | convolution fusion | flops 2825912320 | bytes 9568256 | tf_op jit(solution)/shard_map/dot_general | solution.py:135
  386.5 86.3 %shard_map.121 = f32[32,24,1024]{2,1,0:T(8,128)} custom-call(f32[32,24,1024]{2,1,0:T(8,128)} %bitcast.38), custom_call_target="tpu_custom_call" | custom-call | tf_op jit(solution)/shard_map/pallas_call | solution.py:64
  472.8 2.7 reduce_sum.19
  475.5 0.0 copy-start
  475.5 5.6 %fusion.7 = f32[1024,1792]{1,0:T(8,128)S(1)} fusion(bf16[768,1792]{1,0:T(8,128)(2,1)} %all-gather.5.cloned.1.call-done, bf16[768,2048]{1,0:T(8,128)(2,1)} %bitcast.36), kind=kOutput, calls=%fused_computation.12 | convolution fusion | flops 2818572288 | bytes 11665408 | tf_op jit(solution)/shard_map/dot_general | solution.py:140
  481.0 0.0 copy-done
  481.0 2.8 fusion
  (6 shorter events, 0.1 us)
Async XLA Ops:
  7.2 85.6 %copy-start.5 = (s32[7,8]{1,0:T(8,128)S(1)}, s32[7,8]{1,0:T(8,128)}, u32[]{:S(2)}) copy-start(s32[7,8]{1,0:T(8,128)} %param.14) | copy-start | bytes 676
  7.2 144.4 %reduce-scatter.5.cloned.1.call-start = ((), (), s32[]{:S(2)}) async-start(), calls=%async_computation.4 | async-start | bytes 3096576 | tf_op jit(solution)/shard_map/reduce_scatter | solution.py:131
  92.7 2.4 copy-start.8
  93.9 1.2 copy-start.4
  99.9 0.7 copy-start.6
  99.9 0.9 copy-start.7
  100.0 125.9 %reduce-scatter.3.cloned.1.call-start = ((), (), s32[]{:S(2)}) async-start(), calls=%async_computation.2 | async-start | bytes 6193152 | tf_op jit(solution)/shard_map/reduce_scatter | solution.py:123
  107.7 3.8 copy-start.1
  109.6 1.2 copy-start.2
  109.6 1.9 copy-start.3
  116.4 147.7 %all-gather.3.cloned.1.call-start = ((), (), s32[]{:S(2)}) async-start(), calls=%async_computation.3 | async-start | bytes 1548288 | tf_op jit(solution)/shard_map/all_gather | solution.py:126
  227.9 151.0 %all-gather.5.cloned.1.call-start = ((), (), s32[]{:S(2)}) async-start(), calls=%async_computation.5 | async-start | bytes 3096576 | tf_op jit(solution)/shard_map/all_gather | solution.py:133
  371.3 2.8 copy-start.9
  475.5 5.6 %copy-start = (bf16[1024,896]{1,0:T(8,128)(2,1)S(1)}, bf16[1024,896]{1,0:T(8,128)(2,1)}, u32[]{:S(2)}) copy-start(bf16[1024,896]{1,0:T(8,128)(2,1)} %copy.18) | copy-start | bytes 5505028
Sparse Core Ops, SparseCore 0:
  100.1 51.4 reduce-scatter.4
  154.3 71.5 reduce-scatter.2
  228.1 36.0 all-gather.2
  265.9 105.9 all-gather.4

commit v3 on v2

--- a/solution.py
+++ b/solution.py
@@ -1,6 +1,7 @@
 import functools
 
 import jax
+import numpy as np
 import jax.numpy as jnp
 from jax import lax
 from jax.experimental import pallas as pl
@@ -15,13 +16,18 @@
     return tuple(j if a == axis else lax.axis_index(a) for a in AXES)
 
 
-def exchange_kernel(axis, n, gather, x_ref, y_ref, send_sem, recv_sem, own_sem):
-    me = lax.axis_index(axis)
+def exchange_kernel(axis, n, stride, gather, x_ref, y_ref, send_sem, recv_sem, own_sem):
+    index = lax.axis_index(axis)
+    me = lax.rem(index // stride, n)
+    base = index - me * stride
     barrier = pltpu.get_barrier_semaphore()
+
+    def device(j):
+        return peer(axis, base + j * stride)
 
     def greet(k, carry):
         j = lax.rem(me + k, n)
-        pl.semaphore_signal(barrier, inc=1, device_id=peer(axis, j), device_id_type=MESH)
+        pl.semaphore_signal(barrier, inc=1, device_id=device(j), device_id_type=MESH)
         return carry
 
     lax.fori_loop(1, n, greet, 0)
@@ -36,7 +42,7 @@
             dst_ref=y_ref.at[slot],
             send_sem=send_sem.at[j],
             recv_sem=recv_sem.at[slot],
-            device_id=peer(axis, j),
+            device_id=device(j),
             device_id_type=MESH,
         )
 
@@ -59,10 +65,19 @@
     own.wait()
 
 
-def exchange(x, axis, n, gather, cid):
+class Ids:
+    def __init__(self):
+        self.next = 0
+
+    def take(self):
+        self.next += 1
+        return self.next - 1
+
+
+def exchange(x, axis, n, stride, gather, cid):
     shape = (n,) + x.shape if gather else x.shape
     return pl.pallas_call(
-        functools.partial(exchange_kernel, axis, n, gather),
+        functools.partial(exchange_kernel, axis, n, stride, gather),
         out_shape=jax.ShapeDtypeStruct(shape, x.dtype),
         in_specs=[pl.BlockSpec(memory_space=pl.ANY)],
         out_specs=pl.BlockSpec(memory_space=pl.ANY),
@@ -75,15 +90,17 @@
     )(x)
 
 
-def gather_rows(x, axis, n, cid):
-    y = exchange(x, axis, n, True, cid)
-    return y.reshape((n * x.shape[0],) + x.shape[1:])
-
-
-def sum_scatter_rows(x, axis, n, cid):
-    rows = x.shape[0] // n
-    y = exchange(x.reshape((n, rows) + x.shape[1:]), axis, n, False, cid)
-    return jnp.sum(y, axis=0)
+def gather_rows(x, axis, digits, ids):
+    for n, stride in digits:
+        x = exchange(x, axis, n, stride, True, ids.take())
+    return x.reshape((-1,) + x.shape[-1:])
+
+
+def sum_scatter_rows(x, axis, digits, ids):
+    for n, stride in reversed(digits):
+        x = x.reshape((n, -1) + x.shape[-1:])
+        x = jnp.sum(exchange(x, axis, n, stride, False, ids.take()), axis=0)
+    return x
 
 
 def widen(mask, rows):
@@ -106,7 +123,7 @@
     return jnp.concatenate([dgate, dup], axis=1)
 
 
-def per_device(nseq, ntensor, tokens, w_gate, w_up, w_down, mask_gate, mask_up, mask_down, cotangent):
+def per_device(tensor_digits, tokens, w_gate, w_up, w_down, mask_gate, mask_up, mask_down, cotangent):
     width = w_gate.shape[1]
     feat = tokens.shape[1]
     gate_mask = widen(mask_gate, w_gate.shape[0])
@@ -116,7 +133,8 @@
     down_w = w_down * down_mask
     contract_first = (((0,), (0,)), ((), ()))
     contract_last = (((1,), (1,)), ((), ()))
-    both = gather_rows(jnp.concatenate([tokens, cotangent], axis=1), "tensor", ntensor, 0)
+    ids = Ids()
+    both = gather_rows(jnp.concatenate([tokens, cotangent], axis=1), "tensor", tensor_digits, ids)
     gathered = both[:, :feat]
     cot_rows = both[:, feat:]
     partial_value = jnp.dot(gathered, joined, preferred_element_type=jnp.float32)
@@ -125,7 +143,7 @@
     hidden_part = (act * up).astype(jnp.bfloat16)
     hidden = lax.all_gather(hidden_part, "seq", axis=0, tiled=True)
     output = sum_scatter_rows(
-        jnp.dot(hidden, down_w, preferred_element_type=jnp.float32), "tensor", ntensor, 1
+        jnp.dot(hidden, down_w, preferred_element_type=jnp.float32), "tensor", tensor_digits, ids
     ).astype(jnp.bfloat16)
     grad_part = lax.dot_general(cot_rows, down_w, contract_last, preferred_element_type=jnp.float32)
     grad_hidden = lax.psum_scatter(grad_part, "seq", scatter_dimension=0, tiled=True)
@@ -134,8 +152,8 @@
     grad_tokens = sum_scatter_rows(
         lax.dot_general(grads, joined, contract_last, preferred_element_type=jnp.float32),
         "tensor",
-        ntensor,
-        2,
+        tensor_digits,
+        ids,
     ).astype(jnp.bfloat16)
     weight_grad = lax.dot_general(
         gathered, grads, contract_first, preferred_element_type=jnp.float32
@@ -149,9 +167,42 @@
     return (output, grad_tokens, grad_gate, grad_up, grad_down)
 
 
+def axis_parts(mesh, axis):
+    n = mesh.shape[axis]
+    line = np.moveaxis(mesh.devices, mesh.axis_names.index(axis), -1).reshape(-1, n)[0]
+    try:
+        keys = [tuple(d.coords) + (d.core_on_chip,) for d in line]
+    except AttributeError:
+        return [n]
+    parts, stride = [], 1
+    while stride < n:
+        changed = [c for c in range(len(keys[0])) if keys[stride][c] != keys[0][c]]
+        size = 1
+        while stride * size < n:
+            moved = [c for c in range(len(keys[0])) if keys[stride * size][c] != keys[0][c]]
+            if moved != changed:
+                break
+            size += 1
+        if (n // stride) % size:
+            return [n]
+        parts.append(size)
+        stride *= size
+    return parts[::-1]
+
+
+def digits_of(mesh, axis):
+    sizes = axis_parts(mesh, axis)
+    digits, stride = [], 1
+    for n in reversed(sizes):
+        if n > 1:
+            digits.append((n, stride))
+        stride *= n
+    return tuple(reversed(digits))
+
+
 def solution(mesh):
     return jax.shard_map(
-        functools.partial(per_device, mesh.shape["seq"], mesh.shape["tensor"]),
+        functools.partial(per_device, digits_of(mesh, "tensor")),
         mesh=mesh,
         in_specs=(
             P("tensor", "seq"),

time: 496 us -> 484 us (0.976)
  other arithmetic: 14.4 us -> 23.9 us
  Pallas kernels: 271 us -> 262 us
  waiting for transfers between devices: 135 us -> 127 us
    pallas_call x3 -> x9, Pallas kernels: 271 us -> 262 us  [exchange(): pl.pallas_call(functools.partial(exchange_kernel, axis, n, stride, gather...]
    reduce_sum x2 -> x6, other arithmetic: 5.48 us -> 14.9 us  [sum_scatter_rows(): x = jnp.sum(exchange(x, axis, n, stride, False, ids.take()), axis=0)]
    reduce_scatter x1, waiting for transfers between devices: 35 us -> 27 us  [per_device(): lax.psum_scatter(grad_part, 'seq', scatter_dimension=0, tiled=True)]
  transfers between devices with their start and end apart: 4 -> 4, of which waited for: 3 -> 3; matrix products, arithmetic and copies ran while one was open for 8% -> 9% of each run, Pallas kernels for 21% -> 18%
where the time goes in v3:
time: 484 us; the launch traced here: 482 us
  Pallas kernels  262 us (54%)
  waiting for transfers between devices  127 us (26%)
  matrix products  33.6 us (7%)
  other arithmetic  23.9 us (5%)
  local copies, waits for them, and re-layouts  21.7 us (4%)
  between operations  14 us (3%)
    pallas_call x9, Pallas kernels, exchange(): pl.pallas_call(functools.partial(exchange_kernel, axis, n, stride, gather...  262 us
    reduce_scatter x1, waiting for transfers between devices, per_device(): lax.psum_scatter(partial_value, 'seq', scatter_dimension=0, tiled=True)  74 us
    reduce_scatter x1, waiting for transfers between devices, per_device(): lax.psum_scatter(grad_part, 'seq', scatter_dimension=0, tiled=True)  27 us
    all_gather x1, waiting for transfers between devices, per_device(): hidden = lax.all_gather(hidden_part, 'seq', axis=0, tiled=True)  25.4 us
    reduce_sum x6, other arithmetic, sum_scatter_rows(): x = jnp.sum(exchange(x, axis, n, stride, False, ids.take()), axis=0)  14.9 us
    unnamed x26, local copies, waits for them, and re-layouts  10.5 us
  transfers between devices with their start and end apart: 4, of which 3 were waited for; matrix products, arithmetic and copies ran while one was open for 9% of the time, Pallas kernels for 18%

profile of v3, /device:TPU:1, one launch (start us, length us, event | category | flops | bytes accessed | tf_op | source)
XLA Modules:
  0.0 481.8 jit_solution(16271638163908363201)
XLA Ops:
  7.2 0.0 reduce-scatter.5.cloned.1.call-start
  7.2 1.5 pad_maximum_fusion.4.x_ref
  8.7 16.0 %shard_map.119.x_ref = bf16[4,24,2048]{2,1,0:T(8,128)(2,1)} custom-call(bf16[24,2048]{1,0:T(8,128)(2,1)} %pad_maximum_fusion.4.x_ref), custom_call_target="tpu_custom_call" | custom-call | tf_op jit(solution)/shard_map/pallas_call | solution.py:79
  24.7 20.8 %shard_map.120.x_ref = bf16[4,4,24,2048]{3,2,1,0:T(8,128)(2,1)} custom-call(bf16[4,24,2048]{2,1,0:T(8,128)(2,1)} %shard_map.119.x_ref), custom_call_target="tpu_custom_call" | custom-call | tf_op jit(solution)/shard_map/pallas_call | solution.py:79
  45.5 0.0 copy-start.5
  45.5 51.2 %shard_map.121 = bf16[2,4,4,24,2048]{4,3,2,1,0:T(8,128)(2,1)} custom-call(bf16[4,4,24,2048]{3,2,1,0:T(8,128)(2,1)} %shard_map.120.x_ref), custom_call_target="tpu_custom_call" | custom-call | tf_op jit(solution)/shard_map/pallas_call | solution.py:79
  96.7 0.0 copy-done.5
  96.7 0.0 copy-start.8
  96.8 1.1 broadcast_in_dim.23
  97.9 0.0 copy-start.4
  97.9 1.2 copy-done.4
  99.1 0.0 copy-done.8
  99.1 4.8 fusion.5
  103.9 0.0 reduce-scatter.5.cloned.1.call-update
  103.9 0.0 reduce-scatter.3.cloned.1.call-start
  104.0 0.6 copy-done.6
  104.6 0.1 copy.15
  104.7 0.1 broadcast_bitcast_fusion
  104.8 0.0 copy-done.7
  104.8 0.1 copy.13
  104.9 0.1 broadcast_bitcast_fusion.1
  105.0 2.9 copy.14
  107.9 3.8 copy.16
  111.6 1.9 bitcast_multiply_fusion.1
  113.6 0.0 copy-start.2
  113.6 0.0 copy-start.3
  113.6 1.2 copy-done.2
  114.8 0.6 copy-done.3
  115.4 0.0 copy-done.1
  115.4 4.9 %fusion.3 = f32[768,1792]{1,0:T(8,128)} fusion(bf16[1024,896]{0,1:T(8,128)(2,1)S(1)} %get-tuple-element.10, bf16[1024,896]{0,1:T(8,128)(2,1)S(1)} %get-tuple-element.11, bf16[768,2048]{1,0:T(8,128)(2,1)S(1)} %bitcast.43), kind=kOutput, calls=%fused_computation.7 | convolution fusion | flops 2825912320 | bytes 10747904 | tf_op jit(solution)/shard_map/dot_general | solution.py:140
  120.3 0.0 reduce-scatter.3.cloned.1.call-update
  120.3 0.0 all-gather.3.cloned.1.call-start
  120.4 27.0 %reduce-scatter.5.cloned.1.call-done = f32[96,896]{1,0:T(8,128)} async-done(((f32[768,896]{1,0:T(8,128)}), f32[96,896]{1,0:T(8,128)}) %reduce-scatter.5.cloned.1.call-update) | async-done | bytes 344080 | tf_op jit(solution)/shard_map/reduce_scatter | solution.py:149
  147.4 74.0 %reduce-scatter.3.cloned.1.call-done = f32[96,1792]{1,0:T(8,128)} async-done(((f32[768,1792]{1,0:T(8,128)}), f32[96,1792]{1,0:T(8,128)}) %reduce-scatter.3.cloned.1.call-update) | async-done | bytes 688144 | tf_op jit(solution)/shard_map/reduce_scatter | solution.py:141
  221.4 2.0 multiply_convert_fusion.2
  223.5 0.0 all-gather.3.cloned.1.call-update
  223.5 0.2 all-gather.5.cloned.1.call-start
  223.7 0.8 pad_maximum_fusion.3
  224.5 0.0 all-gather.5.cloned.1.call-update
  224.5 1.5 broadcast_in_dim.19
  226.0 3.1 copy.17
  229.1 1.5 broadcast_in_dim.21
  230.5 3.8 copy.18
  234.3 25.4 %all-gather.3.cloned.1.call-done = bf16[768,896]{1,0:T(8,128)(2,1)} async-done(((bf16[96,896]{1,0:T(8,128)(2,1)}), bf16[768,896]{1,0:T(8,128)(2,1)}) %all-gather.3.cloned.1.call-update) | async-done | bytes 1376272 | tf_op jit(solution)/shard_map/all_gather | solution.py:144
  259.7 6.0 %fusion.10 = f32[768,1024]{1,0:T(8,128)} fusion(bf16[768,896]{1,0:T(8,128)(2,1)} %all-gather.3.cloned.1.call-done, bf16[896,1024]{1,0:T(8,128)(2,1)} %param.11, bf16[112,8,8,128]{3,2,1,0:T(8,128)(2,1)} %bitcast.47), kind=kOutput, calls=%fused_computation.17 | convolution fusion | flops 1410203648 | bytes 8192000 | tf_op jit(solution)/shard_map/dot_general | solution.py:146
  265.8 54.7 %shard_map.122 = f32[2,384,1024]{2,1,0:T(8,128)} custom-call(f32[2,384,1024]{2,1,0:T(8,128)} %bitcast.45), custom_call_target="tpu_custom_call" | custom-call | tf_op jit(solution)/shard_map/pallas_call | solution.py:79
  320.5 3.5 reduce_sum.54
  324.0 21.7 %shard_map.123 = f32[4,96,1024]{2,1,0:T(8,128)} custom-call(f32[4,96,1024]{2,1,0:T(8,128)} %bitcast.38), custom_call_target="tpu_custom_call" | custom-call | tf_op jit(solution)/shard_map/pallas_call | solution.py:79
  345.7 0.0 copy-start.9
  345.7 2.4 reduce_sum.55
  348.1 12.0 %shard_map.124 = f32[4,24,1024]{2,1,0:T(8,128)} custom-call(f32[4,24,1024]{2,1,0:T(8,128)} %bitcast.49), custom_call_target="tpu_custom_call" | custom-call | tf_op jit(solution)/shard_map/pallas_call | solution.py:79
  360.1 1.7 reduce_sum.56
  361.8 0.0 copy-done.9
  361.8 4.8 %multiply_convert_fusion = bf16[896,1024]{1,0:T(8,128)(2,1)} fusion(bf16[768,896]{1,0:T(8,128)(2,1)S(1)} %copy-done.9, bf16[112,8,8,128]{3,2,1,0:T(8,128)(2,1)} %bitcast.48, bf16[768,2048]{1,0:T(8,128)(2,1)} %bitcast.41), kind=kOutput, calls=%fused_computation.5 | convolution fusion | flops 1412038656 | bytes 6619136 | tf_op jit(solution)/shard_map/dot_general | solution.py:163
  366.6 7.5 %fusion.2 = f32[768,1024]{1,0:T(8,128)} fusion(bf16[768,1792]{1,0:T(8,128)(2,1)} %all-gather.5.cloned.1.call-done, bf16[1024,896]{0,1:T(8,128)(2,1)} %copy-done.2, bf16[1024,896]{0,1:T(8,128)(2,1)} %copy-done.3), kind=kOutput, calls=%fused_computation.6 | convolution fusion | flops 2825912320 | bytes 9568256 | tf_op jit(solution)/shard_map/dot_general | solution.py:153
  374.2 51.0 %shard_map.125 = f32[2,384,1024]{2,1,0:T(8,128)} custom-call(f32[2,384,1024]{2,1,0:T(8,128)} %bitcast.44), custom_call_target="tpu_custom_call" | custom-call | tf_op jit(solution)/shard_map/pallas_call | solution.py:79
  425.1 3.5 reduce_sum.57
  428.6 21.2 %shard_map.126 = f32[4,96,1024]{2,1,0:T(8,128)} custom-call(f32[4,96,1024]{2,1,0:T(8,128)} %bitcast.39), custom_call_target="tpu_custom_call" | custom-call | tf_op jit(solution)/shard_map/pallas_call | solution.py:79
  449.8 2.3 reduce_sum.58
  452.1 13.2 %shard_map.127 = f32[4,24,1024]{2,1,0:T(8,128)} custom-call(f32[4,24,1024]{2,1,0:T(8,128)} %bitcast.50), custom_call_target="tpu_custom_call" | custom-call | tf_op jit(solution)/shard_map/pallas_call | solution.py:79
  465.3 1.7 reduce_sum.59
  467.0 5.6 %fusion.7 = f32[1024,1792]{1,0:T(8,128)S(1)} fusion(bf16[768,1792]{1,0:T(8,128)(2,1)} %all-gather.5.cloned.1.call-done, bf16[768,2048]{1,0:T(8,128)(2,1)} %bitcast.42), kind=kOutput, calls=%fused_computation.12 | convolution fusion | flops 2818572288 | bytes 11665408 | tf_op jit(solution)/shard_map/dot_general | solution.py:158
  472.5 0.0 copy-done
  472.5 2.8 fusion
  (11 shorter events, 0.1 us)
Async XLA Ops:
  7.2 140.3 %reduce-scatter.5.cloned.1.call-start = ((), (), s32[]{:S(2)}) async-start(), calls=%async_computation.4 | async-start | bytes 3096576 | tf_op jit(solution)/shard_map/reduce_scatter | solution.py:149
  45.5 51.2 %copy-start.5 = (s32[7,8]{1,0:T(8,128)S(1)}, s32[7,8]{1,0:T(8,128)}, u32[]{:S(2)}) copy-start(s32[7,8]{1,0:T(8,128)} %param.14) | copy-start | bytes 676
  96.7 2.4 copy-start.8
  97.9 1.2 copy-start.4
  103.9 0.7 copy-start.6
  103.9 0.9 copy-start.7
  103.9 117.5 %reduce-scatter.3.cloned.1.call-start = ((), (), s32[]{:S(2)}) async-start(), calls=%async_computation.2 | async-start | bytes 6193152 | tf_op jit(solution)/shard_map/reduce_scatter | solution.py:141
  111.6 3.8 copy-start.1
  113.6 1.2 copy-start.2
  113.6 1.8 copy-start.3
  120.3 139.4 %all-gather.3.cloned.1.call-start = ((), (), s32[]{:S(2)}) async-start(), calls=%async_computation.3 | async-start | bytes 1548288 | tf_op jit(solution)/shard_map/all_gather | solution.py:144
  223.5 143.1 %all-gather.5.cloned.1.call-start = ((), (), s32[]{:S(2)}) async-start(), calls=%async_computation.5 | async-start | bytes 3096576 | tf_op jit(solution)/shard_map/all_gather | solution.py:151
  345.7 16.1 %copy-start.9 = (bf16[768,896]{1,0:T(8,128)(2,1)S(1)}, bf16[768,896]{1,0:T(8,128)(2,1)}, u32[]{:S(2)}) copy-start(bf16[768,896]{1,0:T(8,128)(2,1)} %all-gather.3.cloned.1.call-done) | copy-start | bytes 4128772
  467.0 5.6 %copy-start = (bf16[1024,896]{1,0:T(8,128)(2,1)S(1)}, bf16[1024,896]{1,0:T(8,128)(2,1)}, u32[]{:S(2)}) copy-start(bf16[1024,896]{1,0:T(8,128)(2,1)} %copy.18) | copy-start | bytes 5505028
Sparse Core Ops, SparseCore 0:
  104.0 43.3 reduce-scatter.4
  150.2 71.2 reduce-scatter.2
  223.6 36.0 all-gather.2
  261.5 69.6 all-gather.4

commit v4 on v3

--- a/solution.py
+++ b/solution.py
@@ -16,7 +16,7 @@
     return tuple(j if a == axis else lax.axis_index(a) for a in AXES)
 
 
-def exchange_kernel(axis, n, stride, gather, x_ref, y_ref, send_sem, recv_sem, own_sem):
+def exchange_kernel(axis, n, stride, gather, x_ref, y_ref, send_sem, recv_sem):
     index = lax.axis_index(axis)
     me = lax.rem(index // stride, n)
     base = index - me * stride
@@ -26,43 +26,38 @@
         return peer(axis, base + j * stride)
 
     def greet(k, carry):
-        j = lax.rem(me + k, n)
-        pl.semaphore_signal(barrier, inc=1, device_id=device(j), device_id_type=MESH)
+        pl.semaphore_signal(
+            barrier, inc=1, device_id=device(lax.rem(me + k, n)), device_id_type=MESH
+        )
         return carry
 
     lax.fori_loop(1, n, greet, 0)
     pl.semaphore_wait(barrier, n - 1)
 
-    def src(j):
-        return x_ref if gather else x_ref.at[j]
-
-    def remote(j, slot):
+    def remote(k, direction):
         return pltpu.make_async_remote_copy(
-            src_ref=src(j),
-            dst_ref=y_ref.at[slot],
-            send_sem=send_sem.at[j],
-            recv_sem=recv_sem.at[slot],
-            device_id=device(j),
+            src_ref=x_ref if gather else x_ref.at[k],
+            dst_ref=y_ref.at[k - 1],
+            send_sem=send_sem.at[k - 1],
+            recv_sem=recv_sem.at[k - 1],
+            device_id=device(lax.rem(me + direction * k + n, n)),
             device_id_type=MESH,
         )
 
-    own = pltpu.make_async_copy(src(me), y_ref.at[me], own_sem)
-    own.start()
+    ahead = -1 if gather else 1
 
     def send(k, carry):
-        remote(lax.rem(me + k, n), me).start()
+        remote(k, ahead).start()
         return carry
 
     lax.fori_loop(1, n, send, 0)
 
     def finish(k, carry):
-        remote(lax.rem(me + k, n), me).wait_send()
-        i = lax.rem(me + n - k, n)
-        remote(i, i).wait_recv()
+        remote(k, ahead).wait_send()
+        remote(k, -ahead).wait_recv()
         return carry
 
     lax.fori_loop(1, n, finish, 0)
-    own.wait()
 
 
 class Ids:
@@ -75,16 +70,15 @@
 
 
 def exchange(x, axis, n, stride, gather, cid):
-    shape = (n,) + x.shape if gather else x.shape
+    shape = (n - 1,) + (x.shape if gather else x.shape[1:])
     return pl.pallas_call(
         functools.partial(exchange_kernel, axis, n, stride, gather),
         out_shape=jax.ShapeDtypeStruct(shape, x.dtype),
         in_specs=[pl.BlockSpec(memory_space=pl.ANY)],
         out_specs=pl.BlockSpec(memory_space=pl.ANY),
         scratch_shapes=[
-            pltpu.SemaphoreType.DMA((n,)),
-            pltpu.SemaphoreType.DMA((n,)),
-            pltpu.SemaphoreType.DMA,
+            pltpu.SemaphoreType.DMA((n - 1,)),
+            pltpu.SemaphoreType.DMA((n - 1,)),
         ],
         compiler_params=pltpu.CompilerParams(collective_id=cid, has_side_effects=True),
     )(x)
@@ -92,14 +86,14 @@
 
 def gather_rows(x, axis, digits, ids):
     for n, stride in digits:
-        x = exchange(x, axis, n, stride, True, ids.take())
+        x = jnp.concatenate([x[None], exchange(x, axis, n, stride, True, ids.take())])
     return x.reshape((-1,) + x.shape[-1:])
 
 
 def sum_scatter_rows(x, axis, digits, ids):
     for n, stride in reversed(digits):
         x = x.reshape((n, -1) + x.shape[-1:])
-        x = jnp.sum(exchange(x, axis, n, stride, False, ids.take()), axis=0)
+        x = x[0] + jnp.sum(exchange(x, axis, n, stride, False, ids.take()), axis=0)
     return x
 
 

time: 484 us -> 360 us (0.74)
  Pallas kernels: 262 us -> 130 us
  other arithmetic: 23.9 us -> 32.4 us
  local copies, waits for them, and re-layouts: 21.7 us -> 27.3 us
    pallas_call x9, Pallas kernels: 262 us -> 130 us  [exchange(): pl.pallas_call(functools.partial(exchange_kernel, axis, n, stride, gather...]
    add x0 -> x4, other arithmetic: none -> 9.46 us  [sum_scatter_rows(): x = x[0] + jnp.sum(exchange(x, axis, n, stride, False, ids.take()), axis=0)]
    reduce_sum x6 -> x4, other arithmetic: 14.9 us -> 6.26 us  [sum_scatter_rows(): x = x[0] + jnp.sum(exchange(x, axis, n, stride, False, ids.take()), axis=0)]
    unnamed x26 -> x33, local copies, waits for them, and re-layouts: 10.5 us -> 15.2 us
  transfers between devices with their start and end apart: 4 -> 4, of which waited for: 3 -> 3; matrix products, arithmetic and copies ran while one was open for 9% -> 12% of each run, Pallas kernels for 18% -> 13%
where the time goes in v4:
time: 360 us; the launch traced here: 359 us
  Pallas kernels  130 us (36%)
  waiting for transfers between devices  127 us (35%)
  other arithmetic  32.4 us (9%)
  matrix products  28.9 us (8%)
  local copies, waits for them, and re-layouts  27.3 us (8%)
  between operations  14.1 us (4%)
    pallas_call x9, Pallas kernels, exchange(): pl.pallas_call(functools.partial(exchange_kernel, axis, n, stride, gather...  130 us
    reduce_scatter x1, waiting for transfers between devices, per_device(): lax.psum_scatter(partial_value, 'seq', scatter_dimension=0, tiled=True)  74.2 us
    reduce_scatter x1, waiting for transfers between devices, per_device(): lax.psum_scatter(grad_part, 'seq', scatter_dimension=0, tiled=True)  27.1 us
    all_gather x1, waiting for transfers between devices, per_device(): hidden = lax.all_gather(hidden_part, 'seq', axis=0, tiled=True)  25.4 us
    unnamed x33, local copies, waits for them, and re-layouts  15.2 us
    add x4, other arithmetic, sum_scatter_rows(): x = x[0] + jnp.sum(exchange(x, axis, n, stride, False, ids.take()), axis=0)  9.46 us
  transfers between devices with their start and end apart: 4, of which 3 were waited for; matrix products, arithmetic and copies ran while one was open for 12% of the time, Pallas kernels for 13%

profile of v4, /device:TPU:1, one launch (start us, length us, event | category | flops | bytes accessed | tf_op | source)
XLA Modules:
  0.0 359.4 jit_solution(9846118489048743347)
XLA Ops:
  7.2 0.0 reduce-scatter.5.cloned.1.call-start
  7.2 0.8 constant_dynamic-update-slice_fusion.1
  8.0 0.8 constant_dynamic-update-slice_fusion.x_ref
  8.8 0.6 copy-done.8
  9.5 17.2 %shard_map.119 = bf16[3,24,2048]{2,1,0:T(8,128)(2,1)} custom-call(bf16[24,2048]{1,0:T(8,128)(2,1)} %copy-done.8), custom_call_target="tpu_custom_call" | custom-call | tf_op jit(solution)/shard_map/pallas_call | solution.py:74
  26.6 1.8 fusion.18
  28.4 21.9 %shard_map.120 = bf16[3,4,24,2048]{3,2,1,0:T(8,128)(2,1)} custom-call(bf16[4,24,2048]{2,1,0:T(8,128)(2,1)} %get-tuple-element.13.x_ref), custom_call_target="tpu_custom_call" | custom-call | tf_op jit(solution)/shard_map/pallas_call | solution.py:74
  50.3 2.6 fusion.19
  53.0 4.1 %shard_map.121 = bf16[1,4,4,24,2048]{4,3,2,1,0:T(8,128)(2,1)} custom-call(bf16[4,4,24,2048]{3,2,1,0:T(8,128)(2,1)} %get-tuple-element.8.x_ref), custom_call_target="tpu_custom_call" | custom-call | tf_op jit(solution)/shard_map/pallas_call | solution.py:74
  57.1 1.7 pad_maximum_fusion.1
  58.8 1.1 broadcast_in_dim.35
  60.0 0.5 copy-done.3
  60.5 0.7 copy-done.7
  61.2 0.5 copy-done.12
  61.7 3.4 fusion.5
  65.1 0.0 reduce-scatter.3.cloned.1.call-start
  65.2 2.9 copy.16
  68.1 0.1 copy.15
  68.2 0.1 broadcast_bitcast_fusion
  68.3 3.8 %copy.14 = bf16[1024,896]{0,1:T(8,128)(2,1)} copy(bf16[1024,896]{1,0:T(8,128)(2,1)} %param.9) | data formatting | bytes 3670016 | tf_op args[1]
  72.1 0.1 copy.13
  72.2 0.1 broadcast_bitcast_fusion.1
  72.3 1.9 bitcast_multiply_fusion.1
  74.2 1.2 copy-done.5
  75.5 0.7 copy-done.6
  76.2 4.9 %fusion.3 = f32[768,1792]{1,0:T(8,128)} fusion(bf16[1024,896]{0,1:T(8,128)(2,1)S(1)} %get-tuple-element.14, bf16[1024,896]{0,1:T(8,128)(2,1)S(1)} %get-tuple-element.15, bf16[768,2048]{1,0:T(8,128)(2,1)S(1)} %bitcast.58), kind=kOutput, calls=%fused_computation.8 | convolution fusion | flops 2825912320 | bytes 10747904 | tf_op jit(solution)/shard_map/dot_general | solution.py:134
  81.0 0.0 reduce-scatter.3.cloned.1.call-update
  81.0 0.0 all-gather.3.cloned.1.call-start
  81.1 27.1 %reduce-scatter.5.cloned.1.call-done = f32[96,896]{1,0:T(8,128)} async-done(((f32[768,896]{1,0:T(8,128)}), f32[96,896]{1,0:T(8,128)}) %reduce-scatter.5.cloned.1.call-update) | async-done | bytes 344080 | tf_op jit(solution)/shard_map/reduce_scatter | solution.py:143
  108.2 74.2 %reduce-scatter.3.cloned.1.call-done = f32[96,1792]{1,0:T(8,128)} async-done(((f32[768,1792]{1,0:T(8,128)}), f32[96,1792]{1,0:T(8,128)}) %reduce-scatter.3.cloned.1.call-update) | async-done | bytes 688144 | tf_op jit(solution)/shard_map/reduce_scatter | solution.py:135
  182.4 2.1 multiply_convert_fusion.2
  184.5 0.2 all-gather.5.cloned.1.call-start
  184.7 0.8 pad_maximum_fusion.6
  185.5 0.0 all-gather.5.cloned.1.call-update
  185.5 1.5 broadcast_in_dim.33
  187.0 3.1 copy.18
  190.1 1.5 broadcast_in_dim.31
  191.5 3.8 %copy.17 = bf16[1024,896]{1,0:T(8,128)(2,1)} copy(bf16[1024,896]{0,1:T(8,128)(2,1)} %bitcast.52) | data formatting | bytes 3670016 | tf_op jit(solution)/shard_map/convert_element_type | solution.py:103
  195.4 25.4 %all-gather.3.cloned.1.call-done = bf16[768,896]{1,0:T(8,128)(2,1)} async-done(((bf16[96,896]{1,0:T(8,128)(2,1)}), bf16[768,896]{1,0:T(8,128)(2,1)}) %all-gather.3.cloned.1.call-update) | async-done | bytes 1376272 | tf_op jit(solution)/shard_map/all_gather | solution.py:138
  220.7 4.3 %fusion.10 = f32[768,1024]{1,0:T(8,128)S(1)} fusion(bf16[768,896]{1,0:T(8,128)(2,1)} %all-gather.3.cloned.1.call-done, bf16[896,1024]{1,0:T(8,128)(2,1)} %param.11, bf16[112,8,8,128]{3,2,1,0:T(8,128)(2,1)} %bitcast.62), kind=kOutput, calls=%fused_computation.19 | convolution fusion | flops 1410203648 | bytes 8192000 | tf_op jit(solution)/shard_map/dot_general | solution.py:140
  225.0 1.6 copy-done.2
  226.6 0.1 slice.57
  226.7 9.5 %shard_map.122 = f32[1,384,1024]{2,1,0:T(8,128)} custom-call(f32[2,384,1024]{2,1,0:T(8,128)} %bitcast.54), custom_call_target="tpu_custom_call" | custom-call | tf_op jit(solution)/shard_map/pallas_call | solution.py:74
  236.2 2.8 add.44.x_ref
  239.1 21.3 %shard_map.123 = f32[3,96,1024]{2,1,0:T(8,128)} custom-call(f32[4,96,1024]{2,1,0:T(8,128)} %add.44.x_ref), custom_call_target="tpu_custom_call" | custom-call | tf_op jit(solution)/shard_map/pallas_call | solution.py:74
  260.4 2.1 reduce_sum.54
  262.5 1.9 fusion.12
  264.4 14.8 %shard_map.124 = f32[3,24,1024]{2,1,0:T(8,128)} custom-call(f32[4,24,1024]{2,1,0:T(8,128)} %bitcast.60), custom_call_target="tpu_custom_call" | custom-call | tf_op jit(solution)/shard_map/pallas_call | solution.py:74
  279.2 1.0 reduce_sum.55
  280.2 1.5 fusion.15
  281.7 5.2 %multiply_convert_fusion = bf16[896,1024]{1,0:T(8,128)(2,1)} fusion(bf16[768,896]{1,0:T(8,128)(2,1)} %all-gather.3.cloned.1.call-done, bf16[112,8,8,128]{3,2,1,0:T(8,128)(2,1)} %bitcast.63, bf16[768,2048]{1,0:T(8,128)(2,1)} %bitcast.56), kind=kOutput, calls=%fused_computation.5 | convolution fusion | flops 1412038656 | bytes 6619136 | tf_op jit(solution)/shard_map/dot_general | solution.py:157
  287.0 5.5 %fusion.2 = f32[768,1024]{1,0:T(8,128)S(1)} fusion(bf16[768,1792]{1,0:T(8,128)(2,1)} %all-gather.5.cloned.1.call-done, bf16[1024,896]{0,1:T(8,128)(2,1)} %copy-done.5, bf16[1024,896]{0,1:T(8,128)(2,1)} %copy-done.6), kind=kOutput, calls=%fused_computation.7 | convolution fusion | flops 2825912320 | bytes 9568256 | tf_op jit(solution)/shard_map/dot_general | solution.py:147
  292.5 1.6 copy-done.1
  294.1 0.1 slice.62
  294.2 5.1 %shard_map.125 = f32[1,384,1024]{2,1,0:T(8,128)} custom-call(f32[2,384,1024]{2,1,0:T(8,128)} %bitcast.53), custom_call_target="tpu_custom_call" | custom-call | tf_op jit(solution)/shard_map/pallas_call | solution.py:74
  299.3 2.8 add.50.x_ref
  302.1 21.4 %shard_map.126 = f32[3,96,1024]{2,1,0:T(8,128)} custom-call(f32[4,96,1024]{2,1,0:T(8,128)} %add.50.x_ref), custom_call_target="tpu_custom_call" | custom-call | tf_op jit(solution)/shard_map/pallas_call | solution.py:74
  323.5 2.1 reduce_sum.58
  325.7 1.9 fusion.11
  327.6 14.4 %shard_map.127 = f32[3,24,1024]{2,1,0:T(8,128)} custom-call(f32[4,24,1024]{2,1,0:T(8,128)} %bitcast.59), custom_call_target="tpu_custom_call" | custom-call | tf_op jit(solution)/shard_map/pallas_call | solution.py:74
  342.0 1.0 reduce_sum.59
  343.0 1.5 fusion.14
  344.6 5.6 %fusion.7 = f32[1024,1792]{1,0:T(8,128)S(1)} fusion(bf16[768,1792]{1,0:T(8,128)(2,1)} %all-gather.5.cloned.1.call-done, bf16[768,2048]{1,0:T(8,128)(2,1)} %bitcast.57), kind=kOutput, calls=%fused_computation.14 | convolution fusion | flops 2818572288 | bytes 11665408 | tf_op jit(solution)/shard_map/dot_general | solution.py:152
  350.1 2.8 fusion
  (27 shorter events, 0.1 us)
Async XLA Ops:
  7.2 101.0 %reduce-scatter.5.cloned.1.call-start = ((), (), s32[]{:S(2)}) async-start(), calls=%async_computation.4 | async-start | bytes 3096576 | tf_op jit(solution)/shard_map/reduce_scatter | solution.py:143
  8.8 0.6 copy-start.8
  53.0 4.1 %copy-start.9 = (s32[7,8]{1,0:T(8,128)S(1)}, s32[7,8]{1,0:T(8,128)}, u32[]{:S(2)}) copy-start(s32[7,8]{1,0:T(8,128)} %param.14) | copy-start | bytes 676
  58.8 1.7 copy-start.3
  58.8 2.9 copy-start.12
  60.0 1.2 copy-start.7
  65.1 3.0 copy-start.10
  65.1 117.3 %reduce-scatter.3.cloned.1.call-start = ((), (), s32[]{:S(2)}) async-start(), calls=%async_computation.2 | async-start | bytes 6193152 | tf_op jit(solution)/shard_map/reduce_scatter | solution.py:135
  68.3 3.8 %copy-start.11 = (s32[8,7]{1,0:T(8,128)S(1)}, s32[8,7]{1,0:T(8,128)}, u32[]{:S(2)}) copy-start(s32[8,7]{1,0:T(8,128)} %param.12) | copy-start | bytes 676
  72.3 3.9 %copy-start.4 = (bf16[2,4,4,24,2048]{4,3,2,1,0:T(8,128)(2,1)S(1)}, bf16[2,4,4,24,2048]{4,3,2,1,0:T(8,128)(2,1)}, u32[]{:S(2)}) copy-start(bf16[2,4,4,24,2048]{4,3,2,1,0:T(8,128)(2,1)} %copy-done.3) | copy-start | bytes 9437188
  74.2 1.2 copy-start.5
  74.2 1.9 copy-start.6
  81.0 139.7 %all-gather.3.cloned.1.call-start = ((), (), s32[]{:S(2)}) async-start(), calls=%async_computation.3 | async-start | bytes 1548288 | tf_op jit(solution)/shard_map/all_gather | solution.py:138
  184.5 102.4 %all-gather.5.cloned.1.call-start = ((), (), s32[]{:S(2)}) async-start(), calls=%async_computation.5 | async-start | bytes 3096576 | tf_op jit(solution)/shard_map/all_gather | solution.py:145
  225.0 1.6 copy-start.2
  292.5 1.6 copy-start.1
  344.6 5.6 %copy-start = (bf16[1024,896]{1,0:T(8,128)(2,1)S(1)}, bf16[1024,896]{1,0:T(8,128)(2,1)}, u32[]{:S(2)}) copy-start(bf16[1024,896]{1,0:T(8,128)(2,1)} %copy.17) | copy-start | bytes 5505028
Sparse Core Ops, SparseCore 0:
  65.3 42.9 reduce-scatter.4
  110.9 71.4 reduce-scatter.2
  184.6 36.0 all-gather.2
  222.5 46.8 all-gather.4

commit v5 on v4

--- a/solution.py
+++ b/solution.py
@@ -16,7 +16,7 @@
     return tuple(j if a == axis else lax.axis_index(a) for a in AXES)
 
 
-def exchange_kernel(axis, n, stride, gather, x_ref, y_ref, send_sem, recv_sem):
+def exchange_kernel(axis, n, stride, gather, absolute, x_ref, y_ref, send_sem, recv_sem):
     index = lax.axis_index(axis)
     me = lax.rem(index // stride, n)
     base = index - me * stride
@@ -35,16 +35,21 @@
     pl.semaphore_wait(barrier, n - 1)
 
     def remote(k, direction):
+        other = lax.rem(me + direction * k + n, n)
+        if absolute and gather:
+            slot = me if direction == ahead else other
+        else:
+            slot = k - 1
         return pltpu.make_async_remote_copy(
-            src_ref=x_ref if gather else x_ref.at[k],
-            dst_ref=y_ref.at[k - 1],
+            src_ref=x_ref if gather else x_ref.at[other if absolute else k],
+            dst_ref=y_ref.at[slot],
             send_sem=send_sem.at[k - 1],
-            recv_sem=recv_sem.at[k - 1],
-            device_id=device(lax.rem(me + direction * k + n, n)),
+            recv_sem=recv_sem.at[slot],
+            device_id=device(other),
             device_id_type=MESH,
         )
 
-    ahead = -1 if gather else 1
+    ahead = 1 if absolute or not gather else -1
 
     def send(k, carry):
         remote(k, ahead).start()
@@ -69,16 +74,17 @@
         return self.next - 1
 
 
-def exchange(x, axis, n, stride, gather, cid):
-    shape = (n - 1,) + (x.shape if gather else x.shape[1:])
+def exchange(x, axis, n, stride, gather, cid, absolute=False):
+    slots = n if absolute and gather else n - 1
+    shape = (slots,) + (x.shape if gather else x.shape[1:])
     return pl.pallas_call(
-        functools.partial(exchange_kernel, axis, n, stride, gather),
+        functools.partial(exchange_kernel, axis, n, stride, gather, absolute),
         out_shape=jax.ShapeDtypeStruct(shape, x.dtype),
         in_specs=[pl.BlockSpec(memory_space=pl.ANY)],
         out_specs=pl.BlockSpec(memory_space=pl.ANY),
         scratch_shapes=[
             pltpu.SemaphoreType.DMA((n - 1,)),
-            pltpu.SemaphoreType.DMA((n - 1,)),
+            pltpu.SemaphoreType.DMA((slots,)),
         ],
         compiler_params=pltpu.CompilerParams(collective_id=cid, has_side_effects=True),
     )(x)
@@ -94,6 +100,25 @@
     for n, stride in reversed(digits):
         x = x.reshape((n, -1) + x.shape[-1:])
         x = x[0] + jnp.sum(exchange(x, axis, n, stride, False, ids.take()), axis=0)
+    return x
+
+
+def digit(axis, n, stride):
+    return lax.rem(lax.axis_index(axis) // stride, n)
+
+
+def gather_rows_absolute(x, axis, digits, ids):
+    for n, stride in digits:
+        y = exchange(x, axis, n, stride, True, ids.take(), absolute=True)
+        x = lax.dynamic_update_index_in_dim(y, x, digit(axis, n, stride), 0)
+    return x.reshape((-1,) + x.shape[-1:])
+
+
+def sum_scatter_rows_absolute(x, axis, digits, ids):
+    for n, stride in reversed(digits):
+        x = x.reshape((n, -1) + x.shape[-1:])
+        own = lax.dynamic_index_in_dim(x, digit(axis, n, stride), 0, keepdims=False)
+        x = own + jnp.sum(exchange(x, axis, n, stride, False, ids.take(), absolute=True), axis=0)
     return x
 
 
@@ -117,7 +142,7 @@
     return jnp.concatenate([dgate, dup], axis=1)
 
 
-def per_device(tensor_digits, tokens, w_gate, w_up, w_down, mask_gate, mask_up, mask_down, cotangent):
+def per_device(tensor_digits, seq_digits, tokens, w_gate, w_up, w_down, mask_gate, mask_up, mask_down, cotangent):
     width = w_gate.shape[1]
     feat = tokens.shape[1]
     gate_mask = widen(mask_gate, w_gate.shape[0])
@@ -132,17 +157,17 @@
     gathered = both[:, :feat]
     cot_rows = both[:, feat:]
     partial_value = jnp.dot(gathered, joined, preferred_element_type=jnp.float32)
-    summed = lax.psum_scatter(partial_value, "seq", scatter_dimension=0, tiled=True)
+    summed = sum_scatter_rows_absolute(partial_value, "seq", seq_digits, ids)
     gate, up, sig, act = gating(summed, width)
     hidden_part = (act * up).astype(jnp.bfloat16)
-    hidden = lax.all_gather(hidden_part, "seq", axis=0, tiled=True)
+    hidden = gather_rows_absolute(hidden_part, "seq", seq_digits, ids)
     output = sum_scatter_rows(
         jnp.dot(hidden, down_w, preferred_element_type=jnp.float32), "tensor", tensor_digits, ids
     ).astype(jnp.bfloat16)
     grad_part = lax.dot_general(cot_rows, down_w, contract_last, preferred_element_type=jnp.float32)
-    grad_hidden = lax.psum_scatter(grad_part, "seq", scatter_dimension=0, tiled=True)
+    grad_hidden = sum_scatter_rows_absolute(grad_part, "seq", seq_digits, ids)
     grads_part = gate_up_grads(gate, up, sig, act, grad_hidden)
-    grads = lax.all_gather(grads_part, "seq", axis=0, tiled=True)
+    grads = gather_rows_absolute(grads_part, "seq", seq_digits, ids)
     grad_tokens = sum_scatter_rows(
         lax.dot_general(grads, joined, contract_last, preferred_element_type=jnp.float32),
         "tensor",
@@ -196,7 +221,7 @@
 
 def solution(mesh):
     return jax.shard_map(
-        functools.partial(per_device, digits_of(mesh, "tensor")),
+        functools.partial(per_device, digits_of(mesh, "tensor"), digits_of(mesh, "seq")),
         mesh=mesh,
         in_specs=(
             P("tensor", "seq"),

time: 360 us -> 417 us (1.16); the launches traced: 359 us -> 412 us
  Pallas kernels: 130 us -> 308 us
  waiting for transfers between devices: 127 us -> 0 us
  between operations: 14.1 us -> 1.13 us
  other arithmetic: 32.4 us -> 44.6 us
    pallas_call x9 -> x17, Pallas kernels: 130 us -> 308 us  [exchange(): pl.pallas_call(functools.partial(exchange_kernel, axis, n, stride, gather...]
    reduce_scatter x2 -> x0, waiting for transfers between devices: 101 us -> none  [the longest x1 74.2 us: per_device(): lax.psum_scatter(partial_value, 'seq', scatter_dimension=0, tiled=True)]
    all_gather x2 -> x0, waiting for transfers between devices: 25.4 us -> none  [the longest x1 25.4 us: per_device(): hidden = lax.all_gather(hidden_part, 'seq', axis=0, tiled=True)]
    reduce_sum x0 -> x2, other arithmetic: none -> 4.39 us  [sum_scatter_rows_absolute(): jnp.sum(exchange(x, axis, n, stride, False, ids.take(), absolute=True), a...]
    unnamed x33 -> x53, local copies, waits for them, and re-layouts: 15.2 us -> 12.5 us
  transfers between devices with their start and end apart: 4 -> 0, of which waited for: 3 -> 0; matrix products, arithmetic and copies ran while one was open for 12% -> 0% of each run, Pallas kernels for 13% -> 0%
where the time goes in v5:
time: 417 us; the launch traced here: 412 us
  Pallas kernels  308 us (74%)
  other arithmetic  44.6 us (11%)
  local copies, waits for them, and re-layouts  29.5 us (7%)
  matrix products  29.1 us (7%)
    pallas_call x17, Pallas kernels, exchange(): pl.pallas_call(functools.partial(exchange_kernel, axis, n, stride, gather...  308 us
    unnamed x53, local copies, waits for them, and re-layouts  12.5 us
    add x4, other arithmetic, sum_scatter_rows(): x = x[0] + jnp.sum(exchange(x, axis, n, stride, False, ids.take()), axis=0)  9.23 us

profile of v5, /device:TPU:1, one launch (start us, length us, event | category | flops | bytes accessed | tf_op | source)
XLA Modules:
  0.0 412.2 jit_solution(5876370195403821316)
XLA Ops:
  0.6 2.9 copy.16
  3.8 3.8 copy.14
  7.8 3.6 bitcast_multiply_fusion.1
  11.4 0.6 copy-done.17
  12.1 17.2 %shard_map.119 = bf16[3,24,2048]{2,1,0:T(8,128)(2,1)} custom-call(bf16[24,2048]{1,0:T(8,128)(2,1)} %copy-done.17), custom_call_target="tpu_custom_call" | custom-call | tf_op jit(solution)/shard_map/pallas_call | solution.py:80
  29.2 1.8 fusion.22
  31.0 21.9 %shard_map.120 = bf16[3,4,24,2048]{3,2,1,0:T(8,128)(2,1)} custom-call(bf16[4,24,2048]{2,1,0:T(8,128)(2,1)} %get-tuple-element.13.x_ref), custom_call_target="tpu_custom_call" | custom-call | tf_op jit(solution)/shard_map/pallas_call | solution.py:80
  52.9 2.6 fusion.23
  55.6 4.1 shard_map.121
  59.7 1.8 pad_maximum_fusion.1
  61.6 0.6 copy-done.12
  62.2 4.9 %fusion.3 = f32[768,1792]{1,0:T(8,128)} fusion(bf16[1024,896]{0,1:T(8,128)(2,1)S(1)} %copy-done.10, bf16[1024,896]{0,1:T(8,128)(2,1)S(1)} %copy-done.12, bf16[768,2048]{1,0:T(8,128)(2,1)S(1)} %bitcast.90), kind=kOutput, calls=%fused_computation.8 | convolution fusion | flops 2825912320 | bytes 10747904 | tf_op jit(solution)/shard_map/dot_general | solution.py:159
  67.1 1.4 constant_dynamic-slice_fusion.1
  68.5 63.6 %shard_map.122 = f32[3,192,1792]{2,1,0:T(8,128)} custom-call(f32[4,192,1792]{2,1,0:T(8,128)} %bitcast.75), custom_call_target="tpu_custom_call" | custom-call | tf_op jit(solution)/shard_map/pallas_call | solution.py:80
  132.1 2.6 reduce_sum.82
  134.7 1.2 add.81.x_ref
  135.9 16.9 %shard_map.123 = f32[1,96,1792]{2,1,0:T(8,128)} custom-call(f32[2,96,1792]{2,1,0:T(8,128)} %add.81.x_ref), custom_call_target="tpu_custom_call" | custom-call | tf_op jit(solution)/shard_map/pallas_call | solution.py:80
  152.9 1.3 add_bitcast_fusion
  154.3 1.1 broadcast_in_dim.53
  155.4 4.0 fusion.5
  159.5 1.0 constant_dynamic-slice_fusion
  160.5 0.8 copy-done.4
  161.3 33.9 %shard_map.129 = f32[3,192,896]{2,1,0:T(8,128)} custom-call(f32[4,192,896]{2,1,0:T(8,128)} %bitcast.89), custom_call_target="tpu_custom_call" | custom-call | tf_op jit(solution)/shard_map/pallas_call | solution.py:80
  195.2 1.8 reduce_sum.88
  197.0 0.9 add.91.x_ref
  198.0 7.9 %shard_map.130 = f32[1,96,896]{2,1,0:T(8,128)} custom-call(f32[2,96,896]{2,1,0:T(8,128)} %add.91.x_ref), custom_call_target="tpu_custom_call" | custom-call | tf_op jit(solution)/shard_map/pallas_call | solution.py:80
  205.9 2.0 fusion.15
  207.8 4.6 %shard_map.124 = bf16[2,96,896]{2,1,0:T(8,128)(2,1)} custom-call(bf16[96,896]{1,0:T(8,128)(2,1)} %get-tuple-element.11.x_ref), custom_call_target="tpu_custom_call" | custom-call | tf_op jit(solution)/shard_map/pallas_call | solution.py:80
  212.4 1.6 bitcast_dynamic-update-slice_fusion.3.x_ref
  214.0 19.0 %shard_map.125 = bf16[4,2,96,896]{3,2,1,0:T(8,128)(2,1)} custom-call(bf16[2,96,896]{2,1,0:T(8,128)(2,1)} %bitcast_dynamic-update-slice_fusion.3.x_ref), custom_call_target="tpu_custom_call" | custom-call | tf_op jit(solution)/shard_map/pallas_call | solution.py:80
  233.1 0.8 bitcast_dynamic-update-slice_fusion.2
  233.9 3.7 fusion.10
  237.6 1.7 copy-done.2
  239.3 0.1 slice.57
  239.4 6.2 %shard_map.126 = f32[1,384,1024]{2,1,0:T(8,128)} custom-call(f32[2,384,1024]{2,1,0:T(8,128)} %bitcast.85), custom_call_target="tpu_custom_call" | custom-call | tf_op jit(solution)/shard_map/pallas_call | solution.py:80
  245.7 2.8 add.87.x_ref
  248.5 20.8 %shard_map.127 = f32[3,96,1024]{2,1,0:T(8,128)} custom-call(f32[4,96,1024]{2,1,0:T(8,128)} %add.87.x_ref), custom_call_target="tpu_custom_call" | custom-call | tf_op jit(solution)/shard_map/pallas_call | solution.py:80
  269.3 1.4 reduce_sum.86
  270.7 1.8 fusion.12
  272.5 10.0 %shard_map.128 = f32[3,24,1024]{2,1,0:T(8,128)} custom-call(f32[4,24,1024]{2,1,0:T(8,128)} %bitcast.99), custom_call_target="tpu_custom_call" | custom-call | tf_op jit(solution)/shard_map/pallas_call | solution.py:80
  282.5 1.0 reduce_sum.87
  283.4 1.5 fusion.19
  285.0 0.8 pad_maximum_fusion.6.x_ref
  285.7 13.6 %shard_map.131 = bf16[2,96,1792]{2,1,0:T(8,128)(2,1)} custom-call(bf16[96,1792]{1,0:T(8,128)(2,1)} %pad_maximum_fusion.6.x_ref), custom_call_target="tpu_custom_call" | custom-call | tf_op jit(solution)/shard_map/pallas_call | solution.py:80
  299.3 0.8 bitcast_dynamic-update-slice_fusion.1.x_ref
  300.1 32.4 %shard_map.132 = bf16[4,2,96,1792]{3,2,1,0:T(8,128)(2,1)} custom-call(bf16[2,96,1792]{2,1,0:T(8,128)(2,1)} %bitcast_dynamic-update-slice_fusion.1.x_ref), custom_call_target="tpu_custom_call" | custom-call | tf_op jit(solution)/shard_map/pallas_call | solution.py:80
  332.5 0.9 bitcast_dynamic-update-slice_fusion
  333.4 5.3 %fusion.2 = f32[768,1024]{1,0:T(8,128)S(1)} fusion(bf16[768,1792]{1,0:T(8,128)(2,1)} %bitcast.96, bf16[1024,896]{0,1:T(8,128)(2,1)S(1)} %copy-done.11, bf16[1024,896]{0,1:T(8,128)(2,1)} %get-tuple-element.15), kind=kOutput, calls=%fused_computation.7 | convolution fusion | flops 2825912320 | bytes 9568256 | tf_op jit(solution)/shard_map/dot_general | solution.py:172
  338.8 1.8 copy-done.1
  340.7 5.6 %shard_map.133 = f32[1,384,1024]{2,1,0:T(8,128)} custom-call(f32[2,384,1024]{2,1,0:T(8,128)} %bitcast.84), custom_call_target="tpu_custom_call" | custom-call | tf_op jit(solution)/shard_map/pallas_call | solution.py:80
  346.3 2.8 add.96.x_ref
  349.1 20.7 %shard_map.134 = f32[3,96,1024]{2,1,0:T(8,128)} custom-call(f32[4,96,1024]{2,1,0:T(8,128)} %add.96.x_ref), custom_call_target="tpu_custom_call" | custom-call | tf_op jit(solution)/shard_map/pallas_call | solution.py:80
  369.8 1.4 reduce_sum.92
  371.2 1.8 fusion.11
  373.0 9.4 %shard_map.135 = f32[3,24,1024]{2,1,0:T(8,128)} custom-call(f32[4,24,1024]{2,1,0:T(8,128)} %bitcast.98), custom_call_target="tpu_custom_call" | custom-call | tf_op jit(solution)/shard_map/pallas_call | solution.py:80
  382.4 1.0 reduce_sum.93
  383.4 1.5 fusion.18
  384.9 8.2 %fusion.7 = f32[1024,1792]{1,0:T(8,128)} fusion(bf16[768,1792]{1,0:T(8,128)(2,1)} %bitcast.97, bf16[768,2048]{1,0:T(8,128)(2,1)} %bitcast.91), kind=kOutput, calls=%fused_computation.14 | convolution fusion | flops 2818572288 | bytes 11665408 | tf_op jit(solution)/shard_map/dot_general | solution.py:177
  393.2 1.5 broadcast_in_dim.49
  394.6 3.1 copy.18
  397.7 1.5 broadcast_in_dim.47
  399.1 3.8 copy.17
  402.9 6.4 %fusion = (bf16[1024,896]{1,0:T(8,128)(2,1)}, bf16[1024,896]{1,0:T(8,128)(2,1)}) fusion(f32[1024,1792]{1,0:T(8,128)} %fusion.7, bf16[1024,896]{1,0:T(8,128)(2,1)S(1)} %copy.18, bf16[1024,896]{1,0:T(8,128)(2,1)} %copy.17), kind=kLoop, calls=%fused_computation.1 | loop fusion | flops 5505024 | bytes 14680064 | tf_op jit(solution)/shard_map/convert_element_type | solution.py:181
  409.3 2.9 multiply_convert_fusion
  (54 shorter events, 0.7 us)
Async XLA Ops:
  0.6 2.9 copy-start.20
  3.8 3.8 copy-start.21
  7.7 3.6 copy-start.18
  7.8 3.6 copy-start.19
  11.4 0.6 copy-start.17
  59.7 2.0 copy-start.10
  59.7 2.5 copy-start.12
  61.5 5.5 %copy-start.5 = (bf16[2,4,4,24,2048]{4,3,2,1,0:T(8,128)(2,1)}, bf16[2,4,4,24,2048]{4,3,2,1,0:T(8,128)(2,1)S(1)}, u32[]{:S(2)}) copy-start(bf16[2,4,4,24,2048]{4,3,2,1,0:T(8,128)(2,1)S(1)} %pad_maximum_fusion.1) | copy-start | bytes 9437188
  135.9 17.0 %copy-start = (f32[2,96,1792]{2,1,0:T(8,128)S(1)}, f32[2,96,1792]{2,1,0:T(8,128)}, u32[]{:S(2)}) copy-start(f32[2,96,1792]{2,1,0:T(8,128)} %add.81.x_ref) | copy-start | bytes 4128772
  135.9 18.3 %copy-start.22 = (s32[7,8]{1,0:T(8,128)S(1)}, s32[7,8]{1,0:T(8,128)}, u32[]{:S(2)}) copy-start(s32[7,8]{1,0:T(8,128)} %param.14) | copy-start | bytes 676
  152.9 2.5 copy-start.6
  155.4 4.1 copy-start.13
  159.5 1.8 copy-start.4
  195.2 1.8 copy-start.9
  207.8 26.0 %copy-start.14 = (bf16[896,8,128]{2,1,0:T(8,128)(2,1)S(1)}, bf16[896,8,128]{2,1,0:T(8,128)(2,1)}, u32[]{:S(2)}) copy-start(bf16[896,8,128]{2,1,0:T(8,128)(2,1)} %copy-done.13) | copy-start | bytes 5505028
  214.0 19.0 %copy-start.8 = (bf16[2,96,896]{2,1,0:T(8,128)(2,1)S(1)}, bf16[2,96,896]{2,1,0:T(8,128)(2,1)}, u32[]{:S(2)}) copy-start(bf16[2,96,896]{2,1,0:T(8,128)(2,1)} %bitcast_dynamic-update-slice_fusion.3.x_ref) | copy-start | bytes 1032196
  237.6 1.7 copy-start.2
  300.1 32.4 %copy-start.3 = (bf16[2,96,1792]{2,1,0:T(8,128)(2,1)S(1)}, bf16[2,96,1792]{2,1,0:T(8,128)(2,1)}, u32[]{:S(2)}) copy-start(bf16[2,96,1792]{2,1,0:T(8,128)(2,1)} %bitcast_dynamic-update-slice_fusion.1.x_ref) | copy-start | bytes 2064388
  300.1 33.3 %copy-start.11 = (bf16[1024,896]{0,1:T(8,128)(2,1)S(1)}, bf16[1024,896]{0,1:T(8,128)(2,1)}, u32[]{:S(2)}) copy-start(bf16[1024,896]{0,1:T(8,128)(2,1)} %get-tuple-element.14) | copy-start | bytes 5505028
  338.8 1.8 copy-start.1
  402.9 6.4 %copy-start.7 = (bf16[2,4,4,24,2048]{4,3,2,1,0:T(8,128)(2,1)S(1)}, bf16[2,4,4,24,2048]{4,3,2,1,0:T(8,128)(2,1)}, u32[]{:S(2)}) copy-start(bf16[2,4,4,24,2048]{4,3,2,1,0:T(8,128)(2,1)} %copy-done.5) | copy-start | bytes 9437188
  402.9 6.4 %copy-start.15 = (bf16[896,8,128]{2,1,0:T(8,128)(2,1)S(1)}, bf16[896,8,128]{2,1,0:T(8,128)(2,1)}, u32[]{:S(2)}) copy-start(bf16[896,8,128]{2,1,0:T(8,128)(2,1)} %copy-done.13) | copy-start | bytes 5505028
  402.9 6.4 %copy-start.16 = (bf16[4,2,96,896]{3,2,1,0:T(8,128)(2,1)S(1)}, bf16[4,2,96,896]{3,2,1,0:T(8,128)(2,1)}, u32[]{:S(2)}) copy-start(bf16[4,2,96,896]{3,2,1,0:T(8,128)(2,1)} %bitcast_dynamic-update-slice_fusion.2) | copy-start | bytes 4128772

commit v6 on v5

--- a/solution.py
+++ b/solution.py
@@ -120,6 +120,23 @@
         own = lax.dynamic_index_in_dim(x, digit(axis, n, stride), 0, keepdims=False)
         x = own + jnp.sum(exchange(x, axis, n, stride, False, ids.take(), absolute=True), axis=0)
     return x
+
+
+def reorder_blocks(x, sizes):
+    k = len(sizes)
+    x = x.reshape(tuple(sizes) + (-1, x.shape[-1]))
+    x = jnp.transpose(x, tuple(reversed(range(k))) + (k, k + 1))
+    return x.reshape((-1, x.shape[-1]))
+
+
+def seq_sum_scatter(x, digits, ids):
+    x = reorder_blocks(x, [n for n, _ in digits])
+    return sum_scatter_rows_absolute(x, "seq", digits, ids)
+
+
+def seq_gather(x, digits, ids):
+    x = gather_rows_absolute(x, "seq", digits, ids)
+    return reorder_blocks(x, [n for n, _ in reversed(digits)])
 
 
 def widen(mask, rows):
@@ -157,17 +174,17 @@
     gathered = both[:, :feat]
     cot_rows = both[:, feat:]
     partial_value = jnp.dot(gathered, joined, preferred_element_type=jnp.float32)
-    summed = sum_scatter_rows_absolute(partial_value, "seq", seq_digits, ids)
+    summed = lax.psum_scatter(partial_value, "seq", scatter_dimension=0, tiled=True)
     gate, up, sig, act = gating(summed, width)
     hidden_part = (act * up).astype(jnp.bfloat16)
-    hidden = gather_rows_absolute(hidden_part, "seq", seq_digits, ids)
+    hidden = seq_gather(hidden_part, seq_digits, ids)
     output = sum_scatter_rows(
         jnp.dot(hidden, down_w, preferred_element_type=jnp.float32), "tensor", tensor_digits, ids
     ).astype(jnp.bfloat16)
     grad_part = lax.dot_general(cot_rows, down_w, contract_last, preferred_element_type=jnp.float32)
-    grad_hidden = sum_scatter_rows_absolute(grad_part, "seq", seq_digits, ids)
+    grad_hidden = seq_sum_scatter(grad_part, seq_digits, ids)
     grads_part = gate_up_grads(gate, up, sig, act, grad_hidden)
-    grads = gather_rows_absolute(grads_part, "seq", seq_digits, ids)
+    grads = lax.all_gather(grads_part, "seq", axis=0, tiled=True)
     grad_tokens = sum_scatter_rows(
         lax.dot_general(grads, joined, contract_last, preferred_element_type=jnp.float32),
         "tensor",

time: 417 us -> 373 us (0.89)
  Pallas kernels: 308 us -> 262 us
  between operations: 1.13 us -> 14.5 us
  other arithmetic: 44.6 us -> 33.8 us
    pallas_call x17 -> x13, Pallas kernels: 308 us -> 262 us  [exchange(): pl.pallas_call(functools.partial(exchange_kernel, axis, n, stride, gather...]
    unnamed x53 -> x47, local copies, waits for them, and re-layouts: 12.5 us -> 14.7 us
  transfers between devices with their start and end apart: 0 -> 2, of which waited for: 0 -> 0; matrix products, arithmetic and copies ran while one was open for 0% -> 11% of each run, Pallas kernels for 0% -> 48%
where the time goes in v6:
time: 373 us; the launch traced here: 370 us
  Pallas kernels  262 us (70%)
  other arithmetic  33.8 us (9%)
  local copies, waits for them, and re-layouts  31.9 us (9%)
  matrix products  26.9 us (7%)
  between operations  14.5 us (4%)
    pallas_call x13, Pallas kernels, exchange(): pl.pallas_call(functools.partial(exchange_kernel, axis, n, stride, gather...  262 us
    unnamed x47, local copies, waits for them, and re-layouts  14.7 us
    add x4, other arithmetic, sum_scatter_rows(): x = x[0] + jnp.sum(exchange(x, axis, n, stride, False, ids.take()), axis=0)  9.46 us
  transfers between devices with their start and end apart: 2, of which 0 were waited for; matrix products, arithmetic and copies ran while one was open for 11% of the time, Pallas kernels for 48%

profile of v6, /device:TPU:1, one launch (start us, length us, event | category | flops | bytes accessed | tf_op | source)
XLA Modules:
  0.0 369.6 jit_solution(10468000603951132439)
XLA Ops:
  7.2 2.9 copy.17
  10.1 0.1 copy.16
  10.4 3.8 %copy.15 = bf16[1024,896]{0,1:T(8,128)(2,1)} copy(bf16[1024,896]{1,0:T(8,128)(2,1)} %param.9) | data formatting | bytes 3670016 | tf_op args[1]
  14.2 0.1 copy.14
  14.4 0.6 copy-done.13
  15.0 17.2 %shard_map.119 = bf16[3,24,2048]{2,1,0:T(8,128)(2,1)} custom-call(bf16[24,2048]{1,0:T(8,128)(2,1)} %copy-done.13), custom_call_target="tpu_custom_call" | custom-call | tf_op jit(solution)/shard_map/pallas_call | solution.py:80
  32.2 1.9 fusion.22
  34.1 21.9 %shard_map.120 = bf16[3,4,24,2048]{3,2,1,0:T(8,128)(2,1)} custom-call(bf16[4,24,2048]{2,1,0:T(8,128)(2,1)} %get-tuple-element.13.x_ref), custom_call_target="tpu_custom_call" | custom-call | tf_op jit(solution)/shard_map/pallas_call | solution.py:80
  56.1 2.7 fusion.23
  58.8 4.1 %shard_map.121 = bf16[1,4,4,24,2048]{4,3,2,1,0:T(8,128)(2,1)} custom-call(bf16[4,4,24,2048]{3,2,1,0:T(8,128)(2,1)} %get-tuple-element.10.x_ref), custom_call_target="tpu_custom_call" | custom-call | tf_op jit(solution)/shard_map/pallas_call | solution.py:80
  62.9 1.8 pad_maximum_fusion.1
  64.7 0.1 copy-done.1
  64.8 0.3 bitcast_multiply_fusion.1
  65.1 1.2 copy-done.4
  66.3 0.6 copy-done.7
  67.0 0.7 copy-done.8
  67.6 4.9 %fusion.3 = f32[768,1792]{1,0:T(8,128)} fusion(bf16[1024,896]{0,1:T(8,128)(2,1)S(1)} %get-tuple-element.14, bf16[1024,896]{0,1:T(8,128)(2,1)S(1)} %get-tuple-element.15, bf16[768,2048]{1,0:T(8,128)(2,1)S(1)} %bitcast.81), kind=kOutput, calls=%fused_computation.8 | convolution fusion | flops 2825912320 | bytes 10747904 | tf_op jit(solution)/shard_map/dot_general | solution.py:176
  72.5 0.2 all-gather.2.cloned.1.call-start
  72.8 0.4 copy-done.18
  73.2 1.1 broadcast_in_dim.45
  74.4 0.7 copy-done.19
  75.1 1.8 fusion.5
  77.0 1.8 copy.19
  78.8 85.5 %shard_map.127 = f32[3,192,896]{2,1,0:T(8,128)} custom-call(f32[4,192,896]{2,1,0:T(8,128)} %bitcast.68), custom_call_target="tpu_custom_call" | custom-call | tf_op jit(solution)/shard_map/pallas_call | solution.py:80
  164.3 1.8 reduce_sum.71
  166.1 1.2 constant_dynamic-slice_fusion
  167.3 0.9 add.72.x_ref
  168.2 9.6 %shard_map.128 = f32[1,96,896]{2,1,0:T(8,128)} custom-call(f32[2,96,896]{2,1,0:T(8,128)} %add.72.x_ref), custom_call_target="tpu_custom_call" | custom-call | tf_op jit(solution)/shard_map/pallas_call | solution.py:80
  177.8 2.1 fusion.15
  180.0 0.8 pad_maximum_fusion.6
  180.8 1.5 broadcast_in_dim.41
  182.2 3.1 copy.21
  185.3 1.5 broadcast_in_dim.39
  186.8 3.8 %copy.20 = bf16[1024,896]{1,0:T(8,128)(2,1)} copy(bf16[1024,896]{0,1:T(8,128)(2,1)} %bitcast.77) | data formatting | bytes 3670016 | tf_op jit(solution)/shard_map/convert_element_type | solution.py:145
  190.6 8.0 %shard_map.122 = bf16[2,96,896]{2,1,0:T(8,128)(2,1)} custom-call(bf16[96,896]{1,0:T(8,128)(2,1)} %get-tuple-element.11.x_ref), custom_call_target="tpu_custom_call" | custom-call | tf_op jit(solution)/shard_map/pallas_call | solution.py:80
  198.6 0.7 bitcast_dynamic-update-slice_fusion.1.x_ref
  199.3 41.4 %shard_map.123 = bf16[4,2,96,896]{3,2,1,0:T(8,128)(2,1)} custom-call(bf16[2,96,896]{2,1,0:T(8,128)(2,1)} %bitcast_dynamic-update-slice_fusion.1.x_ref), custom_call_target="tpu_custom_call" | custom-call | tf_op jit(solution)/shard_map/pallas_call | solution.py:80
  240.7 0.8 bitcast_dynamic-update-slice_fusion
  241.5 1.4 copy.18
  243.0 3.8 %fusion.10 = f32[768,1024]{1,0:T(8,128)S(1)} fusion(bf16[768,896]{1,0:T(8,128)(2,1)S(1)} %bitcast.93, bf16[896,1024]{1,0:T(8,128)(2,1)} %param.11, bf16[112,8,8,128]{3,2,1,0:T(8,128)(2,1)S(1)} %bitcast.92), kind=kOutput, calls=%fused_computation.19 | convolution fusion | flops 1410203648 | bytes 8192000 | tf_op jit(solution)/shard_map/dot_general | solution.py:182
  246.8 1.6 copy-done.3
  248.5 0.1 slice.57
  248.6 4.0 %shard_map.124 = f32[1,384,1024]{2,1,0:T(8,128)} custom-call(f32[2,384,1024]{2,1,0:T(8,128)} %bitcast.79), custom_call_target="tpu_custom_call" | custom-call | tf_op jit(solution)/shard_map/pallas_call | solution.py:80
  252.6 2.8 add.68.x_ref
  255.4 20.8 %shard_map.125 = f32[3,96,1024]{2,1,0:T(8,128)} custom-call(f32[4,96,1024]{2,1,0:T(8,128)} %add.68.x_ref), custom_call_target="tpu_custom_call" | custom-call | tf_op jit(solution)/shard_map/pallas_call | solution.py:80
  276.2 2.1 reduce_sum.69
  278.4 1.9 fusion.12
  280.3 9.5 %shard_map.126 = f32[3,24,1024]{2,1,0:T(8,128)} custom-call(f32[4,24,1024]{2,1,0:T(8,128)} %bitcast.89), custom_call_target="tpu_custom_call" | custom-call | tf_op jit(solution)/shard_map/pallas_call | solution.py:80
  289.8 1.0 reduce_sum.70
  290.8 1.5 fusion.19
  292.3 5.2 %multiply_convert_fusion = bf16[896,1024]{1,0:T(8,128)(2,1)} fusion(bf16[768,896]{1,0:T(8,128)(2,1)} %bitcast.94, bf16[112,8,8,128]{3,2,1,0:T(8,128)(2,1)} %bitcast.91, bf16[768,2048]{1,0:T(8,128)(2,1)} %bitcast.82), kind=kOutput, calls=%fused_computation.5 | convolution fusion | flops 1412038656 | bytes 6619136 | tf_op jit(solution)/shard_map/dot_general | solution.py:199
  297.5 5.5 %fusion.2 = f32[768,1024]{1,0:T(8,128)S(1)} fusion(bf16[768,1792]{1,0:T(8,128)(2,1)} %all-gather.2.cloned.1.call-done, bf16[1024,896]{0,1:T(8,128)(2,1)} %copy-done.7, bf16[1024,896]{0,1:T(8,128)(2,1)} %copy-done.8), kind=kOutput, calls=%fused_computation.7 | convolution fusion | flops 2825912320 | bytes 9568256 | tf_op jit(solution)/shard_map/dot_general | solution.py:189
  303.1 1.6 copy-done.2
  304.7 0.1 slice.62
  304.8 8.0 %shard_map.129 = f32[1,384,1024]{2,1,0:T(8,128)} custom-call(f32[2,384,1024]{2,1,0:T(8,128)} %bitcast.78), custom_call_target="tpu_custom_call" | custom-call | tf_op jit(solution)/shard_map/pallas_call | solution.py:80
  312.9 2.8 add.77.x_ref
  315.7 21.6 %shard_map.130 = f32[3,96,1024]{2,1,0:T(8,128)} custom-call(f32[4,96,1024]{2,1,0:T(8,128)} %add.77.x_ref), custom_call_target="tpu_custom_call" | custom-call | tf_op jit(solution)/shard_map/pallas_call | solution.py:80
  337.2 2.1 reduce_sum.75
  339.4 1.9 fusion.11
  341.3 10.6 %shard_map.131 = f32[3,24,1024]{2,1,0:T(8,128)} custom-call(f32[4,24,1024]{2,1,0:T(8,128)} %bitcast.88), custom_call_target="tpu_custom_call" | custom-call | tf_op jit(solution)/shard_map/pallas_call | solution.py:80
  351.9 1.0 reduce_sum.76
  352.9 1.5 fusion.18
  354.4 5.6 %fusion.7 = f32[1024,1792]{1,0:T(8,128)S(1)} fusion(bf16[768,1792]{1,0:T(8,128)(2,1)} %all-gather.2.cloned.1.call-done, bf16[768,2048]{1,0:T(8,128)(2,1)} %bitcast.83), kind=kOutput, calls=%fused_computation.14 | convolution fusion | flops 2818572288 | bytes 11665408 | tf_op jit(solution)/shard_map/dot_general | solution.py:194
  360.0 2.8 fusion
  (46 shorter events, 0.4 us)
Async XLA Ops:
  7.2 3.0 copy-start.16
  7.2 170.6 %reduce-scatter.2.cloned.1.call-start = ((), (), s32[]{:S(2)}) async-start(), calls=%async_computation.1 | async-start | bytes 6193152 | tf_op jit(solution)/shard_map/reduce_scatter | solution.py:177
  10.3 3.8 %copy-start.17 = (s32[8,7]{1,0:T(8,128)S(1)}, s32[8,7]{1,0:T(8,128)}, u32[]{:S(2)}) copy-start(s32[8,7]{1,0:T(8,128)} %param.12) | copy-start | bytes 676
  10.3 4.0 %copy-start.14 = (bf16[24,1024]{1,0:T(8,128)(2,1)S(1)}, bf16[24,1024]{1,0:T(8,128)(2,1)}, u32[]{:S(2)}) copy-start(bf16[24,1024]{1,0:T(8,128)(2,1)} %param.8) | copy-start | bytes 147460
  10.4 4.0 %copy-start.15 = (bf16[24,1024]{1,0:T(8,128)(2,1)S(1)}, bf16[24,1024]{1,0:T(8,128)(2,1)}, u32[]{:S(2)}) copy-start(bf16[24,1024]{1,0:T(8,128)(2,1)} %param.15) | copy-start | bytes 147460
  14.4 0.6 copy-start.13
  62.9 2.0 copy-start.1
  64.7 1.6 copy-start.4
  65.1 1.9 copy-start.7
  65.1 2.5 copy-start.8
  72.5 0.7 copy-start.18
  72.5 1.9 copy-start.5
  72.5 225.0 %all-gather.2.cloned.1.call-start = ((), (), s32[]{:S(2)}) async-start(), calls=%async_computation.2 | async-start | bytes 3096576 | tf_op jit(solution)/shard_map/all_gather | solution.py:187
  73.2 1.9 copy-start.19
  74.4 2.6 copy-start.9
  186.8 11.9 %copy-start.11 = (bf16[96,896]{1,0:T(8,128)(2,1)S(1)}, bf16[96,896]{1,0:T(8,128)(2,1)}, u32[]{:S(2)}) copy-start(bf16[96,896]{1,0:T(8,128)(2,1)} %get-tuple-element.11.x_ref) | copy-start | bytes 516100
  199.3 41.4 %copy-start.6 = (bf16[2,96,896]{2,1,0:T(8,128)(2,1)S(1)}, bf16[2,96,896]{2,1,0:T(8,128)(2,1)}, u32[]{:S(2)}) copy-start(bf16[2,96,896]{2,1,0:T(8,128)(2,1)} %bitcast_dynamic-update-slice_fusion.1.x_ref) | copy-start | bytes 1032196
  240.7 2.3 copy-start.10
  243.0 3.9 %copy-start.12 = (bf16[2,4,96,896]{3,2,1,0:T(8,128)(2,1)}, bf16[2,4,96,896]{3,2,1,0:T(8,128)(2,1)S(1)}, u32[]{:S(2)}) copy-start(bf16[2,4,96,896]{3,2,1,0:T(8,128)(2,1)S(1)} %copy.18) | copy-start | bytes 4128772
  246.8 1.7 copy-start.3
  303.1 1.7 copy-start.2
  354.4 5.6 %copy-start = (bf16[1024,896]{1,0:T(8,128)(2,1)S(1)}, bf16[1024,896]{1,0:T(8,128)(2,1)}, u32[]{:S(2)}) copy-start(bf16[1024,896]{1,0:T(8,128)(2,1)} %copy.20) | copy-start | bytes 5505028
Sparse Core Ops, SparseCore 0:
  72.7 93.1 reduce-scatter.1
  180.9 57.9 all-gather.1

commit v7 on v6

--- a/solution.py
+++ b/solution.py
@@ -182,8 +182,9 @@
         jnp.dot(hidden, down_w, preferred_element_type=jnp.float32), "tensor", tensor_digits, ids
     ).astype(jnp.bfloat16)
     grad_part = lax.dot_general(cot_rows, down_w, contract_last, preferred_element_type=jnp.float32)
-    grad_hidden = seq_sum_scatter(grad_part, seq_digits, ids)
+    grad_hidden = lax.psum_scatter(grad_part, "seq", scatter_dimension=0, tiled=True)
     grads_part = gate_up_grads(gate, up, sig, act, grad_hidden)
+    grads_part, hidden = lax.optimization_barrier((grads_part, hidden))
     grads = lax.all_gather(grads_part, "seq", axis=0, tiled=True)
     grad_tokens = sum_scatter_rows(
         lax.dot_general(grads, joined, contract_last, preferred_element_type=jnp.float32),

time: 373 us -> 355 us (0.952)
  Pallas kernels: 262 us -> 143 us
  waiting for transfers between devices: 0.06 us -> 101 us
    pallas_call x13 -> x11, Pallas kernels: 262 us -> 143 us  [exchange(): pl.pallas_call(functools.partial(exchange_kernel, axis, n, stride, gather...]
    reduce_scatter x1, waiting for transfers between devices: 0.02 us -> 74.2 us  [per_device(): lax.psum_scatter(partial_value, 'seq', scatter_dimension=0, tiled=True)]
    reduce_scatter x0 -> x1, waiting for transfers between devices: none -> 26.8 us  [per_device(): lax.psum_scatter(grad_part, 'seq', scatter_dimension=0, tiled=True)]
    unnamed x47 -> x37, local copies, waits for them, and re-layouts: 14.7 us -> 15.2 us
  transfers between devices with their start and end apart: 2 -> 3, of which waited for: 0 -> 2; matrix products, arithmetic and copies ran while one was open for 11% -> 12% of each run, Pallas kernels for 48% -> 11%
where the time goes in v7:
time: 355 us; the launch traced here: 351 us
  Pallas kernels  143 us (40%)
  waiting for transfers between devices  101 us (28%)
  other arithmetic  32.4 us (9%)
  local copies, waits for them, and re-layouts  31.1 us (9%)
  matrix products  28.5 us (8%)
  between operations  14.1 us (4%)
    pallas_call x11, Pallas kernels, exchange(): pl.pallas_call(functools.partial(exchange_kernel, axis, n, stride, gather...  143 us
    reduce_scatter x1, waiting for transfers between devices, per_device(): lax.psum_scatter(partial_value, 'seq', scatter_dimension=0, tiled=True)  74.2 us
    reduce_scatter x1, waiting for transfers between devices, per_device(): lax.psum_scatter(grad_part, 'seq', scatter_dimension=0, tiled=True)  26.8 us
    unnamed x37, local copies, waits for them, and re-layouts  15.2 us
    add x4, other arithmetic, sum_scatter_rows(): x = x[0] + jnp.sum(exchange(x, axis, n, stride, False, ids.take()), axis=0)  9.47 us
  transfers between devices with their start and end apart: 3, of which 2 were waited for; matrix products, arithmetic and copies ran while one was open for 12% of the time, Pallas kernels for 11%

profile of v7, /device:TPU:1, one launch (start us, length us, event | category | flops | bytes accessed | tf_op | source)
XLA Modules:
  0.0 350.8 jit_solution(17010358475924829301)
XLA Ops:
  7.2 0.8 constant_dynamic-update-slice_fusion.1
  8.0 0.8 constant_dynamic-update-slice_fusion.x_ref
  8.8 0.6 copy-done.10
  9.5 17.2 %shard_map.119 = bf16[3,24,2048]{2,1,0:T(8,128)(2,1)} custom-call(bf16[24,2048]{1,0:T(8,128)(2,1)} %copy-done.10), custom_call_target="tpu_custom_call" | custom-call | tf_op jit(solution)/shard_map/pallas_call | solution.py:80
  26.6 1.8 fusion.18
  28.4 21.9 %shard_map.120 = bf16[3,4,24,2048]{3,2,1,0:T(8,128)(2,1)} custom-call(bf16[4,24,2048]{2,1,0:T(8,128)(2,1)} %get-tuple-element.17.x_ref), custom_call_target="tpu_custom_call" | custom-call | tf_op jit(solution)/shard_map/pallas_call | solution.py:80
  50.3 2.6 fusion.19
  53.0 4.1 %shard_map.121 = bf16[1,4,4,24,2048]{4,3,2,1,0:T(8,128)(2,1)} custom-call(bf16[4,4,24,2048]{3,2,1,0:T(8,128)(2,1)} %get-tuple-element.12.x_ref), custom_call_target="tpu_custom_call" | custom-call | tf_op jit(solution)/shard_map/pallas_call | solution.py:80
  57.1 1.7 pad_maximum_fusion.1
  58.8 1.1 broadcast_in_dim.45
  60.0 0.4 copy-done.3
  60.4 0.8 copy-done.8
  61.2 0.5 copy-done.14
  61.7 3.4 fusion.5
  65.1 0.0 reduce-scatter.3.cloned.1.call-start
  65.1 2.9 copy.16
  68.0 0.1 copy.15
  68.1 0.1 broadcast_bitcast_fusion
  68.2 3.8 %copy.14 = bf16[1024,896]{0,1:T(8,128)(2,1)} copy(bf16[1024,896]{1,0:T(8,128)(2,1)} %param.9) | data formatting | bytes 3670016 | tf_op args[1]
  72.0 0.1 copy.13
  72.1 0.1 broadcast_bitcast_fusion.1
  72.2 1.9 bitcast_multiply_fusion.1
  74.2 1.2 copy-done.6
  75.4 0.7 copy-done.7
  76.0 4.9 %fusion.3 = f32[768,1792]{1,0:T(8,128)} fusion(bf16[1024,896]{0,1:T(8,128)(2,1)S(1)} %get-tuple-element.18, bf16[1024,896]{0,1:T(8,128)(2,1)S(1)} %get-tuple-element.19, bf16[768,2048]{1,0:T(8,128)(2,1)S(1)} %bitcast.65), kind=kOutput, calls=%fused_computation.8 | convolution fusion | flops 2825912320 | bytes 10747904 | tf_op jit(solution)/shard_map/dot_general | solution.py:176
  81.0 0.2 all-gather.2.cloned.1.call-start
  81.2 26.8 %reduce-scatter.5.cloned.1.call-done = f32[96,896]{1,0:T(8,128)} async-done(((f32[768,896]{1,0:T(8,128)}), f32[96,896]{1,0:T(8,128)}) %reduce-scatter.5.cloned.1.call-update) | async-done | bytes 344080 | tf_op jit(solution)/shard_map/reduce_scatter | solution.py:185
  108.1 74.2 %reduce-scatter.3.cloned.1.call-done = f32[96,1792]{1,0:T(8,128)} async-done(((f32[768,1792]{1,0:T(8,128)}), f32[96,1792]{1,0:T(8,128)}) %reduce-scatter.3.cloned.1.call-update) | async-done | bytes 688144 | tf_op jit(solution)/shard_map/reduce_scatter | solution.py:177
  182.3 2.0 multiply_convert_fusion.2
  184.3 5.6 %shard_map.122 = bf16[2,96,896]{2,1,0:T(8,128)(2,1)} custom-call(bf16[96,896]{1,0:T(8,128)(2,1)} %get-tuple-element.15.x_ref), custom_call_target="tpu_custom_call" | custom-call | tf_op jit(solution)/shard_map/pallas_call | solution.py:80
  189.9 1.6 bitcast_dynamic-update-slice_fusion.1.x_ref
  191.6 17.3 %shard_map.123 = bf16[4,2,96,896]{3,2,1,0:T(8,128)(2,1)} custom-call(bf16[2,96,896]{2,1,0:T(8,128)(2,1)} %bitcast_dynamic-update-slice_fusion.1.x_ref), custom_call_target="tpu_custom_call" | custom-call | tf_op jit(solution)/shard_map/pallas_call | solution.py:80
  208.9 0.8 bitcast_dynamic-update-slice_fusion
  209.7 1.4 copy.17
  211.1 0.8 pad_maximum_fusion.6
  212.0 1.5 broadcast_in_dim.41
  213.5 3.1 copy.19
  216.5 1.5 broadcast_in_dim.39
  218.0 3.8 %copy.18 = bf16[1024,896]{1,0:T(8,128)(2,1)} copy(bf16[1024,896]{0,1:T(8,128)(2,1)} %bitcast.58) | data formatting | bytes 3670016 | tf_op jit(solution)/shard_map/convert_element_type | solution.py:145
  221.8 3.9 %fusion.10 = f32[768,1024]{1,0:T(8,128)S(1)} fusion(bf16[768,896]{1,0:T(8,128)(2,1)S(1)} %bitcast.71, bf16[896,1024]{1,0:T(8,128)(2,1)} %param.11, bf16[112,8,8,128]{3,2,1,0:T(8,128)(2,1)} %bitcast.69), kind=kOutput, calls=%fused_computation.19 | convolution fusion | flops 1410203648 | bytes 8192000 | tf_op jit(solution)/shard_map/dot_general | solution.py:182
  225.7 1.6 copy-done.2
  227.3 0.1 slice.57
  227.4 6.1 %shard_map.124 = f32[1,384,1024]{2,1,0:T(8,128)} custom-call(f32[2,384,1024]{2,1,0:T(8,128)} %bitcast.60), custom_call_target="tpu_custom_call" | custom-call | tf_op jit(solution)/shard_map/pallas_call | solution.py:80
  233.5 2.8 add.56.x_ref
  236.3 21.2 %shard_map.125 = f32[3,96,1024]{2,1,0:T(8,128)} custom-call(f32[4,96,1024]{2,1,0:T(8,128)} %add.56.x_ref), custom_call_target="tpu_custom_call" | custom-call | tf_op jit(solution)/shard_map/pallas_call | solution.py:80
  257.5 2.1 reduce_sum.54
  259.6 1.9 fusion.12
  261.5 11.8 %shard_map.126 = f32[3,24,1024]{2,1,0:T(8,128)} custom-call(f32[4,24,1024]{2,1,0:T(8,128)} %bitcast.67), custom_call_target="tpu_custom_call" | custom-call | tf_op jit(solution)/shard_map/pallas_call | solution.py:80
  273.3 1.0 reduce_sum.55
  274.3 1.5 fusion.15
  275.9 5.2 %multiply_convert_fusion = bf16[896,1024]{1,0:T(8,128)(2,1)} fusion(bf16[768,896]{1,0:T(8,128)(2,1)} %bitcast.72, bf16[112,8,8,128]{3,2,1,0:T(8,128)(2,1)} %bitcast.70, bf16[768,2048]{1,0:T(8,128)(2,1)} %bitcast.63), kind=kOutput, calls=%fused_computation.5 | convolution fusion | flops 1412038656 | bytes 6619136 | tf_op jit(solution)/shard_map/dot_general | solution.py:200
  281.1 5.5 %fusion.2 = f32[768,1024]{1,0:T(8,128)S(1)} fusion(bf16[768,1792]{1,0:T(8,128)(2,1)} %all-gather.2.cloned.1.call-done, bf16[1024,896]{0,1:T(8,128)(2,1)} %copy-done.6, bf16[1024,896]{0,1:T(8,128)(2,1)} %copy-done.7), kind=kOutput, calls=%fused_computation.7 | convolution fusion | flops 2825912320 | bytes 9568256 | tf_op jit(solution)/shard_map/dot_general | solution.py:190
  286.7 1.7 copy-done.1
  288.3 0.1 slice.62
  288.4 5.9 %shard_map.127 = f32[1,384,1024]{2,1,0:T(8,128)} custom-call(f32[2,384,1024]{2,1,0:T(8,128)} %bitcast.59), custom_call_target="tpu_custom_call" | custom-call | tf_op jit(solution)/shard_map/pallas_call | solution.py:80
  294.4 2.8 add.62.x_ref
  297.2 21.2 %shard_map.128 = f32[3,96,1024]{2,1,0:T(8,128)} custom-call(f32[4,96,1024]{2,1,0:T(8,128)} %add.62.x_ref), custom_call_target="tpu_custom_call" | custom-call | tf_op jit(solution)/shard_map/pallas_call | solution.py:80
  318.4 2.1 reduce_sum.58
  320.5 1.9 fusion.11
  322.4 11.0 %shard_map.129 = f32[3,24,1024]{2,1,0:T(8,128)} custom-call(f32[4,24,1024]{2,1,0:T(8,128)} %bitcast.66), custom_call_target="tpu_custom_call" | custom-call | tf_op jit(solution)/shard_map/pallas_call | solution.py:80
  333.5 1.0 reduce_sum.59
  334.5 1.5 fusion.14
  336.0 5.6 %fusion.7 = f32[1024,1792]{1,0:T(8,128)S(1)} fusion(bf16[768,1792]{1,0:T(8,128)(2,1)} %all-gather.2.cloned.1.call-done, bf16[768,2048]{1,0:T(8,128)(2,1)} %bitcast.64), kind=kOutput, calls=%fused_computation.14 | convolution fusion | flops 2818572288 | bytes 11665408 | tf_op jit(solution)/shard_map/dot_general | solution.py:195
  341.6 2.8 fusion
  (33 shorter events, 0.2 us)
Async XLA Ops:
  7.2 100.9 %reduce-scatter.5.cloned.1.call-start = ((), (), s32[]{:S(2)}) async-start(), calls=%async_computation.3 | async-start | bytes 3096576 | tf_op jit(solution)/shard_map/reduce_scatter | solution.py:185
  8.8 0.6 copy-start.10
  53.0 4.1 %copy-start.11 = (s32[7,8]{1,0:T(8,128)S(1)}, s32[7,8]{1,0:T(8,128)}, u32[]{:S(2)}) copy-start(s32[7,8]{1,0:T(8,128)} %param.14) | copy-start | bytes 676
  58.8 1.6 copy-start.3
  58.8 2.9 copy-start.14
  60.0 1.2 copy-start.8
  65.0 3.0 copy-start.12
  65.1 117.2 %reduce-scatter.3.cloned.1.call-start = ((), (), s32[]{:S(2)}) async-start(), calls=%async_computation.2 | async-start | bytes 6193152 | tf_op jit(solution)/shard_map/reduce_scatter | solution.py:177
  68.2 3.8 %copy-start.13 = (s32[8,7]{1,0:T(8,128)S(1)}, s32[8,7]{1,0:T(8,128)}, u32[]{:S(2)}) copy-start(s32[8,7]{1,0:T(8,128)} %param.12) | copy-start | bytes 676
  72.2 3.8 %copy-start.4 = (bf16[2,4,4,24,2048]{4,3,2,1,0:T(8,128)(2,1)S(1)}, bf16[2,4,4,24,2048]{4,3,2,1,0:T(8,128)(2,1)}, u32[]{:S(2)}) copy-start(bf16[2,4,4,24,2048]{4,3,2,1,0:T(8,128)(2,1)} %copy-done.3) | copy-start | bytes 9437188
  74.1 1.2 copy-start.6
  74.1 1.9 copy-start.7
  81.0 200.1 %all-gather.2.cloned.1.call-start = ((), (), s32[]{:S(2)}) async-start(), calls=%async_computation.4 | async-start | bytes 3096576 | tf_op jit(solution)/shard_map/all_gather | solution.py:188
  191.6 17.3 %copy-start.5 = (bf16[2,96,896]{2,1,0:T(8,128)(2,1)S(1)}, bf16[2,96,896]{2,1,0:T(8,128)(2,1)}, u32[]{:S(2)}) copy-start(bf16[2,96,896]{2,1,0:T(8,128)(2,1)} %bitcast_dynamic-update-slice_fusion.1.x_ref) | copy-start | bytes 1032196
  211.1 10.7 %copy-start.9 = (bf16[2,4,96,896]{3,2,1,0:T(8,128)(2,1)}, bf16[2,4,96,896]{3,2,1,0:T(8,128)(2,1)S(1)}, u32[]{:S(2)}) copy-start(bf16[2,4,96,896]{3,2,1,0:T(8,128)(2,1)S(1)} %copy.17) | copy-start | bytes 4128772
  225.6 1.6 copy-start.2
  286.7 1.7 copy-start.1
  336.0 5.6 %copy-start = (bf16[1024,896]{1,0:T(8,128)(2,1)S(1)}, bf16[1024,896]{1,0:T(8,128)(2,1)}, u32[]{:S(2)}) copy-start(bf16[1024,896]{1,0:T(8,128)(2,1)} %copy.18) | copy-start | bytes 5505028
Sparse Core Ops, SparseCore 0:
  65.2 42.8 reduce-scatter.4
  110.8 71.4 reduce-scatter.2
  212.1 42.8 all-gather.1

commit v8 on v7

--- a/solution.py
+++ b/solution.py
@@ -63,6 +63,92 @@
         return carry
 
     lax.fori_loop(1, n, finish, 0)
+
+
+def multi_sum_kernel(axis, groups, *refs):
+    m = len(groups)
+    x_refs, y_refs, sems = refs[:m], refs[m:2 * m], refs[2 * m:]
+    index = lax.axis_index(axis)
+    barrier = pltpu.get_barrier_semaphore()
+    infos = []
+    for n, stride in groups:
+        me = lax.rem(index // stride, n)
+        infos.append((n, stride, me, index - me * stride))
+    for n, stride, me, base in infos:
+
+        def greet(k, carry, n=n, stride=stride, me=me, base=base):
+            j = lax.rem(me + k, n)
+            pl.semaphore_signal(
+                barrier, inc=1, device_id=peer(axis, base + j * stride), device_id_type=MESH
+            )
+            return carry
+
+        lax.fori_loop(1, n, greet, 0)
+    pl.semaphore_wait(barrier, sum(n - 1 for n, _ in groups))
+
+    def remote(g, k, direction):
+        n, stride, me, base = infos[g]
+        other = lax.rem(me + direction * k + n, n)
+        return pltpu.make_async_remote_copy(
+            src_ref=x_refs[g].at[other],
+            dst_ref=y_refs[g].at[k - 1],
+            send_sem=sems[2 * g].at[k - 1],
+            recv_sem=sems[2 * g + 1].at[k - 1],
+            device_id=peer(axis, base + other * stride),
+            device_id_type=MESH,
+        )
+
+    for g in range(m):
+
+        def send(k, carry, g=g):
+            remote(g, k, 1).start()
+            return carry
+
+        lax.fori_loop(1, groups[g][0], send, 0)
+    for g in range(m):
+
+        def finish(k, carry, g=g):
+            remote(g, k, 1).wait_send()
+            remote(g, k, -1).wait_recv()
+            return carry
+
+        lax.fori_loop(1, groups[g][0], finish, 0)
+
+
+def multi_sum(xs, axis, groups, cid):
+    sems = []
+    for n, _ in groups:
+        sems += [pltpu.SemaphoreType.DMA((n - 1,)), pltpu.SemaphoreType.DMA((n - 1,))]
+    ys = pl.pallas_call(
+        functools.partial(multi_sum_kernel, axis, tuple(groups)),
+        out_shape=[
+            jax.ShapeDtypeStruct((n - 1,) + x.shape[1:], x.dtype) for x, (n, _) in zip(xs, groups)
+        ],
+        in_specs=[pl.BlockSpec(memory_space=pl.ANY)] * len(xs),
+        out_specs=[pl.BlockSpec(memory_space=pl.ANY)] * len(xs),
+        scratch_shapes=sems,
+        compiler_params=pltpu.CompilerParams(collective_id=cid, has_side_effects=True),
+    )(*xs)
+    out = []
+    for x, y, (n, stride) in zip(xs, ys, groups):
+        own = lax.dynamic_index_in_dim(x, digit(axis, n, stride), 0, keepdims=False)
+        out.append(own + jnp.sum(y, axis=0))
+    return out
+
+
+def seq_sum_scatter_2d(x, digits, ids):
+    if len(digits) != 2:
+        return lax.psum_scatter(x, "seq", scatter_dimension=0, tiled=True)
+    (ns, ss), (nf, sf) = digits
+    half = x.shape[1] // 2
+    width = x.shape[1] - half
+    a = reorder_blocks(x[:, :half], [ns, nf]).reshape((nf, -1, half))
+    b = x[:, half:].reshape((ns, -1, width))
+    a, b = multi_sum([a, b], "seq", [(nf, sf), (ns, ss)], ids.take())
+    a = a.reshape((ns, -1, half))
+    b = b.reshape((nf, -1, width))
+    a, b = multi_sum([a, b], "seq", [(ns, ss), (nf, sf)], ids.take())
+    return jnp.concatenate([a, b], axis=1)
 
 
 class Ids:
@@ -174,7 +260,7 @@
     gathered = both[:, :feat]
     cot_rows = both[:, feat:]
     partial_value = jnp.dot(gathered, joined, preferred_element_type=jnp.float32)
-    summed = lax.psum_scatter(partial_value, "seq", scatter_dimension=0, tiled=True)
+    summed = seq_sum_scatter_2d(partial_value, seq_digits, ids)
     gate, up, sig, act = gating(summed, width)
     hidden_part = (act * up).astype(jnp.bfloat16)
     hidden = seq_gather(hidden_part, seq_digits, ids)
@@ -182,7 +268,7 @@
         jnp.dot(hidden, down_w, preferred_element_type=jnp.float32), "tensor", tensor_digits, ids
     ).astype(jnp.bfloat16)
     grad_part = lax.dot_general(cot_rows, down_w, contract_last, preferred_element_type=jnp.float32)
-    grad_hidden = lax.psum_scatter(grad_part, "seq", scatter_dimension=0, tiled=True)
+    grad_hidden = seq_sum_scatter_2d(grad_part, seq_digits, ids)
     grads_part = gate_up_grads(gate, up, sig, act, grad_hidden)
     grads_part, hidden = lax.optimization_barrier((grads_part, hidden))
     grads = lax.all_gather(grads_part, "seq", axis=0, tiled=True)

time: 355 us -> 358 us (level)
  waiting for transfers between devices: 101 us -> 0.02 us
  Pallas kernels: 143 us -> 235 us
  other arithmetic: 32.4 us -> 47.7 us
  local copies, waits for them, and re-layouts: 31.1 us -> 35.8 us
  matrix products: 28.5 us -> 24.1 us
    reduce_scatter x2 -> x0, waiting for transfers between devices: 101 us -> none  [the longest x1 74.2 us: per_device(): lax.psum_scatter(partial_value, 'seq', scatter_dimension=0, tiled=True)]
    pallas_call x0 -> x4, Pallas kernels: none -> 85.4 us  [multi_sum(): pl.pallas_call(functools.partial(multi_sum_kernel, axis, tuple(groups)),...]
    add x0 -> x6, other arithmetic: none -> 8.68 us  [multi_sum(): out.append(own + jnp.sum(y, axis=0))]
    reduce_sum x0 -> x4, other arithmetic: none -> 6.8 us  [multi_sum(): out.append(own + jnp.sum(y, axis=0))]
    pallas_call x11, Pallas kernels: 143 us -> 149 us  [exchange(): pl.pallas_call(functools.partial(exchange_kernel, axis, n, stride, gather...]
    slice x0 -> x2, local copies, waits for them, and re-layouts: none -> 3.63 us  [seq_sum_scatter_2d(): b = x[:, half:].reshape((ns, -1, width))]
    unnamed x37 -> x61, local copies, waits for them, and re-layouts: 15.2 us -> 17.3 us
  transfers between devices with their start and end apart: 3 -> 1, of which waited for: 2 -> 0; matrix products, arithmetic and copies ran while one was open for 12% -> 7% of each run, Pallas kernels for 11% -> 11%
where the time goes in v8:
time: 358 us; the launch traced here: 357 us
  Pallas kernels  235 us (66%)
  other arithmetic  47.7 us (13%)
  local copies, waits for them, and re-layouts  35.8 us (10%)
  matrix products  24.1 us (7%)
  between operations  14.6 us (4%)
    pallas_call x11, Pallas kernels, exchange(): pl.pallas_call(functools.partial(exchange_kernel, axis, n, stride, gather...  149 us
    pallas_call x4, Pallas kernels, multi_sum(): pl.pallas_call(functools.partial(multi_sum_kernel, axis, tuple(groups)),...  85.4 us
    unnamed x61, local copies, waits for them, and re-layouts  17.3 us
    add x4, other arithmetic, sum_scatter_rows(): x = x[0] + jnp.sum(exchange(x, axis, n, stride, False, ids.take()), axis=0)  9.34 us
    add x6, other arithmetic, multi_sum(): out.append(own + jnp.sum(y, axis=0))  8.68 us
  transfers between devices with their start and end apart: 1, of which 0 were waited for; matrix products, arithmetic and copies ran while one was open for 7% of the time, Pallas kernels for 11%

profile of v8, /device:TPU:1, one launch (start us, length us, event | category | flops | bytes accessed | tf_op | source)
XLA Modules:
  0.0 357.0 jit_solution(13811038355791295243)
XLA Ops:
  7.2 0.8 constant_dynamic-update-slice_fusion.1
  9.5 17.2 %shard_map.119 = bf16[3,24,2048]{2,1,0:T(8,128)(2,1)} custom-call(bf16[24,2048]{1,0:T(8,128)(2,1)} %copy-done.22), custom_call_target="tpu_custom_call" | custom-call | tf_op jit(solution)/shard_map/pallas_call | solution.py:166
  26.7 1.8 fusion.26
  28.4 21.9 %shard_map.120 = bf16[3,4,24,2048]{3,2,1,0:T(8,128)(2,1)} custom-call(bf16[4,24,2048]{2,1,0:T(8,128)(2,1)} %get-tuple-element.36.x_ref), custom_call_target="tpu_custom_call" | custom-call | tf_op jit(solution)/shard_map/pallas_call | solution.py:166
  50.4 2.6 fusion.27
  53.0 4.1 %shard_map.121 = bf16[1,4,4,24,2048]{4,3,2,1,0:T(8,128)(2,1)} custom-call(bf16[4,4,24,2048]{3,2,1,0:T(8,128)(2,1)} %get-tuple-element.34.x_ref), custom_call_target="tpu_custom_call" | custom-call | tf_op jit(solution)/shard_map/pallas_call | solution.py:166
  57.1 1.7 pad_maximum_fusion.1
  58.9 1.1 broadcast_in_dim.42
  60.0 1.7 copy-done.26
  61.7 1.8 fusion.5
  63.6 1.7 fusion.29
  65.5 1.1 copy-done.4
  66.6 22.4 %shard_map.129 = (f32[3,192,448]{2,1,0:T(8,128)}, f32[1,384,448]{2,1,0:T(8,128)}) custom-call(f32[4,192,448]{2,1,0:T(8,128)} %bitcast.119, f32[2,384,448]{2,1,0:T(8,128)} %bitcast.116), custom_call_target="tpu_custom_call" | custom-call | tf_op jit(solution)/shard_map/pallas_call | solution.py:122
  89.0 1.6 reduce_sum.118
  91.3 1.0 dynamic-slice_add_fusion.1
  92.4 11.3 %shard_map.130 = (f32[1,96,448]{2,1,0:T(8,128)}, f32[3,96,448]{2,1,0:T(8,128)}) custom-call(f32[2,96,448]{2,1,0:T(8,128)} %add.127.refs_0_, f32[4,96,448]{2,1,0:T(8,128)} %bitcast.132), custom_call_target="tpu_custom_call" | custom-call | tf_op jit(solution)/shard_map/pallas_call | solution.py:122
  103.7 1.1 reduce_sum.120
  104.8 1.6 bitcast_add_fusion.2
  106.5 1.6 add_bitcast_fusion
  108.1 2.9 copy.18
  111.2 3.8 %copy.16 = bf16[1024,896]{0,1:T(8,128)(2,1)} copy(bf16[1024,896]{1,0:T(8,128)(2,1)} %param.9) | data formatting | bytes 3670016 | tf_op args[1]
  115.2 1.9 bitcast_multiply_fusion.1
  117.2 1.2 copy-done.14
  118.4 3.1 fusion.3
  121.4 1.9 fusion.28
  123.6 1.5 copy-done.1
  125.1 33.8 %shard_map.122 = (f32[3,192,896]{2,1,0:T(8,128)}, f32[1,384,896]{2,1,0:T(8,128)}) custom-call(f32[4,192,896]{2,1,0:T(8,128)} %bitcast.110, f32[2,384,896]{2,1,0:T(8,128)} %bitcast.107), custom_call_target="tpu_custom_call" | custom-call | tf_op jit(solution)/shard_map/pallas_call | solution.py:122
  159.0 2.8 reduce_sum.93
  161.7 2.6 dynamic-slice_add_fusion
  164.4 1.0 add.112.refs_0_
  165.3 17.9 %shard_map.123 = (f32[1,96,896]{2,1,0:T(8,128)}, f32[3,96,896]{2,1,0:T(8,128)}) custom-call(f32[2,96,896]{2,1,0:T(8,128)} %add.112.refs_0_, f32[4,96,896]{2,1,0:T(8,128)} %bitcast.112), custom_call_target="tpu_custom_call" | custom-call | tf_op jit(solution)/shard_map/pallas_call | solution.py:122
  183.3 1.3 reduce_sum.112
  184.6 1.2 fusion.20
  185.8 0.9 multiply_convert_fusion.1
  186.6 5.2 %shard_map.124 = bf16[2,96,896]{2,1,0:T(8,128)(2,1)} custom-call(bf16[96,896]{1,0:T(8,128)(2,1)} %get-tuple-element.38.x_ref), custom_call_target="tpu_custom_call" | custom-call | tf_op jit(solution)/shard_map/pallas_call | solution.py:166
  192.6 19.3 %shard_map.125 = bf16[4,2,96,896]{3,2,1,0:T(8,128)(2,1)} custom-call(bf16[2,96,896]{2,1,0:T(8,128)(2,1)} %fusion.21.x_ref), custom_call_target="tpu_custom_call" | custom-call | tf_op jit(solution)/shard_map/pallas_call | solution.py:166
  212.7 1.6 copy.20
  215.1 3.3 fusion.10
  218.5 1.7 copy-done.7
  220.3 6.2 %shard_map.126 = f32[1,384,1024]{2,1,0:T(8,128)} custom-call(f32[2,384,1024]{2,1,0:T(8,128)} %bitcast.129), custom_call_target="tpu_custom_call" | custom-call | tf_op jit(solution)/shard_map/pallas_call | solution.py:166
  226.4 2.8 add.123.x_ref
  229.2 20.9 %shard_map.127 = f32[3,96,1024]{2,1,0:T(8,128)} custom-call(f32[4,96,1024]{2,1,0:T(8,128)} %add.123.x_ref), custom_call_target="tpu_custom_call" | custom-call | tf_op jit(solution)/shard_map/pallas_call | solution.py:166
  250.1 1.4 reduce_sum.116
  251.5 1.8 fusion.12
  253.3 13.8 %shard_map.128 = f32[3,24,1024]{2,1,0:T(8,128)} custom-call(f32[4,24,1024]{2,1,0:T(8,128)} %bitcast.140), custom_call_target="tpu_custom_call" | custom-call | tf_op jit(solution)/shard_map/pallas_call | solution.py:166
  267.1 1.0 reduce_sum.117
  268.1 1.5 broadcast_in_dim.39
  269.6 3.1 copy.23
  272.6 1.5 broadcast_in_dim.37
  274.1 3.8 %copy.22 = bf16[1024,896]{1,0:T(8,128)(2,1)} copy(bf16[1024,896]{0,1:T(8,128)(2,1)} %bitcast.127) | data formatting | bytes 3670016 | tf_op jit(solution)/shard_map/convert_element_type | solution.py:231
  277.9 1.5 fusion.23
  279.4 4.8 %multiply_convert_fusion = bf16[896,1024]{1,0:T(8,128)(2,1)} fusion(bf16[768,896]{1,0:T(8,128)(2,1)S(1)} %bitcast.148, bf16[112,8,8,128]{3,2,1,0:T(8,128)(2,1)} %bitcast.143, bf16[768,2048]{1,0:T(8,128)(2,1)} %bitcast.135), kind=kOutput, calls=%fused_computation.5 | convolution fusion | flops 1412038656 | bytes 6619136 | tf_op jit(solution)/shard_map/dot_general | solution.py:286
  284.2 5.5 %fusion.2 = f32[768,1024]{1,0:T(8,128)S(1)} fusion(bf16[768,1792]{1,0:T(8,128)(2,1)} %all-gather.2.cloned.1.call-done, bf16[1024,896]{0,1:T(8,128)(2,1)} %copy-done.14, bf16[1024,896]{0,1:T(8,128)(2,1)} %copy-done.15), kind=kOutput, calls=%fused_computation.7 | convolution fusion | flops 2825912320 | bytes 9568256 | tf_op jit(solution)/shard_map/dot_general | solution.py:276
  289.8 1.7 copy-done.6
  291.6 5.8 %shard_map.131 = f32[1,384,1024]{2,1,0:T(8,128)} custom-call(f32[2,384,1024]{2,1,0:T(8,128)} %bitcast.128), custom_call_target="tpu_custom_call" | custom-call | tf_op jit(solution)/shard_map/pallas_call | solution.py:166
  297.3 2.8 add.135.x_ref
  300.1 21.4 %shard_map.132 = f32[3,96,1024]{2,1,0:T(8,128)} custom-call(f32[4,96,1024]{2,1,0:T(8,128)} %add.135.x_ref), custom_call_target="tpu_custom_call" | custom-call | tf_op jit(solution)/shard_map/pallas_call | solution.py:166
  321.6 2.1 reduce_sum.123
  323.7 1.9 fusion.11
  325.6 13.6 %shard_map.133 = f32[3,24,1024]{2,1,0:T(8,128)} custom-call(f32[4,24,1024]{2,1,0:T(8,128)} %bitcast.141), custom_call_target="tpu_custom_call" | custom-call | tf_op jit(solution)/shard_map/pallas_call | solution.py:166
  339.2 1.0 reduce_sum.124
  340.2 1.5 fusion.22
  341.8 5.6 %fusion.7 = f32[1024,1792]{1,0:T(8,128)S(1)} fusion(bf16[768,1792]{1,0:T(8,128)(2,1)} %all-gather.2.cloned.1.call-done, bf16[768,2048]{1,0:T(8,128)(2,1)} %bitcast.136), kind=kOutput, calls=%fused_computation.14 | convolution fusion | flops 2818572288 | bytes 11665408 | tf_op jit(solution)/shard_map/dot_general | solution.py:281
  347.3 2.8 fusion
  (72 shorter events, 5.7 us)
Async XLA Ops:
  7.2 277.1 %all-gather.2.cloned.1.call-start = ((), (), s32[]{:S(2)}) async-start(), calls=%async_computation | async-start | bytes 3096576 | tf_op jit(solution)/shard_map/all_gather | solution.py:274
  8.8 0.6 copy-start.22
  53.0 4.1 %copy-start.23 = (s32[7,8]{1,0:T(8,128)S(1)}, s32[7,8]{1,0:T(8,128)}, u32[]{:S(2)}) copy-start(s32[7,8]{1,0:T(8,128)} %param.14) | copy-start | bytes 676
  58.8 4.7 %copy-start.9 = (bf16[2,4,4,24,2048]{4,3,2,1,0:T(8,128)(2,1)}, bf16[2,4,4,24,2048]{4,3,2,1,0:T(8,128)(2,1)S(1)}, u32[]{:S(2)}) copy-start(bf16[2,4,4,24,2048]{4,3,2,1,0:T(8,128)(2,1)S(1)} %pad_maximum_fusion.1) | copy-start | bytes 9437188
  58.8 2.9 copy-start.26
  60.0 3.6 copy-start.16
  65.4 1.1 copy-start.4
  88.9 2.4 copy-start.3
  89.0 2.4 copy-start.20
  92.4 14.1 %copy-start.13 = (f32[2,96,448]{2,1,0:T(8,128)S(1)}, f32[2,96,448]{2,1,0:T(8,128)}, u32[]{:S(2)}) copy-start(f32[2,96,448]{2,1,0:T(8,128)} %add.127.refs_0_) | copy-start | bytes 1032196
  108.1 2.9 copy-start.24
  111.2 3.8 %copy-start.25 = (s32[8,7]{1,0:T(8,128)S(1)}, s32[8,7]{1,0:T(8,128)}, u32[]{:S(2)}) copy-start(s32[8,7]{1,0:T(8,128)} %param.12) | copy-start | bytes 676
  115.2 3.2 copy-start.10
  117.1 1.2 copy-start.14
  117.1 4.3 %copy-start.15 = (bf16[1024,896]{0,1:T(8,128)(2,1)}, bf16[1024,896]{0,1:T(8,128)(2,1)S(1)}, u32[]{:S(2)}) copy-start(bf16[1024,896]{0,1:T(8,128)(2,1)S(1)} %get-tuple-element.40) | copy-start | bytes 5505028
  123.5 1.6 copy-start.1
  159.0 2.8 copy-start
  161.7 2.6 copy-start.12
  165.3 19.2 %copy-start.2 = (f32[1,384,896]{2,1,0:T(8,128)S(1)}, f32[1,384,896]{2,1,0:T(8,128)}, u32[]{:S(2)}) copy-start(f32[1,384,896]{2,1,0:T(8,128)} %dynamic-slice_add_fusion) | copy-start | bytes 4128772
  165.3 19.2 %copy-start.8 = (f32[2,96,896]{2,1,0:T(8,128)S(1)}, f32[2,96,896]{2,1,0:T(8,128)}, u32[]{:S(2)}) copy-start(f32[2,96,896]{2,1,0:T(8,128)} %add.112.refs_0_) | copy-start | bytes 2064388
  165.3 19.3 %copy-start.18 = (f32[96,448]{1,0:T(8,128)S(1)}, f32[96,448]{1,0:T(8,128)}, u32[]{:S(2)}) copy-start(f32[96,448]{1,0:T(8,128)} %bitcast_add_fusion.2) | copy-start | bytes 516100
  165.3 19.3 %copy-start.19 = (f32[96,448]{1,0:T(8,128)S(1)}, f32[96,448]{1,0:T(8,128)}, u32[]{:S(2)}) copy-start(f32[96,448]{1,0:T(8,128)} %add_bitcast_fusion) | copy-start | bytes 516100
  192.6 19.3 %copy-start.11 = (bf16[2,96,896]{2,1,0:T(8,128)(2,1)S(1)}, bf16[2,96,896]{2,1,0:T(8,128)(2,1)}, u32[]{:S(2)}) copy-start(bf16[2,96,896]{2,1,0:T(8,128)(2,1)} %fusion.21.x_ref) | copy-start | bytes 1032196
  211.9 2.4 copy-start.21
  212.7 2.4 copy-start.17
  218.4 1.7 copy-start.7
  289.8 1.7 copy-start.6
  341.8 5.6 %copy-start.5 = (bf16[1024,896]{1,0:T(8,128)(2,1)S(1)}, bf16[1024,896]{1,0:T(8,128)(2,1)}, u32[]{:S(2)}) copy-start(bf16[1024,896]{1,0:T(8,128)(2,1)} %copy.22) | copy-start | bytes 5505028
Sparse Core Ops, SparseCore 0:
  215.2 42.3 all-gather.1

commit v9 on v8

--- a/solution.py
+++ b/solution.py
@@ -256,9 +256,11 @@
     contract_first = (((0,), (0,)), ((), ()))
     contract_last = (((1,), (1,)), ((), ()))
     ids = Ids()
-    both = gather_rows(jnp.concatenate([tokens, cotangent], axis=1), "tensor", tensor_digits, ids)
-    gathered = both[:, :feat]
-    cot_rows = both[:, feat:]
+    cot_rows = gather_rows(cotangent, "tensor", tensor_digits, ids)
+    grad_part = lax.dot_general(cot_rows, down_w, contract_last, preferred_element_type=jnp.float32)
+    grad_part, tokens = lax.optimization_barrier((grad_part, tokens))
+    grad_hidden = lax.psum_scatter(grad_part, "seq", scatter_dimension=0, tiled=True)
+    gathered = gather_rows(tokens, "tensor", tensor_digits, ids)
     partial_value = jnp.dot(gathered, joined, preferred_element_type=jnp.float32)
     summed = seq_sum_scatter_2d(partial_value, seq_digits, ids)
     gate, up, sig, act = gating(summed, width)
@@ -267,8 +269,6 @@
     output = sum_scatter_rows(
         jnp.dot(hidden, down_w, preferred_element_type=jnp.float32), "tensor", tensor_digits, ids
     ).astype(jnp.bfloat16)
-    grad_part = lax.dot_general(cot_rows, down_w, contract_last, preferred_element_type=jnp.float32)
-    grad_hidden = seq_sum_scatter_2d(grad_part, seq_digits, ids)
     grads_part = gate_up_grads(gate, up, sig, act, grad_hidden)
     grads_part, hidden = lax.optimization_barrier((grads_part, hidden))
     grads = lax.all_gather(grads_part, "seq", axis=0, tiled=True)

time: 358 us -> 328 us (0.916)
  Pallas kernels: 235 us -> 211 us
  other arithmetic: 47.7 us -> 42.4 us
  local copies, waits for them, and re-layouts: 35.8 us -> 31.6 us
    pallas_call x4 -> x2, Pallas kernels: 85.4 us -> 53 us  [multi_sum(): pl.pallas_call(functools.partial(multi_sum_kernel, axis, tuple(groups)),...]
    pallas_call x11 -> x14, Pallas kernels: 149 us -> 159 us  [exchange(): pl.pallas_call(functools.partial(exchange_kernel, axis, n, stride, gather...]
    add x6 -> x2, other arithmetic: 8.68 us -> 3.49 us  [multi_sum(): out.append(own + jnp.sum(y, axis=0))]
    unnamed x61 -> x54, local copies, waits for them, and re-layouts: 17.3 us -> 13.1 us
    reduce_sum x4 -> x2, other arithmetic: 6.8 us -> 3.08 us  [multi_sum(): out.append(own + jnp.sum(y, axis=0))]
    broadcast_in_dim x2 -> x4, other arithmetic: 4.4 us -> 7.34 us  [gather_rows(): x[None]]
  transfers between devices with their start and end apart: 1 -> 2, of which waited for: 0 -> 0; matrix products, arithmetic and copies ran while one was open for 7% -> 17% of each run, Pallas kernels for 11% -> 37%
where the time goes in v9:
time: 328 us; the launch traced here: 327 us
  Pallas kernels  211 us (64%)
  other arithmetic  42.4 us (13%)
  local copies, waits for them, and re-layouts  31.6 us (10%)
  matrix products  26.6 us (8%)
  between operations  14.6 us (4%)
    pallas_call x14, Pallas kernels, exchange(): pl.pallas_call(functools.partial(exchange_kernel, axis, n, stride, gather...  159 us
    pallas_call x2, Pallas kernels, multi_sum(): pl.pallas_call(functools.partial(multi_sum_kernel, axis, tuple(groups)),...  53 us
    unnamed x54, local copies, waits for them, and re-layouts  13.1 us
    add x4, other arithmetic, sum_scatter_rows(): x = x[0] + jnp.sum(exchange(x, axis, n, stride, False, ids.take()), axis=0)  9.47 us
    broadcast_in_dim x4, other arithmetic, gather_rows(): x[None]  7.34 us
    convert_element_type x4, local copies, waits for them, and re-layouts, widen(): return full.astype(jnp.bfloat16)  7.06 us
  transfers between devices with their start and end apart: 2, of which 0 were waited for; matrix products, arithmetic and copies ran while one was open for 17% of the time, Pallas kernels for 37%

profile of v9, /device:TPU:1, one launch (start us, length us, event | category | flops | bytes accessed | tf_op | source)
XLA Modules:
  0.0 327.0 jit_solution(7846047776684370102)
XLA Ops:
  7.2 12.6 %shard_map.119 = bf16[3,24,1024]{2,1,0:T(8,128)(2,1)} custom-call(bf16[24,1024]{1,0:T(8,128)(2,1)} %x_ref.1), custom_call_target="tpu_custom_call" | custom-call | tf_op jit(solution)/shard_map/pallas_call | solution.py:166
  19.8 1.6 fusion.22
  21.4 13.1 %shard_map.120 = bf16[3,4,24,1024]{3,2,1,0:T(8,128)(2,1)} custom-call(bf16[4,24,1024]{2,1,0:T(8,128)(2,1)} %get-tuple-element.36.x_ref), custom_call_target="tpu_custom_call" | custom-call | tf_op jit(solution)/shard_map/pallas_call | solution.py:166
  34.5 2.1 fusion.24
  36.6 3.4 %shard_map.121 = bf16[1,4,4,24,1024]{4,3,2,1,0:T(8,128)(2,1)} custom-call(bf16[4,4,24,1024]{3,2,1,0:T(8,128)(2,1)} %get-tuple-element.30.x_ref), custom_call_target="tpu_custom_call" | custom-call | tf_op jit(solution)/shard_map/pallas_call | solution.py:166
  40.0 1.3 pad_maximum_fusion.3
  41.3 1.1 broadcast_in_dim.46
  42.5 1.2 copy-done.10
  43.7 3.4 %fusion.5 = f32[768,896]{1,0:T(8,128)} fusion(bf16[768,1024]{1,0:T(8,128)(2,1)S(1)} %bitcast.132, bf16[896,1024]{1,0:T(8,128)(2,1)S(1)} %copy-done.23, bf16[112,8,8,128]{3,2,1,0:T(8,128)(2,1)S(1)} %bitcast.129), kind=kOutput, calls=%fused_computation.17 | convolution fusion | flops 1410203648 | bytes 7995392 | tf_op jit(solution)/shard_map/dot_general | solution.py:260
  47.3 11.4 %shard_map.122 = bf16[3,24,1024]{2,1,0:T(8,128)(2,1)} custom-call(bf16[24,1024]{1,0:T(8,128)(2,1)} %x_ref.2), custom_call_target="tpu_custom_call" | custom-call | tf_op jit(solution)/shard_map/pallas_call | solution.py:166
  58.8 1.6 fusion.21
  60.4 13.1 %shard_map.123 = bf16[3,4,24,1024]{3,2,1,0:T(8,128)(2,1)} custom-call(bf16[4,24,1024]{2,1,0:T(8,128)(2,1)} %get-tuple-element.34.x_ref), custom_call_target="tpu_custom_call" | custom-call | tf_op jit(solution)/shard_map/pallas_call | solution.py:166
  73.5 2.1 fusion.23
  75.6 2.8 shard_map.124
  78.4 2.9 copy.17
  81.5 3.8 %copy.15 = bf16[1024,896]{0,1:T(8,128)(2,1)} copy(bf16[1024,896]{1,0:T(8,128)(2,1)} %param.9) | data formatting | bytes 3670016 | tf_op args[1]
  85.6 1.8 bitcast_multiply_fusion.1
  87.6 1.0 copy-done.8
  88.6 0.6 copy-done.9
  89.2 3.1 fusion.3
  92.3 1.9 fusion.25
  94.2 1.7 copy.18
  95.9 34.0 %shard_map.125 = (f32[3,192,896]{2,1,0:T(8,128)}, f32[1,384,896]{2,1,0:T(8,128)}) custom-call(f32[4,192,896]{2,1,0:T(8,128)} %bitcast.107, f32[2,384,896]{2,1,0:T(8,128)} %bitcast.105), custom_call_target="tpu_custom_call" | custom-call | tf_op jit(solution)/shard_map/pallas_call | solution.py:122
  129.9 1.8 reduce_sum.82
  131.7 1.3 constant_dynamic-slice_fusion
  133.0 0.9 add.86.refs_0_
  133.9 2.6 dynamic-slice_add_fusion
  136.5 19.0 %shard_map.126 = (f32[1,96,896]{2,1,0:T(8,128)}, f32[3,96,896]{2,1,0:T(8,128)}) custom-call(f32[2,96,896]{2,1,0:T(8,128)} %add.86.refs_0_, f32[4,96,896]{2,1,0:T(8,128)} %bitcast.110), custom_call_target="tpu_custom_call" | custom-call | tf_op jit(solution)/shard_map/pallas_call | solution.py:122
  155.5 1.3 reduce_sum.84
  156.9 1.3 fusion.15
  158.2 0.8 multiply_convert_fusion.1
  159.0 4.6 %shard_map.127 = bf16[2,96,896]{2,1,0:T(8,128)(2,1)} custom-call(bf16[96,896]{1,0:T(8,128)(2,1)} %get-tuple-element.32.x_ref), custom_call_target="tpu_custom_call" | custom-call | tf_op jit(solution)/shard_map/pallas_call | solution.py:166
  163.6 0.8 fusion.16.x_ref
  164.4 18.2 %shard_map.128 = bf16[4,2,96,896]{3,2,1,0:T(8,128)(2,1)} custom-call(bf16[2,96,896]{2,1,0:T(8,128)(2,1)} %fusion.16.x_ref), custom_call_target="tpu_custom_call" | custom-call | tf_op jit(solution)/shard_map/pallas_call | solution.py:166
  182.6 0.8 bitcast_dynamic-update-slice_fusion
  183.3 1.5 copy.19
  184.8 0.8 pad_maximum_fusion.7
  185.7 1.5 broadcast_in_dim.53
  187.1 3.1 copy.21
  190.2 1.5 broadcast_in_dim.51
  191.7 3.8 %copy.20 = bf16[1024,896]{1,0:T(8,128)(2,1)} copy(bf16[1024,896]{0,1:T(8,128)(2,1)} %bitcast.121) | data formatting | bytes 3670016 | tf_op jit(solution)/shard_map/convert_element_type | solution.py:231
  195.5 3.9 %fusion.4 = f32[768,1024]{1,0:T(8,128)S(1)} fusion(bf16[768,896]{1,0:T(8,128)(2,1)S(1)} %bitcast.136, bf16[896,1024]{1,0:T(8,128)(2,1)} %param.11, bf16[112,8,8,128]{3,2,1,0:T(8,128)(2,1)} %bitcast.130), kind=kOutput, calls=%fused_computation.16 | convolution fusion | flops 1410203648 | bytes 8192000 | tf_op jit(solution)/shard_map/dot_general | solution.py:270
  199.3 1.6 copy-done.4
  201.1 6.2 %shard_map.129 = f32[1,384,1024]{2,1,0:T(8,128)} custom-call(f32[2,384,1024]{2,1,0:T(8,128)} %bitcast.123), custom_call_target="tpu_custom_call" | custom-call | tf_op jit(solution)/shard_map/pallas_call | solution.py:166
  207.3 2.8 add.97.x_ref
  210.2 20.7 %shard_map.130 = f32[3,96,1024]{2,1,0:T(8,128)} custom-call(f32[4,96,1024]{2,1,0:T(8,128)} %add.97.x_ref), custom_call_target="tpu_custom_call" | custom-call | tf_op jit(solution)/shard_map/pallas_call | solution.py:166
  230.8 2.1 reduce_sum.88
  233.0 1.9 fusion.7
  234.9 12.6 %shard_map.131 = f32[3,24,1024]{2,1,0:T(8,128)} custom-call(f32[4,24,1024]{2,1,0:T(8,128)} %bitcast.128), custom_call_target="tpu_custom_call" | custom-call | tf_op jit(solution)/shard_map/pallas_call | solution.py:166
  247.5 1.0 reduce_sum.89
  248.5 1.5 fusion.18
  250.0 5.2 %multiply_convert_fusion = bf16[896,1024]{1,0:T(8,128)(2,1)} fusion(bf16[768,896]{1,0:T(8,128)(2,1)} %bitcast.137, bf16[768,1024]{1,0:T(8,128)(2,1)} %bitcast.133, bf16[112,8,8,128]{3,2,1,0:T(8,128)(2,1)} %bitcast.131), kind=kOutput, calls=%fused_computation.5 | convolution fusion | flops 1412038656 | bytes 6619136 | tf_op jit(solution)/shard_map/dot_general | solution.py:286
  255.3 5.5 %fusion.2 = f32[768,1024]{1,0:T(8,128)S(1)} fusion(bf16[768,1792]{1,0:T(8,128)(2,1)} %all-gather.2.cloned.1.call-done, bf16[1024,896]{0,1:T(8,128)(2,1)} %copy-done.8, bf16[1024,896]{0,1:T(8,128)(2,1)} %copy-done.9), kind=kOutput, calls=%fused_computation.6 | convolution fusion | flops 2825912320 | bytes 9568256 | tf_op jit(solution)/shard_map/dot_general | solution.py:276
  260.8 1.6 copy-done.3
  262.6 6.8 %shard_map.132 = f32[1,384,1024]{2,1,0:T(8,128)} custom-call(f32[2,384,1024]{2,1,0:T(8,128)} %bitcast.122), custom_call_target="tpu_custom_call" | custom-call | tf_op jit(solution)/shard_map/pallas_call | solution.py:166
  269.4 2.8 add.103.x_ref
  272.2 20.8 %shard_map.133 = f32[3,96,1024]{2,1,0:T(8,128)} custom-call(f32[4,96,1024]{2,1,0:T(8,128)} %add.103.x_ref), custom_call_target="tpu_custom_call" | custom-call | tf_op jit(solution)/shard_map/pallas_call | solution.py:166
  292.9 2.1 reduce_sum.92
  295.1 1.9 fusion.6
  297.0 12.3 %shard_map.134 = f32[3,24,1024]{2,1,0:T(8,128)} custom-call(f32[4,24,1024]{2,1,0:T(8,128)} %bitcast.127), custom_call_target="tpu_custom_call" | custom-call | tf_op jit(solution)/shard_map/pallas_call | solution.py:166
  309.3 1.0 reduce_sum.93
  310.3 1.5 fusion.17
  311.8 5.6 %fusion.26 = f32[1024,1792]{1,0:T(8,128)S(1)} fusion(bf16[768,1024]{1,0:T(8,128)(2,1)} %bitcast.135, bf16[768,1792]{1,0:T(8,128)(2,1)} %all-gather.2.cloned.1.call-done), kind=kOutput, calls=%fused_computation.59 | convolution fusion | flops 2818572288 | bytes 11665408 | tf_op jit(solution)/shard_map/dot_general | solution.py:281
  317.4 2.8 fusion
  (62 shorter events, 1.2 us)
Async XLA Ops:
  7.2 149.7 %reduce-scatter.2.cloned.1.call-start = ((), (), s32[]{:S(2)}) async-start(), calls=%async_computation.1 | async-start | bytes 3096576 | tf_op jit(solution)/shard_map/reduce_scatter | solution.py:262
  34.5 5.4 %copy-start.20 = (s32[7,8]{1,0:T(8,128)S(1)}, s32[7,8]{1,0:T(8,128)}, u32[]{:S(2)}) copy-start(s32[7,8]{1,0:T(8,128)} %param.14) | copy-start | bytes 676
  41.2 1.2 copy-start.11
  41.3 2.4 copy-start.23
  42.4 1.2 copy-start.10
  47.0 11.7 %copy-start.15 = (bf16[24,1024]{1,0:T(8,128)(2,1)S(1)}, bf16[24,1024]{1,0:T(8,128)(2,1)}, u32[]{:S(2)}) copy-start(bf16[24,1024]{1,0:T(8,128)(2,1)} %x_ref.2) | copy-start | bytes 147460
  47.1 208.2 %all-gather.2.cloned.1.call-start = ((), (), s32[]{:S(2)}) async-start(), calls=%async_computation.2 | async-start | bytes 3096576 | tf_op jit(solution)/shard_map/all_gather | solution.py:274
  78.4 2.9 copy-start.21
  81.5 4.0 %copy-start.16 = (bf16[1,7,8,128]{3,1,2,0:T(8,128)(2,1)}, bf16[1,7,8,128]{3,1,2,0:T(8,128)(2,1)S(1)}, u32[]{:S(2)}) copy-start(bf16[1,7,8,128]{3,1,2,0:T(8,128)(2,1)S(1)} %copy.31) | copy-start | bytes 43012
  81.5 3.8 %copy-start.22 = (s32[8,7]{1,0:T(8,128)S(1)}, s32[8,7]{1,0:T(8,128)}, u32[]{:S(2)}) copy-start(s32[8,7]{1,0:T(8,128)} %param.12) | copy-start | bytes 676
  85.5 1.9 copy-start.18
  85.6 1.9 copy-start.6
  87.4 1.2 copy-start.8
  87.4 1.8 copy-start.9
  87.6 4.7 %copy-start.12 = (bf16[2,4,4,24,1024]{4,3,2,1,0:T(8,128)(2,1)}, bf16[2,4,4,24,1024]{4,3,2,1,0:T(8,128)(2,1)S(1)}, u32[]{:S(2)}) copy-start(bf16[2,4,4,24,1024]{4,3,2,1,0:T(8,128)(2,1)S(1)} %pad_maximum_fusion.4) | copy-start | bytes 4718596
  131.7 2.2 copy-start
  136.5 20.4 %copy-start.1 = (f32[1,384,896]{2,1,0:T(8,128)S(1)}, f32[1,384,896]{2,1,0:T(8,128)}, u32[]{:S(2)}) copy-start(f32[1,384,896]{2,1,0:T(8,128)} %dynamic-slice_add_fusion) | copy-start | bytes 4128772
  136.5 20.4 %copy-start.5 = (f32[2,96,896]{2,1,0:T(8,128)S(1)}, f32[2,96,896]{2,1,0:T(8,128)}, u32[]{:S(2)}) copy-start(f32[2,96,896]{2,1,0:T(8,128)} %add.86.refs_0_) | copy-start | bytes 2064388
  156.8 1.3 copy-start.14
  164.4 18.2 %copy-start.7 = (bf16[2,96,896]{2,1,0:T(8,128)(2,1)S(1)}, bf16[2,96,896]{2,1,0:T(8,128)(2,1)}, u32[]{:S(2)}) copy-start(bf16[2,96,896]{2,1,0:T(8,128)(2,1)} %fusion.16.x_ref) | copy-start | bytes 1032196
  183.3 2.3 copy-start.17
  184.8 10.7 %copy-start.13 = (bf16[2,4,96,896]{3,2,1,0:T(8,128)(2,1)}, bf16[2,4,96,896]{3,2,1,0:T(8,128)(2,1)S(1)}, u32[]{:S(2)}) copy-start(bf16[2,4,96,896]{3,2,1,0:T(8,128)(2,1)S(1)} %copy.19) | copy-start | bytes 4128772
  187.1 3.1 copy-start.19
  199.3 1.7 copy-start.4
  260.8 1.7 copy-start.3
  311.8 5.6 %copy-start.2 = (bf16[1024,896]{1,0:T(8,128)(2,1)S(1)}, bf16[1024,896]{1,0:T(8,128)(2,1)}, u32[]{:S(2)}) copy-start(bf16[1024,896]{1,0:T(8,128)(2,1)} %copy.20) | copy-start | bytes 5505028
Sparse Core Ops, SparseCore 0:
  47.2 42.6 reduce-scatter.1
  185.8 40.3 all-gather.1

commit v10 on v9

--- a/solution.py
+++ b/solution.py
@@ -65,7 +65,7 @@
     lax.fori_loop(1, n, finish, 0)
 
 
-def multi_sum_kernel(axis, groups, *refs):
+def multi_sum_kernel(axis, groups, relative, *refs):
     m = len(groups)
     x_refs, y_refs, sems = refs[:m], refs[m:2 * m], refs[2 * m:]
     index = lax.axis_index(axis)
@@ -90,7 +90,7 @@
         n, stride, me, base = infos[g]
         other = lax.rem(me + direction * k + n, n)
         return pltpu.make_async_remote_copy(
-            src_ref=x_refs[g].at[other],
+            src_ref=x_refs[g].at[k if relative else other],
             dst_ref=y_refs[g].at[k - 1],
             send_sem=sems[2 * g].at[k - 1],
             recv_sem=sems[2 * g + 1].at[k - 1],
@@ -115,12 +115,12 @@
         lax.fori_loop(1, groups[g][0], finish, 0)
 
 
-def multi_sum(xs, axis, groups, cid):
+def multi_sum(xs, axis, groups, cid, relative=False):
     sems = []
     for n, _ in groups:
         sems += [pltpu.SemaphoreType.DMA((n - 1,)), pltpu.SemaphoreType.DMA((n - 1,))]
     ys = pl.pallas_call(
-        functools.partial(multi_sum_kernel, axis, tuple(groups)),
+        functools.partial(multi_sum_kernel, axis, tuple(groups), relative),
         out_shape=[
             jax.ShapeDtypeStruct((n - 1,) + x.shape[1:], x.dtype) for x, (n, _) in zip(xs, groups)
         ],
@@ -131,9 +131,30 @@
     )(*xs)
     out = []
     for x, y, (n, stride) in zip(xs, ys, groups):
-        own = lax.dynamic_index_in_dim(x, digit(axis, n, stride), 0, keepdims=False)
+        if relative:
+            own = x[0]
+        else:
+            own = lax.dynamic_index_in_dim(x, digit(axis, n, stride), 0, keepdims=False)
         out.append(own + jnp.sum(y, axis=0))
     return out
+
+
+def tensor_sum_scatter(x, digits, ids):
+    if len(digits) != 3:
+        return sum_scatter_rows(x, "tensor", digits, ids)
+    (nf, sf), (nn, sn), (nc, sc) = digits
+    cols = x.shape[-1]
+    x = x.reshape((nc, -1, cols))
+    x = x[0] + jnp.sum(exchange(x, "tensor", nc, sc, False, ids.take()), axis=0)
+    half = cols // 2
+    a = x[:, :half].reshape((nn, -1, half))
+    b = x[:, half:].reshape((nn, nf, -1, cols - half))
+    b = jnp.swapaxes(b, 0, 1).reshape((nf, -1, cols - half))
+    a, b = multi_sum([a, b], "tensor", [(nn, sn), (nf, sf)], ids.take(), relative=True)
+    a = a.reshape((nf, -1, half))
+    b = b.reshape((nn, -1, cols - half))
+    a, b = multi_sum([a, b], "tensor", [(nf, sf), (nn, sn)], ids.take(), relative=True)
+    return jnp.concatenate([a, b], axis=1)
 
 
 def seq_sum_scatter_2d(x, digits, ids):
@@ -266,15 +287,14 @@
     gate, up, sig, act = gating(summed, width)
     hidden_part = (act * up).astype(jnp.bfloat16)
     hidden = seq_gather(hidden_part, seq_digits, ids)
-    output = sum_scatter_rows(
-        jnp.dot(hidden, down_w, preferred_element_type=jnp.float32), "tensor", tensor_digits, ids
+    output = tensor_sum_scatter(
+        jnp.dot(hidden, down_w, preferred_element_type=jnp.float32), tensor_digits, ids
     ).astype(jnp.bfloat16)
     grads_part = gate_up_grads(gate, up, sig, act, grad_hidden)
     grads_part, hidden = lax.optimization_barrier((grads_part, hidden))
     grads = lax.all_gather(grads_part, "seq", axis=0, tiled=True)
-    grad_tokens = sum_scatter_rows(
+    grad_tokens = tensor_sum_scatter(
         lax.dot_general(grads, joined, contract_last, preferred_element_type=jnp.float32),
-        "tensor",
         tensor_digits,
         ids,
     ).astype(jnp.bfloat16)

time: 328 us -> 347 us (1.058)
  other arithmetic: 42.4 us -> 50.2 us
  Pallas kernels: 211 us -> 215 us
  local copies, waits for them, and re-layouts: 31.6 us -> 35.4 us
    pallas_call x2 -> x6, Pallas kernels: 53 us -> 125 us  [multi_sum(): pl.pallas_call(functools.partial(multi_sum_kernel, axis, tuple(groups), r...]
    pallas_call x14 -> x10, Pallas kernels: 159 us -> 90 us  [exchange(): pl.pallas_call(functools.partial(exchange_kernel, axis, n, stride, gather...]
    reduce_sum x2 -> x10, other arithmetic: 3.08 us -> 14.1 us  [multi_sum(): out.append(own + jnp.sum(y, axis=0))]
    add x2 -> x6, other arithmetic: 3.49 us -> 10.2 us  [multi_sum(): out.append(own + jnp.sum(y, axis=0))]
    reduce_sum x4 -> x0, other arithmetic: 6.24 us -> none  [sum_scatter_rows(): x = x[0] + jnp.sum(exchange(x, axis, n, stride, False, ids.take()), axis=0)]
    add x4 -> x2, other arithmetic: 9.47 us -> 4.32 us  [tensor_sum_scatter(): x = x[0] + jnp.sum(exchange(x, 'tensor', nc, sc, False, ids.take()), axis=0)]
    slice x2 -> x4, local copies, waits for them, and re-layouts: 0.2 us -> 5.27 us  [the longest x2 3.23 us: multi_sum(): own = x[0]]
    unnamed x54 -> x52, local copies, waits for them, and re-layouts: 13.1 us -> 9.83 us
  transfers between devices with their start and end apart: 2 -> 2, of which waited for: 0 -> 0; matrix products, arithmetic and copies ran while one was open for 17% -> 19% of each run, Pallas kernels for 37% -> 37%
where the time goes in v10:
time: 347 us; the launch traced here: 345 us
  Pallas kernels  215 us (62%)
  other arithmetic  50.2 us (14%)
  local copies, waits for them, and re-layouts  35.4 us (10%)
  matrix products  29.7 us (9%)
  between operations  14.6 us (4%)
    pallas_call x6, Pallas kernels, multi_sum(): pl.pallas_call(functools.partial(multi_sum_kernel, axis, tuple(groups), r...  125 us
    pallas_call x10, Pallas kernels, exchange(): pl.pallas_call(functools.partial(exchange_kernel, axis, n, stride, gather...  90 us
    reduce_sum x10, other arithmetic, multi_sum(): out.append(own + jnp.sum(y, axis=0))  14.1 us
    add x6, other arithmetic, multi_sum(): out.append(own + jnp.sum(y, axis=0))  10.2 us
    unnamed x52, local copies, waits for them, and re-layouts  9.83 us
    dot_general x1, matrix products, per_device(): lax.dot_general(grads, joined, contract_last, preferred_element_type=jnp....  7.52 us
    broadcast_in_dim x4, other arithmetic, gather_rows(): x[None]  7.34 us
    convert_element_type x4, local copies, waits for them, and re-layouts, widen(): return full.astype(jnp.bfloat16)  7.04 us
  transfers between devices with their start and end apart: 2, of which 0 were waited for; matrix products, arithmetic and copies ran while one was open for 19% of the time, Pallas kernels for 37%

profile of v10, /device:TPU:1, one launch (start us, length us, event | category | flops | bytes accessed | tf_op | source)
XLA Modules:
  0.0 345.5 jit_solution(5385273136628075392)
XLA Ops:
  7.2 12.6 %shard_map.119 = bf16[3,24,1024]{2,1,0:T(8,128)(2,1)} custom-call(bf16[24,1024]{1,0:T(8,128)(2,1)} %x_ref.1), custom_call_target="tpu_custom_call" | custom-call | tf_op jit(solution)/shard_map/pallas_call | solution.py:187
  19.8 1.6 fusion.24
  21.4 13.1 %shard_map.120 = bf16[3,4,24,1024]{3,2,1,0:T(8,128)(2,1)} custom-call(bf16[4,24,1024]{2,1,0:T(8,128)(2,1)} %get-tuple-element.60.x_ref), custom_call_target="tpu_custom_call" | custom-call | tf_op jit(solution)/shard_map/pallas_call | solution.py:187
  34.5 2.1 fusion.26
  36.6 3.4 shard_map.121
  40.0 1.3 pad_maximum_fusion.3
  41.3 1.1 broadcast_in_dim.46
  42.5 1.2 copy-done.8
  43.7 3.4 fusion.5
  47.3 11.4 %shard_map.122 = bf16[3,24,1024]{2,1,0:T(8,128)(2,1)} custom-call(bf16[24,1024]{1,0:T(8,128)(2,1)} %x_ref.2), custom_call_target="tpu_custom_call" | custom-call | tf_op jit(solution)/shard_map/pallas_call | solution.py:187
  58.8 1.6 fusion.23
  60.4 13.1 %shard_map.123 = bf16[3,4,24,1024]{3,2,1,0:T(8,128)(2,1)} custom-call(bf16[4,24,1024]{2,1,0:T(8,128)(2,1)} %get-tuple-element.58.x_ref), custom_call_target="tpu_custom_call" | custom-call | tf_op jit(solution)/shard_map/pallas_call | solution.py:187
  73.5 2.1 fusion.25
  75.6 2.8 shard_map.124
  78.4 2.9 copy.17
  81.5 3.8 %copy.15 = bf16[1024,896]{0,1:T(8,128)(2,1)} copy(bf16[1024,896]{1,0:T(8,128)(2,1)} %param.9) | data formatting | bytes 3670016 | tf_op args[1]
  85.6 1.8 bitcast_multiply_fusion.1
  87.6 1.0 copy-done.6
  89.2 3.1 fusion.3
  92.3 1.9 fusion.27
  94.2 1.7 copy.18
  96.0 34.0 %shard_map.125 = (f32[3,192,896]{2,1,0:T(8,128)}, f32[1,384,896]{2,1,0:T(8,128)}) custom-call(f32[4,192,896]{2,1,0:T(8,128)} %bitcast.127, f32[2,384,896]{2,1,0:T(8,128)} %bitcast.125), custom_call_target="tpu_custom_call" | custom-call | tf_op jit(solution)/shard_map/pallas_call | solution.py:122
  129.9 1.8 reduce_sum.118
  131.7 1.3 constant_dynamic-slice_fusion
  133.9 2.6 dynamic-slice_add_fusion
  136.5 19.0 %shard_map.126 = (f32[1,96,896]{2,1,0:T(8,128)}, f32[3,96,896]{2,1,0:T(8,128)}) custom-call(f32[2,96,896]{2,1,0:T(8,128)} %add.98.refs_0_, f32[4,96,896]{2,1,0:T(8,128)} %bitcast.130), custom_call_target="tpu_custom_call" | custom-call | tf_op jit(solution)/shard_map/pallas_call | solution.py:122
  155.5 1.3 reduce_sum.120
  156.9 1.3 fusion.13
  159.0 4.6 %shard_map.127 = bf16[2,96,896]{2,1,0:T(8,128)(2,1)} custom-call(bf16[96,896]{1,0:T(8,128)(2,1)} %get-tuple-element.56.x_ref), custom_call_target="tpu_custom_call" | custom-call | tf_op jit(solution)/shard_map/pallas_call | solution.py:187
  164.4 18.2 %shard_map.128 = bf16[4,2,96,896]{3,2,1,0:T(8,128)(2,1)} custom-call(bf16[2,96,896]{2,1,0:T(8,128)(2,1)} %fusion.14.x_ref), custom_call_target="tpu_custom_call" | custom-call | tf_op jit(solution)/shard_map/pallas_call | solution.py:187
  183.3 1.5 copy.19
  185.7 1.5 broadcast_in_dim.53
  187.1 3.1 copy.23
  190.2 1.5 broadcast_in_dim.51
  191.7 3.8 %copy.22 = bf16[1024,896]{1,0:T(8,128)(2,1)} copy(bf16[1024,896]{0,1:T(8,128)(2,1)} %bitcast.135) | data formatting | bytes 3670016 | tf_op jit(solution)/shard_map/convert_element_type | solution.py:252
  195.5 5.5 %fusion.4 = f32[768,1024]{1,0:T(8,128)} fusion(bf16[768,896]{1,0:T(8,128)(2,1)S(1)} %bitcast.158, bf16[896,1024]{1,0:T(8,128)(2,1)} %param.11, bf16[112,8,8,128]{3,2,1,0:T(8,128)(2,1)} %bitcast.152), kind=kOutput, calls=%fused_computation.18 | convolution fusion | flops 1410203648 | bytes 8192000 | tf_op jit(solution)/shard_map/dot_general | solution.py:291
  201.0 6.1 %shard_map.129 = f32[1,384,1024]{2,1,0:T(8,128)} custom-call(f32[2,384,1024]{2,1,0:T(8,128)} %bitcast.137), custom_call_target="tpu_custom_call" | custom-call | tf_op jit(solution)/shard_map/pallas_call | solution.py:187
  207.1 2.2 slice_add_fusion.1
  209.2 1.0 fusion.29
  210.3 1.0 copy.40
  211.3 32.1 %shard_map.130 = (f32[3,96,512]{2,1,0:T(8,128)}, f32[3,96,512]{2,1,0:T(8,128)}) custom-call(f32[4,96,512]{2,1,0:T(8,128)} %bitcast.145, f32[4,96,512]{2,1,0:T(8,128)} %bitcast.139), custom_call_target="tpu_custom_call" | custom-call | tf_op jit(solution)/shard_map/pallas_call | solution.py:122
  243.4 1.8 reduce_sum.123
  245.2 1.8 reduce_sum.124
  247.0 1.6 slice.91
  248.7 1.6 slice_add_fusion.3
  250.3 1.7 bitcast_add_fusion.3.refs_1_
  252.0 9.9 %shard_map.131 = (f32[3,24,512]{2,1,0:T(8,128)}, f32[3,24,512]{2,1,0:T(8,128)}) custom-call(f32[4,24,512]{2,1,0:T(8,128)} %bitcast.163, f32[4,24,512]{2,1,0:T(8,128)} %bitcast_add_fusion.3.refs_1_), custom_call_target="tpu_custom_call" | custom-call | tf_op jit(solution)/shard_map/pallas_call | solution.py:122
  261.9 0.9 reduce_sum.127
  262.9 0.9 reduce_sum.126
  266.1 5.2 %multiply_convert_fusion = bf16[896,1024]{1,0:T(8,128)(2,1)} fusion(bf16[768,896]{1,0:T(8,128)(2,1)} %bitcast.159, bf16[768,1024]{1,0:T(8,128)(2,1)} %bitcast.155, bf16[112,8,8,128]{3,2,1,0:T(8,128)(2,1)} %bitcast.153), kind=kOutput, calls=%fused_computation.5 | convolution fusion | flops 1412038656 | bytes 6619136 | tf_op jit(solution)/shard_map/dot_general | solution.py:306
  271.3 7.5 %fusion.2 = f32[768,1024]{1,0:T(8,128)} fusion(bf16[768,1792]{1,0:T(8,128)(2,1)} %all-gather.2.cloned.1.call-done, bf16[1024,896]{0,1:T(8,128)(2,1)} %copy-done.6, bf16[1024,896]{0,1:T(8,128)(2,1)} %copy-done.7), kind=kOutput, calls=%fused_computation.6 | convolution fusion | flops 2825912320 | bytes 9568256 | tf_op jit(solution)/shard_map/dot_general | solution.py:297
  278.8 4.7 %shard_map.132 = f32[1,384,1024]{2,1,0:T(8,128)} custom-call(f32[2,384,1024]{2,1,0:T(8,128)} %bitcast.136), custom_call_target="tpu_custom_call" | custom-call | tf_op jit(solution)/shard_map/pallas_call | solution.py:187
  283.6 2.1 slice_add_fusion
  285.7 1.0 fusion.28
  286.7 0.9 copy.39
  287.7 22.3 %shard_map.133 = (f32[3,96,512]{2,1,0:T(8,128)}, f32[3,96,512]{2,1,0:T(8,128)}) custom-call(f32[4,96,512]{2,1,0:T(8,128)} %bitcast.146, f32[4,96,512]{2,1,0:T(8,128)} %bitcast.142), custom_call_target="tpu_custom_call" | custom-call | tf_op jit(solution)/shard_map/pallas_call | solution.py:122
  310.0 1.8 reduce_sum.129
  311.8 1.6 slice_add_fusion.2
  313.4 1.9 reduce_sum.130
  315.4 1.6 slice.99
  317.0 1.7 bitcast_add_fusion.2.refs_1_
  318.7 7.9 %shard_map.134 = (f32[3,24,512]{2,1,0:T(8,128)}, f32[3,24,512]{2,1,0:T(8,128)}) custom-call(f32[4,24,512]{2,1,0:T(8,128)} %bitcast.161, f32[4,24,512]{2,1,0:T(8,128)} %bitcast_add_fusion.2.refs_1_), custom_call_target="tpu_custom_call" | custom-call | tf_op jit(solution)/shard_map/pallas_call | solution.py:122
  330.8 5.0 %fusion.30 = f32[1024,1792]{1,0:T(8,128)S(1)} fusion(bf16[768,1024]{1,0:T(8,128)(2,1)S(1)} %bitcast.157, bf16[768,1792]{1,0:T(8,128)(2,1)} %all-gather.2.cloned.1.call-done), kind=kOutput, calls=%fused_computation.73 | convolution fusion | flops 2818572288 | bytes 11665408 | tf_op jit(solution)/shard_map/dot_general | solution.py:301
  335.9 2.8 fusion
  (74 shorter events, 12.1 us)
Async XLA Ops:
  7.2 149.7 %reduce-scatter.2.cloned.1.call-start = ((), (), s32[]{:S(2)}) async-start(), calls=%async_computation.1 | async-start | bytes 3096576 | tf_op jit(solution)/shard_map/reduce_scatter | solution.py:283
  34.5 5.4 %copy-start.19 = (s32[7,8]{1,0:T(8,128)S(1)}, s32[7,8]{1,0:T(8,128)}, u32[]{:S(2)}) copy-start(s32[7,8]{1,0:T(8,128)} %param.14) | copy-start | bytes 676
  41.2 1.2 copy-start.9
  41.3 2.4 copy-start.22
  42.4 1.2 copy-start.8
  47.0 11.7 %copy-start.14 = (bf16[24,1024]{1,0:T(8,128)(2,1)S(1)}, bf16[24,1024]{1,0:T(8,128)(2,1)}, u32[]{:S(2)}) copy-start(bf16[24,1024]{1,0:T(8,128)(2,1)} %x_ref.2) | copy-start | bytes 147460
  47.1 224.2 %all-gather.2.cloned.1.call-start = ((), (), s32[]{:S(2)}) async-start(), calls=%async_computation.2 | async-start | bytes 3096576 | tf_op jit(solution)/shard_map/all_gather | solution.py:295
  78.4 2.9 copy-start.20
  81.5 4.0 %copy-start.15 = (bf16[1,7,8,128]{3,1,2,0:T(8,128)(2,1)}, bf16[1,7,8,128]{3,1,2,0:T(8,128)(2,1)S(1)}, u32[]{:S(2)}) copy-start(bf16[1,7,8,128]{3,1,2,0:T(8,128)(2,1)S(1)} %copy.37) | copy-start | bytes 43012
  81.5 3.8 %copy-start.21 = (s32[8,7]{1,0:T(8,128)S(1)}, s32[8,7]{1,0:T(8,128)}, u32[]{:S(2)}) copy-start(s32[8,7]{1,0:T(8,128)} %param.12) | copy-start | bytes 676
  85.5 1.9 copy-start.17
  85.5 1.9 copy-start.4
  87.4 1.2 copy-start.6
  87.4 1.8 copy-start.7
  87.6 4.7 %copy-start.10 = (bf16[2,4,4,24,1024]{4,3,2,1,0:T(8,128)(2,1)}, bf16[2,4,4,24,1024]{4,3,2,1,0:T(8,128)(2,1)S(1)}, u32[]{:S(2)}) copy-start(bf16[2,4,4,24,1024]{4,3,2,1,0:T(8,128)(2,1)S(1)} %pad_maximum_fusion.4) | copy-start | bytes 4718596
  131.7 2.2 copy-start
  136.5 20.4 %copy-start.1 = (f32[1,384,896]{2,1,0:T(8,128)S(1)}, f32[1,384,896]{2,1,0:T(8,128)}, u32[]{:S(2)}) copy-start(f32[1,384,896]{2,1,0:T(8,128)} %dynamic-slice_add_fusion) | copy-start | bytes 4128772
  136.5 20.4 %copy-start.3 = (f32[2,96,896]{2,1,0:T(8,128)S(1)}, f32[2,96,896]{2,1,0:T(8,128)}, u32[]{:S(2)}) copy-start(f32[2,96,896]{2,1,0:T(8,128)} %add.98.refs_0_) | copy-start | bytes 2064388
  156.8 1.3 copy-start.13
  164.4 18.2 %copy-start.5 = (bf16[2,96,896]{2,1,0:T(8,128)(2,1)S(1)}, bf16[2,96,896]{2,1,0:T(8,128)(2,1)}, u32[]{:S(2)}) copy-start(bf16[2,96,896]{2,1,0:T(8,128)(2,1)} %fusion.14.x_ref) | copy-start | bytes 1032196
  183.3 2.3 copy-start.16
  184.8 10.7 %copy-start.12 = (bf16[2,4,96,896]{3,2,1,0:T(8,128)(2,1)}, bf16[2,4,96,896]{3,2,1,0:T(8,128)(2,1)S(1)}, u32[]{:S(2)}) copy-start(bf16[2,4,96,896]{3,2,1,0:T(8,128)(2,1)S(1)} %copy.19) | copy-start | bytes 4128772
  187.1 3.1 copy-start.18
  313.4 17.4 %copy-start.11 = (bf16[2,4,4,24,1024]{4,3,2,1,0:T(8,128)(2,1)S(1)}, bf16[2,4,4,24,1024]{4,3,2,1,0:T(8,128)(2,1)}, u32[]{:S(2)}) copy-start(bf16[2,4,4,24,1024]{4,3,2,1,0:T(8,128)(2,1)} %copy-done.10) | copy-start | bytes 4718596
  330.8 5.1 %copy-start.2 = (bf16[1024,896]{1,0:T(8,128)(2,1)S(1)}, bf16[1024,896]{1,0:T(8,128)(2,1)}, u32[]{:S(2)}) copy-start(bf16[1024,896]{1,0:T(8,128)(2,1)} %copy.22) | copy-start | bytes 5505028
Sparse Core Ops, SparseCore 0:
  47.2 42.6 reduce-scatter.1
  185.8 56.7 all-gather.1

commit v11 on v9

--- a/solution.py
+++ b/solution.py
@@ -225,10 +225,10 @@
     return reorder_blocks(x, [n for n, _ in reversed(digits)])
 
 
-def widen(mask, rows):
-    block = rows // mask.shape[0]
-    full = jnp.repeat(jnp.repeat(mask, block, axis=0), block, axis=1)
-    return full.astype(jnp.bfloat16)
+def apply_mask(w, mask):
+    r, c = mask.shape
+    blocks = w.reshape((r, w.shape[0] // r, c, w.shape[1] // c))
+    return (blocks * mask.astype(w.dtype)[:, None, :, None]).reshape(w.shape)
 
 
 def gating(summed, width):
@@ -248,11 +248,8 @@
 def per_device(tensor_digits, seq_digits, tokens, w_gate, w_up, w_down, mask_gate, mask_up, mask_down, cotangent):
     width = w_gate.shape[1]
     feat = tokens.shape[1]
-    gate_mask = widen(mask_gate, w_gate.shape[0])
-    up_mask = widen(mask_up, w_up.shape[0])
-    down_mask = widen(mask_down, w_down.shape[0])
-    joined = jnp.concatenate([w_gate * gate_mask, w_up * up_mask], axis=1)
-    down_w = w_down * down_mask
+    joined = jnp.concatenate([apply_mask(w_gate, mask_gate), apply_mask(w_up, mask_up)], axis=1)
+    down_w = apply_mask(w_down, mask_down)
     contract_first = (((0,), (0,)), ((), ()))
     contract_last = (((1,), (1,)), ((), ()))
     ids = Ids()
@@ -281,12 +278,12 @@
     weight_grad = lax.dot_general(
         gathered, grads, contract_first, preferred_element_type=jnp.float32
     )
-    grad_gate = (weight_grad[:, :width] * gate_mask).astype(jnp.bfloat16)
-    grad_up = (weight_grad[:, width:] * up_mask).astype(jnp.bfloat16)
+    grad_gate = apply_mask(weight_grad[:, :width], mask_gate).astype(jnp.bfloat16)
+    grad_up = apply_mask(weight_grad[:, width:], mask_up).astype(jnp.bfloat16)
     down_grad = lax.dot_general(
         hidden, cot_rows, contract_first, preferred_element_type=jnp.float32
     )
-    grad_down = (down_grad * down_mask).astype(jnp.bfloat16)
+    grad_down = apply_mask(down_grad, mask_down).astype(jnp.bfloat16)
     return (output, grad_tokens, grad_gate, grad_up, grad_down)
 
 

time: 328 us -> 335 us (1.021)
  local copies, waits for them, and re-layouts: 31.6 us -> 43.9 us
    mul x0 -> x7, local copies, waits for them, and re-layouts: none -> 11.7 us  [apply_mask(): return (blocks * mask.astype(w.dtype)[:, None, :, None]).reshape(w.shape)]
    unnamed x54 -> x53, local copies, waits for them, and re-layouts: 13.1 us -> 20.2 us
    convert_element_type x4 -> x5, local copies, waits for them, and re-layouts: 7.06 us -> 1.55 us  [the longest x1 1.2 us: per_device(): grad_down = apply_mask(down_grad, mask_down).astype(jnp.bfloat16)]
    broadcast_in_dim x4 -> x0, local copies, waits for them, and re-layouts: 4.06 us -> none  [widen(): full = jnp.repeat(jnp.repeat(mask, block, axis=0), block, axis=1)]
  transfers between devices with their start and end apart: 2 -> 2, of which waited for: 0 -> 0; matrix products, arithmetic and copies ran while one was open for 17% -> 19% of each run, Pallas kernels for 37% -> 36%
where the time goes in v11:
time: 335 us; the launch traced here: 334 us
  Pallas kernels  212 us (63%)
  local copies, waits for them, and re-layouts  43.9 us (13%)
  other arithmetic  39.3 us (12%)
  matrix products  24.2 us (7%)
  between operations  14.6 us (4%)
    pallas_call x14, Pallas kernels, exchange(): pl.pallas_call(functools.partial(exchange_kernel, axis, n, stride, gather...  159 us
    pallas_call x2, Pallas kernels, multi_sum(): pl.pallas_call(functools.partial(multi_sum_kernel, axis, tuple(groups)),...  52.9 us
    unnamed x53, local copies, waits for them, and re-layouts  20.2 us
    mul x7, local copies, waits for them, and re-layouts, apply_mask(): return (blocks * mask.astype(w.dtype)[:, None, :, None]).reshape(w.shape)  11.7 us
    add x4, other arithmetic, sum_scatter_rows(): x = x[0] + jnp.sum(exchange(x, axis, n, stride, False, ids.take()), axis=0)  9.23 us
    broadcast_in_dim x4, other arithmetic, gather_rows(): x[None]  7.34 us
  transfers between devices with their start and end apart: 2, of which 0 were waited for; matrix products, arithmetic and copies ran while one was open for 19% of the time, Pallas kernels for 36%

profile of v11, /device:TPU:1, one launch (start us, length us, event | category | flops | bytes accessed | tf_op | source)
XLA Modules:
  0.0 333.8 jit_solution(9539141719428314744)
XLA Ops:
  7.2 12.6 %shard_map.119 = bf16[3,24,1024]{2,1,0:T(8,128)(2,1)} custom-call(bf16[24,1024]{1,0:T(8,128)(2,1)} %x_ref.1), custom_call_target="tpu_custom_call" | custom-call | tf_op jit(solution)/shard_map/pallas_call | solution.py:166
  19.8 1.6 fusion.22
  21.4 13.1 %shard_map.120 = bf16[3,4,24,1024]{3,2,1,0:T(8,128)(2,1)} custom-call(bf16[4,24,1024]{2,1,0:T(8,128)(2,1)} %get-tuple-element.36.x_ref), custom_call_target="tpu_custom_call" | custom-call | tf_op jit(solution)/shard_map/pallas_call | solution.py:166
  34.5 2.1 fusion.24
  36.6 3.4 %shard_map.121 = bf16[1,4,4,24,1024]{4,3,2,1,0:T(8,128)(2,1)} custom-call(bf16[4,4,24,1024]{3,2,1,0:T(8,128)(2,1)} %get-tuple-element.30.x_ref), custom_call_target="tpu_custom_call" | custom-call | tf_op jit(solution)/shard_map/pallas_call | solution.py:166
  40.0 1.4 pad_maximum_fusion.3
  41.7 0.8 copy-done.7
  43.1 3.4 %fusion.5 = f32[768,896]{1,0:T(8,128)} fusion(bf16[768,1024]{1,0:T(8,128)(2,1)S(1)} %bitcast.152, bf16[896,1024]{1,0:T(8,128)(2,1)S(1)} %copy-done.23, bf16[112,8,8,128]{3,2,1,0:T(8,128)(2,1)S(1)} %bitcast.162), kind=kOutput, calls=%fused_computation.20 | convolution fusion | flops 1410203648 | bytes 7995392 | tf_op jit(solution)/shard_map/dot_general | solution.py:257
  46.8 11.4 %shard_map.122 = bf16[3,24,1024]{2,1,0:T(8,128)(2,1)} custom-call(bf16[24,1024]{1,0:T(8,128)(2,1)} %x_ref.2), custom_call_target="tpu_custom_call" | custom-call | tf_op jit(solution)/shard_map/pallas_call | solution.py:166
  58.3 1.6 fusion.21
  59.9 13.1 %shard_map.123 = bf16[3,4,24,1024]{3,2,1,0:T(8,128)(2,1)} custom-call(bf16[4,24,1024]{2,1,0:T(8,128)(2,1)} %get-tuple-element.34.x_ref), custom_call_target="tpu_custom_call" | custom-call | tf_op jit(solution)/shard_map/pallas_call | solution.py:166
  73.0 2.1 fusion.23
  75.0 2.8 shard_map.124
  77.8 2.9 copy.31
  80.9 3.9 %copy.29 = bf16[1024,896]{0,1:T(8,128)(2,1)} copy(bf16[1024,896]{1,0:T(8,128)(2,1)} %param.9) | data formatting | bytes 3670016 | tf_op args[1]
  85.7 1.4 copy-done.4
  87.8 3.1 fusion.3
  90.8 2.0 fusion.25
  92.8 1.7 copy.32
  94.5 34.0 %shard_map.125 = (f32[3,192,896]{2,1,0:T(8,128)}, f32[1,384,896]{2,1,0:T(8,128)}) custom-call(f32[4,192,896]{2,1,0:T(8,128)} %bitcast.134, f32[2,384,896]{2,1,0:T(8,128)} %bitcast.128), custom_call_target="tpu_custom_call" | custom-call | tf_op jit(solution)/shard_map/pallas_call | solution.py:122
  128.5 1.8 reduce_sum.82
  130.3 1.3 constant_dynamic-slice_fusion
  131.6 0.9 add.86.refs_0_
  132.5 2.6 dynamic-slice_add_fusion
  135.1 18.9 %shard_map.126 = (f32[1,96,896]{2,1,0:T(8,128)}, f32[3,96,896]{2,1,0:T(8,128)}) custom-call(f32[2,96,896]{2,1,0:T(8,128)} %add.86.refs_0_, f32[4,96,896]{2,1,0:T(8,128)} %bitcast.137), custom_call_target="tpu_custom_call" | custom-call | tf_op jit(solution)/shard_map/pallas_call | solution.py:122
  154.0 1.3 reduce_sum.84
  155.3 1.3 fusion.15
  156.6 0.8 multiply_convert_fusion.1
  157.4 4.6 %shard_map.127 = bf16[2,96,896]{2,1,0:T(8,128)(2,1)} custom-call(bf16[96,896]{1,0:T(8,128)(2,1)} %get-tuple-element.32.x_ref), custom_call_target="tpu_custom_call" | custom-call | tf_op jit(solution)/shard_map/pallas_call | solution.py:166
  162.0 0.8 fusion.16.x_ref
  162.8 18.3 %shard_map.128 = bf16[4,2,96,896]{3,2,1,0:T(8,128)(2,1)} custom-call(bf16[2,96,896]{2,1,0:T(8,128)(2,1)} %fusion.16.x_ref), custom_call_target="tpu_custom_call" | custom-call | tf_op jit(solution)/shard_map/pallas_call | solution.py:166
  181.1 0.8 bitcast_dynamic-update-slice_fusion
  181.9 1.4 copy.33
  184.5 2.8 copy.56
  187.3 5.0 %copy.37 = f32[1024,896]{1,0:T(8,128)} copy(f32[1024,896]{0,1:T(8,128)} %bitcast.130) | data formatting | bytes 7340032 | tf_op jit(solution)/shard_map/mul | solution.py:231
  192.7 2.7 copy.57
  195.4 5.1 %copy.35 = f32[1024,896]{1,0:T(8,128)} copy(f32[1024,896]{0,1:T(8,128)} %bitcast.131) | data formatting | bytes 7340032 | tf_op jit(solution)/shard_map/mul | solution.py:231
  200.5 1.6 copy.39
  202.1 3.9 %fusion.4 = f32[768,1024]{1,0:T(8,128)S(1)} fusion(bf16[768,896]{1,0:T(8,128)(2,1)S(1)} %bitcast.154, bf16[896,1024]{1,0:T(8,128)(2,1)} %param.11, bf16[112,8,8,128]{3,2,1,0:T(8,128)(2,1)} %bitcast.163), kind=kOutput, calls=%fused_computation.19 | convolution fusion | flops 1410203648 | bytes 8192000 | tf_op jit(solution)/shard_map/dot_general | solution.py:267
  206.0 1.6 copy-done.6
  207.7 6.3 %shard_map.129 = f32[1,384,1024]{2,1,0:T(8,128)} custom-call(f32[2,384,1024]{2,1,0:T(8,128)} %bitcast.151), custom_call_target="tpu_custom_call" | custom-call | tf_op jit(solution)/shard_map/pallas_call | solution.py:166
  214.0 2.8 add.97.x_ref
  216.8 20.6 %shard_map.130 = f32[3,96,1024]{2,1,0:T(8,128)} custom-call(f32[4,96,1024]{2,1,0:T(8,128)} %add.97.x_ref), custom_call_target="tpu_custom_call" | custom-call | tf_op jit(solution)/shard_map/pallas_call | solution.py:166
  237.4 1.4 reduce_sum.88
  238.8 1.8 fusion.7
  240.6 12.4 %shard_map.131 = f32[3,24,1024]{2,1,0:T(8,128)} custom-call(f32[4,24,1024]{2,1,0:T(8,128)} %bitcast.159), custom_call_target="tpu_custom_call" | custom-call | tf_op jit(solution)/shard_map/pallas_call | solution.py:166
  253.0 1.0 reduce_sum.89
  254.0 1.5 copy.38
  255.6 3.0 multiply_convert_fusion
  258.5 1.2 copy.40
  259.8 1.8 copy.58
  261.5 1.5 fusion.18
  263.1 5.3 %fusion.2 = f32[768,1024]{1,0:T(8,128)S(1)} fusion(bf16[768,1792]{1,0:T(8,128)(2,1)} %all-gather.2.cloned.1.call-done, bf16[1024,896]{0,1:T(8,128)(2,1)S(1)} %copy-done.14, bf16[1024,896]{0,1:T(8,128)(2,1)} %copy-done.15), kind=kOutput, calls=%fused_computation.8 | convolution fusion | flops 2825912320 | bytes 9568256 | tf_op jit(solution)/shard_map/dot_general | solution.py:273
  268.4 1.6 copy-done.5
  270.1 6.9 %shard_map.132 = f32[1,384,1024]{2,1,0:T(8,128)} custom-call(f32[2,384,1024]{2,1,0:T(8,128)} %bitcast.150), custom_call_target="tpu_custom_call" | custom-call | tf_op jit(solution)/shard_map/pallas_call | solution.py:166
  277.1 2.8 add.103.x_ref
  279.9 20.6 %shard_map.133 = f32[3,96,1024]{2,1,0:T(8,128)} custom-call(f32[4,96,1024]{2,1,0:T(8,128)} %add.103.x_ref), custom_call_target="tpu_custom_call" | custom-call | tf_op jit(solution)/shard_map/pallas_call | solution.py:166
  300.6 1.4 reduce_sum.92
  301.9 1.8 fusion.6
  303.7 12.5 %shard_map.134 = f32[3,24,1024]{2,1,0:T(8,128)} custom-call(f32[4,24,1024]{2,1,0:T(8,128)} %bitcast.160), custom_call_target="tpu_custom_call" | custom-call | tf_op jit(solution)/shard_map/pallas_call | solution.py:166
  316.3 1.0 reduce_sum.93
  317.3 1.5 fusion.17
  318.8 5.6 %fusion.29 = f32[1024,1792]{1,0:T(8,128)S(1)} fusion(bf16[768,1024]{1,0:T(8,128)(2,1)} %bitcast.165, bf16[768,1792]{1,0:T(8,128)(2,1)} %all-gather.2.cloned.1.call-done), kind=kOutput, calls=%fused_computation.61 | convolution fusion | flops 2818572288 | bytes 11665408 | tf_op jit(solution)/shard_map/dot_general | solution.py:278
  324.4 2.6 fusion
  (67 shorter events, 4.6 us)
Async XLA Ops:
  7.2 148.1 %reduce-scatter.2.cloned.1.call-start = ((), (), s32[]{:S(2)}) async-start(), calls=%async_computation.1 | async-start | bytes 3096576 | tf_op jit(solution)/shard_map/reduce_scatter | solution.py:259
  34.5 5.4 %copy-start.20 = (s32[7,8]{1,0:T(8,128)S(1)}, s32[7,8]{1,0:T(8,128)}, u32[]{:S(2)}) copy-start(s32[7,8]{1,0:T(8,128)} %param.14) | copy-start | bytes 676
  40.0 3.2 copy-start.23
  41.4 1.1 copy-start.7
  41.7 1.4 copy-start.12
  46.5 11.7 %copy-start.19 = (bf16[24,1024]{1,0:T(8,128)(2,1)S(1)}, bf16[24,1024]{1,0:T(8,128)(2,1)}, u32[]{:S(2)}) copy-start(bf16[24,1024]{1,0:T(8,128)(2,1)} %x_ref.2) | copy-start | bytes 147460
  46.5 216.5 %all-gather.2.cloned.1.call-start = ((), (), s32[]{:S(2)}) async-start(), calls=%async_computation.2 | async-start | bytes 3096576 | tf_op jit(solution)/shard_map/all_gather | solution.py:271
  77.8 2.9 copy-start.21
  80.9 3.9 %copy-start.22 = (s32[8,7]{1,0:T(8,128)S(1)}, s32[8,7]{1,0:T(8,128)}, u32[]{:S(2)}) copy-start(s32[8,7]{1,0:T(8,128)} %param.12) | copy-start | bytes 676
  80.9 4.0 %copy-start.10 = (bf16[1,4,4,24,1024]{4,3,2,1,0:T(8,128)(2,1)S(1)}, bf16[1,4,4,24,1024]{4,3,2,1,0:T(8,128)(2,1)}, u32[]{:S(2)}) copy-start(bf16[1,4,4,24,1024]{4,3,2,1,0:T(8,128)(2,1)} %shard_map.124) | copy-start | bytes 2359300
  85.0 2.7 copy-start.16
  85.0 2.1 copy-start.4
  87.7 3.1 copy-start.13
  87.7 3.1 copy-start.15
  130.3 2.2 copy-start
  135.1 20.2 %copy-start.3 = (f32[1,384,896]{2,1,0:T(8,128)S(1)}, f32[1,384,896]{2,1,0:T(8,128)}, u32[]{:S(2)}) copy-start(f32[1,384,896]{2,1,0:T(8,128)} %dynamic-slice_add_fusion) | copy-start | bytes 4128772
  135.1 20.3 %copy-start.9 = (f32[2,96,896]{2,1,0:T(8,128)S(1)}, f32[2,96,896]{2,1,0:T(8,128)}, u32[]{:S(2)}) copy-start(f32[2,96,896]{2,1,0:T(8,128)} %add.86.refs_0_) | copy-start | bytes 2064388
  155.3 1.3 copy-start.18
  162.8 18.3 %copy-start.11 = (bf16[2,96,896]{2,1,0:T(8,128)(2,1)S(1)}, bf16[2,96,896]{2,1,0:T(8,128)(2,1)}, u32[]{:S(2)}) copy-start(bf16[2,96,896]{2,1,0:T(8,128)(2,1)} %fusion.16.x_ref) | copy-start | bytes 1032196
  195.4 5.1 %copy-start.8 = (bf16[2,4,4,24,1024]{4,3,2,1,0:T(8,128)(2,1)S(1)}, bf16[2,4,4,24,1024]{4,3,2,1,0:T(8,128)(2,1)}, u32[]{:S(2)}) copy-start(bf16[2,4,4,24,1024]{4,3,2,1,0:T(8,128)(2,1)} %copy-done.7) | copy-start | bytes 4718596
  205.9 1.6 copy-start.6
  240.6 15.0 %copy-start.17 = (bf16[1024,768]{1,0:T(8,128)(2,1)S(1)}, bf16[1024,768]{1,0:T(8,128)(2,1)}, u32[]{:S(2)}) copy-start(bf16[1024,768]{1,0:T(8,128)(2,1)} %copy.39) | copy-start | bytes 4718596
  259.7 3.3 copy-start.14
  268.4 1.7 copy-start.5
  318.8 5.6 %copy-start.1 = (f32[1024,896]{1,0:T(8,128)S(1)}, f32[1024,896]{1,0:T(8,128)}, u32[]{:S(2)}) copy-start(f32[1024,896]{1,0:T(8,128)} %copy.37) | copy-start | bytes 11010052
  318.8 5.6 %copy-start.2 = (f32[1024,896]{1,0:T(8,128)S(1)}, f32[1024,896]{1,0:T(8,128)}, u32[]{:S(2)}) copy-start(f32[1024,896]{1,0:T(8,128)} %copy.35) | copy-start | bytes 11010052
Sparse Core Ops, SparseCore 0:
  46.7 42.7 reduce-scatter.1
  184.2 40.3 all-gather.1

commit v12 on v9

--- a/solution.py
+++ b/solution.py
@@ -65,7 +65,7 @@
     lax.fori_loop(1, n, finish, 0)
 
 
-def multi_sum_kernel(axis, groups, *refs):
+def multi_sum_kernel(axis, groups, gather, *refs):
     m = len(groups)
     x_refs, y_refs, sems = refs[:m], refs[m:2 * m], refs[2 * m:]
     index = lax.axis_index(axis)
@@ -89,11 +89,15 @@
     def remote(g, k, direction):
         n, stride, me, base = infos[g]
         other = lax.rem(me + direction * k + n, n)
+        if gather:
+            slot = me if direction == 1 else other
+        else:
+            slot = k - 1
         return pltpu.make_async_remote_copy(
-            src_ref=x_refs[g].at[other],
-            dst_ref=y_refs[g].at[k - 1],
+            src_ref=x_refs[g] if gather else x_refs[g].at[other],
+            dst_ref=y_refs[g].at[slot],
             send_sem=sems[2 * g].at[k - 1],
-            recv_sem=sems[2 * g + 1].at[k - 1],
+            recv_sem=sems[2 * g + 1].at[slot],
             device_id=peer(axis, base + other * stride),
             device_id_type=MESH,
         )
@@ -115,25 +119,48 @@
         lax.fori_loop(1, groups[g][0], finish, 0)
 
 
-def multi_sum(xs, axis, groups, cid):
+def multi_call(xs, axis, groups, cid, gather):
     sems = []
     for n, _ in groups:
-        sems += [pltpu.SemaphoreType.DMA((n - 1,)), pltpu.SemaphoreType.DMA((n - 1,))]
-    ys = pl.pallas_call(
-        functools.partial(multi_sum_kernel, axis, tuple(groups)),
-        out_shape=[
-            jax.ShapeDtypeStruct((n - 1,) + x.shape[1:], x.dtype) for x, (n, _) in zip(xs, groups)
-        ],
+        sems += [pltpu.SemaphoreType.DMA((n - 1,)), pltpu.SemaphoreType.DMA((n if gather else n - 1,))]
+    shapes = [(n,) + x.shape if gather else (n - 1,) + x.shape[1:] for x, (n, _) in zip(xs, groups)]
+    return pl.pallas_call(
+        functools.partial(multi_sum_kernel, axis, tuple(groups), gather),
+        out_shape=[jax.ShapeDtypeStruct(shape, x.dtype) for x, shape in zip(xs, shapes)],
         in_specs=[pl.BlockSpec(memory_space=pl.ANY)] * len(xs),
         out_specs=[pl.BlockSpec(memory_space=pl.ANY)] * len(xs),
         scratch_shapes=sems,
         compiler_params=pltpu.CompilerParams(collective_id=cid, has_side_effects=True),
     )(*xs)
+
+
+def multi_gather(xs, axis, groups, cid):
+    ys = multi_call(xs, axis, groups, cid, True)
+    return [
+        lax.dynamic_update_index_in_dim(y, x, digit(axis, n, stride), 0)
+        for x, y, (n, stride) in zip(xs, ys, groups)
+    ]
+
+
+def multi_sum(xs, axis, groups, cid):
+    ys = multi_call(xs, axis, groups, cid, False)
     out = []
     for x, y, (n, stride) in zip(xs, ys, groups):
         own = lax.dynamic_index_in_dim(x, digit(axis, n, stride), 0, keepdims=False)
         out.append(own + jnp.sum(y, axis=0))
     return out
+
+
+def seq_gather_2d(x, digits, ids):
+    if len(digits) != 2:
+        return seq_gather(x, digits, ids)
+    (ns, ss), (nf, sf) = digits
+    half = x.shape[1] // 2
+    a, b = multi_gather([x[:, :half], x[:, half:]], "seq", [(ns, ss), (nf, sf)], ids.take())
+    a, b = multi_gather([a, b], "seq", [(nf, sf), (ns, ss)], ids.take())
+    a = jnp.swapaxes(a, 0, 1).reshape((-1, half))
+    b = b.reshape((-1, b.shape[-1]))
+    return jnp.concatenate([a, b], axis=1)
 
 
 def seq_sum_scatter_2d(x, digits, ids):
@@ -265,7 +292,7 @@
     summed = seq_sum_scatter_2d(partial_value, seq_digits, ids)
     gate, up, sig, act = gating(summed, width)
     hidden_part = (act * up).astype(jnp.bfloat16)
-    hidden = seq_gather(hidden_part, seq_digits, ids)
+    hidden = seq_gather_2d(hidden_part, seq_digits, ids)
     output = sum_scatter_rows(
         jnp.dot(hidden, down_w, preferred_element_type=jnp.float32), "tensor", tensor_digits, ids
     ).astype(jnp.bfloat16)

time: 328 us -> 327 us (level)
  local copies, waits for them, and re-layouts: 31.6 us -> 35.5 us
    pallas_call x14 -> x12, Pallas kernels: 159 us -> 135 us  [exchange(): pl.pallas_call(functools.partial(exchange_kernel, axis, n, stride, gather...]
    pallas_call x2 -> x4, Pallas kernels: 53 us -> 72.5 us  [multi_call(): pl.pallas_call(functools.partial(multi_sum_kernel, axis, tuple(groups), g...]
    dynamic_update_slice x1 -> x3, local copies, waits for them, and re-layouts: 0.77 us -> 4.2 us  [multi_gather(): lax.dynamic_update_index_in_dim(y, x, digit(axis, n, stride), 0)]
    unnamed x54 -> x42, local copies, waits for them, and re-layouts: 13.1 us -> 13.1 us
  transfers between devices with their start and end apart: 2 -> 2, of which waited for: 0 -> 0; matrix products, arithmetic and copies ran while one was open for 17% -> 17% of each run, Pallas kernels for 37% -> 36%
where the time goes in v12:
time: 327 us; the launch traced here: 326 us
  Pallas kernels  208 us (64%)
  other arithmetic  41.4 us (13%)
  local copies, waits for them, and re-layouts  35.5 us (11%)
  matrix products  26.6 us (8%)
  between operations  14.5 us (4%)
    pallas_call x12, Pallas kernels, exchange(): pl.pallas_call(functools.partial(exchange_kernel, axis, n, stride, gather...  135 us
    pallas_call x4, Pallas kernels, multi_call(): pl.pallas_call(functools.partial(multi_sum_kernel, axis, tuple(groups), g...  72.5 us
    unnamed x42, local copies, waits for them, and re-layouts  13.1 us
    add x4, other arithmetic, sum_scatter_rows(): x = x[0] + jnp.sum(exchange(x, axis, n, stride, False, ids.take()), axis=0)  9.46 us
    broadcast_in_dim x4, other arithmetic, gather_rows(): x[None]  7.34 us
    convert_element_type x4, local copies, waits for them, and re-layouts, widen(): return full.astype(jnp.bfloat16)  7.04 us
  transfers between devices with their start and end apart: 2, of which 0 were waited for; matrix products, arithmetic and copies ran while one was open for 17% of the time, Pallas kernels for 36%

profile of v12, /device:TPU:1, one launch (start us, length us, event | category | flops | bytes accessed | tf_op | source)
XLA Modules:
  0.0 326.1 jit_solution(12292328540764885338)
XLA Ops:
  7.2 12.6 %shard_map.119 = bf16[3,24,1024]{2,1,0:T(8,128)(2,1)} custom-call(bf16[24,1024]{1,0:T(8,128)(2,1)} %x_ref.1), custom_call_target="tpu_custom_call" | custom-call | tf_op jit(solution)/shard_map/pallas_call | solution.py:193
  19.8 1.6 fusion.19
  21.4 13.1 %shard_map.120 = bf16[3,4,24,1024]{3,2,1,0:T(8,128)(2,1)} custom-call(bf16[4,24,1024]{2,1,0:T(8,128)(2,1)} %get-tuple-element.43.x_ref), custom_call_target="tpu_custom_call" | custom-call | tf_op jit(solution)/shard_map/pallas_call | solution.py:193
  34.5 2.1 fusion.21
  36.6 3.4 %shard_map.121 = bf16[1,4,4,24,1024]{4,3,2,1,0:T(8,128)(2,1)} custom-call(bf16[4,4,24,1024]{3,2,1,0:T(8,128)(2,1)} %get-tuple-element.39.x_ref), custom_call_target="tpu_custom_call" | custom-call | tf_op jit(solution)/shard_map/pallas_call | solution.py:193
  40.0 1.3 pad_maximum_fusion.3
  41.3 1.1 broadcast_in_dim.56
  42.5 1.2 copy-done.8
  43.7 3.4 %fusion.5 = f32[768,896]{1,0:T(8,128)} fusion(bf16[768,1024]{1,0:T(8,128)(2,1)S(1)} %bitcast.129, bf16[896,1024]{1,0:T(8,128)(2,1)S(1)} %copy-done.17, bf16[112,8,8,128]{3,2,1,0:T(8,128)(2,1)S(1)} %bitcast.126), kind=kOutput, calls=%fused_computation.18 | convolution fusion | flops 1410203648 | bytes 7995392 | tf_op jit(solution)/shard_map/dot_general | solution.py:287
  47.3 11.4 %shard_map.122 = bf16[3,24,1024]{2,1,0:T(8,128)(2,1)} custom-call(bf16[24,1024]{1,0:T(8,128)(2,1)} %x_ref.2), custom_call_target="tpu_custom_call" | custom-call | tf_op jit(solution)/shard_map/pallas_call | solution.py:193
  58.8 1.6 fusion.18
  60.4 13.1 %shard_map.123 = bf16[3,4,24,1024]{3,2,1,0:T(8,128)(2,1)} custom-call(bf16[4,24,1024]{2,1,0:T(8,128)(2,1)} %get-tuple-element.41.x_ref), custom_call_target="tpu_custom_call" | custom-call | tf_op jit(solution)/shard_map/pallas_call | solution.py:193
  73.5 2.1 fusion.20
  75.6 2.8 shard_map.124
  78.4 2.9 copy.17
  81.5 3.8 %copy.15 = bf16[1024,896]{0,1:T(8,128)(2,1)} copy(bf16[1024,896]{1,0:T(8,128)(2,1)} %param.9) | data formatting | bytes 3670016 | tf_op args[1]
  85.5 1.8 bitcast_multiply_fusion.1
  87.6 1.0 copy-done.6
  89.2 3.1 fusion.3
  92.3 1.9 fusion.22
  94.2 1.7 copy.18
  95.9 34.0 %shard_map.125 = (f32[3,192,896]{2,1,0:T(8,128)}, f32[1,384,896]{2,1,0:T(8,128)}) custom-call(f32[4,192,896]{2,1,0:T(8,128)} %bitcast.106, f32[2,384,896]{2,1,0:T(8,128)} %bitcast.104), custom_call_target="tpu_custom_call" | custom-call | tf_op jit(solution)/shard_map/pallas_call | solution.py:127
  129.9 1.8 reduce_sum.80
  131.7 1.3 constant_dynamic-slice_fusion
  133.0 0.9 add.83.refs_0_
  133.9 2.6 dynamic-slice_add_fusion
  136.5 19.0 %shard_map.126 = (f32[1,96,896]{2,1,0:T(8,128)}, f32[3,96,896]{2,1,0:T(8,128)}) custom-call(f32[2,96,896]{2,1,0:T(8,128)} %add.83.refs_0_, f32[4,96,896]{2,1,0:T(8,128)} %bitcast.119), custom_call_target="tpu_custom_call" | custom-call | tf_op jit(solution)/shard_map/pallas_call | solution.py:127
  155.4 1.3 reduce_sum.82
  156.8 1.4 fusion.13
  158.2 0.7 fusion.23
  159.0 7.3 %shard_map.127 = (bf16[2,96,448]{2,1,0:T(8,128)(2,1)}, bf16[4,96,448]{2,1,0:T(8,128)(2,1)}) custom-call(bf16[96,448]{1,0:T(8,128)(2,1)} %get-tuple-element.47.refs_0_, bf16[96,448]{1,0:T(8,128)(2,1)} %get-tuple-element.46.refs_1_), custom_call_target="tpu_custom_call" | custom-call | tf_op jit(solution)/shard_map/pallas_call | solution.py:127
  166.3 0.7 bitcast_dynamic-update-slice_fusion.2
  167.0 12.3 %shard_map.128 = (bf16[4,2,96,448]{3,2,1,0:T(8,128)(2,1)}, bf16[2,4,96,448]{3,2,1,0:T(8,128)(2,1)}) custom-call(bf16[2,96,448]{2,1,0:T(8,128)(2,1)} %get-tuple-element.45.refs_0_, bf16[4,96,448]{2,1,0:T(8,128)(2,1)} %get-tuple-element.44.refs_1_), custom_call_target="tpu_custom_call" | custom-call | tf_op jit(solution)/shard_map/pallas_call | solution.py:127
  179.3 1.8 bitcast_dynamic-update-slice_fusion
  181.1 1.7 bitcast_dynamic-update-slice_fusion.1
  182.8 1.2 copy.19
  184.5 0.8 pad_maximum_fusion.8
  185.3 1.5 broadcast_in_dim.63
  186.8 3.1 copy.21
  189.8 1.5 broadcast_in_dim.61
  191.3 3.8 %copy.20 = bf16[1024,896]{1,0:T(8,128)(2,1)} copy(bf16[1024,896]{0,1:T(8,128)(2,1)} %bitcast.116) | data formatting | bytes 3670016 | tf_op jit(solution)/shard_map/convert_element_type | solution.py:258
  195.1 3.9 %fusion.4 = f32[768,1024]{1,0:T(8,128)S(1)} fusion(bf16[768,896]{1,0:T(8,128)(2,1)S(1)} %pad_maximum_fusion.5, bf16[896,1024]{1,0:T(8,128)(2,1)} %param.11, bf16[112,8,8,128]{3,2,1,0:T(8,128)(2,1)} %bitcast.127), kind=kOutput, calls=%fused_computation.17 | convolution fusion | flops 1410203648 | bytes 8192000 | tf_op jit(solution)/shard_map/dot_general | solution.py:297
  199.0 1.6 copy-done.3
  200.7 5.7 %shard_map.129 = f32[1,384,1024]{2,1,0:T(8,128)} custom-call(f32[2,384,1024]{2,1,0:T(8,128)} %bitcast.118), custom_call_target="tpu_custom_call" | custom-call | tf_op jit(solution)/shard_map/pallas_call | solution.py:193
  206.4 2.8 add.92.x_ref
  209.2 20.6 %shard_map.130 = f32[3,96,1024]{2,1,0:T(8,128)} custom-call(f32[4,96,1024]{2,1,0:T(8,128)} %add.92.x_ref), custom_call_target="tpu_custom_call" | custom-call | tf_op jit(solution)/shard_map/pallas_call | solution.py:193
  229.8 2.1 reduce_sum.85
  232.0 1.9 fusion.7
  233.9 12.3 %shard_map.131 = f32[3,24,1024]{2,1,0:T(8,128)} custom-call(f32[4,24,1024]{2,1,0:T(8,128)} %bitcast.125), custom_call_target="tpu_custom_call" | custom-call | tf_op jit(solution)/shard_map/pallas_call | solution.py:193
  246.1 1.0 reduce_sum.86
  247.1 1.5 fusion.15
  248.7 5.2 %multiply_convert_fusion = bf16[896,1024]{1,0:T(8,128)(2,1)} fusion(bf16[768,896]{1,0:T(8,128)(2,1)} %copy-done.11, bf16[768,1024]{1,0:T(8,128)(2,1)} %bitcast.130, bf16[112,8,8,128]{3,2,1,0:T(8,128)(2,1)} %bitcast.128), kind=kOutput, calls=%fused_computation.5 | convolution fusion | flops 1412038656 | bytes 6619136 | tf_op jit(solution)/shard_map/dot_general | solution.py:313
  253.9 5.5 %fusion.2 = f32[768,1024]{1,0:T(8,128)S(1)} fusion(bf16[768,1792]{1,0:T(8,128)(2,1)} %all-gather.2.cloned.1.call-done, bf16[1024,896]{0,1:T(8,128)(2,1)} %copy-done.6, bf16[1024,896]{0,1:T(8,128)(2,1)} %copy-done.7), kind=kOutput, calls=%fused_computation.6 | convolution fusion | flops 2825912320 | bytes 9568256 | tf_op jit(solution)/shard_map/dot_general | solution.py:303
  259.5 1.6 copy-done.2
  261.2 7.1 %shard_map.132 = f32[1,384,1024]{2,1,0:T(8,128)} custom-call(f32[2,384,1024]{2,1,0:T(8,128)} %bitcast.117), custom_call_target="tpu_custom_call" | custom-call | tf_op jit(solution)/shard_map/pallas_call | solution.py:193
  268.3 2.8 add.98.x_ref
  271.1 20.8 %shard_map.133 = f32[3,96,1024]{2,1,0:T(8,128)} custom-call(f32[4,96,1024]{2,1,0:T(8,128)} %add.98.x_ref), custom_call_target="tpu_custom_call" | custom-call | tf_op jit(solution)/shard_map/pallas_call | solution.py:193
  292.0 2.1 reduce_sum.89
  294.1 1.9 fusion.6
  296.0 12.4 %shard_map.134 = f32[3,24,1024]{2,1,0:T(8,128)} custom-call(f32[4,24,1024]{2,1,0:T(8,128)} %bitcast.124), custom_call_target="tpu_custom_call" | custom-call | tf_op jit(solution)/shard_map/pallas_call | solution.py:193
  308.4 1.0 reduce_sum.90
  309.4 1.5 fusion.14
  310.9 5.6 %fusion.24 = f32[1024,1792]{1,0:T(8,128)S(1)} fusion(bf16[768,1024]{1,0:T(8,128)(2,1)} %bitcast.132, bf16[768,1792]{1,0:T(8,128)(2,1)} %all-gather.2.cloned.1.call-done), kind=kOutput, calls=%fused_computation.60 | convolution fusion | flops 2818572288 | bytes 11665408 | tf_op jit(solution)/shard_map/dot_general | solution.py:308
  316.5 2.8 fusion
  (52 shorter events, 2.2 us)
Async XLA Ops:
  7.2 149.6 %reduce-scatter.2.cloned.1.call-start = ((), (), s32[]{:S(2)}) async-start(), calls=%async_computation.1 | async-start | bytes 3096576 | tf_op jit(solution)/shard_map/reduce_scatter | solution.py:289
  34.5 5.4 %copy-start.14 = (s32[7,8]{1,0:T(8,128)S(1)}, s32[7,8]{1,0:T(8,128)}, u32[]{:S(2)}) copy-start(s32[7,8]{1,0:T(8,128)} %param.14) | copy-start | bytes 676
  41.2 1.2 copy-start.9
  41.3 2.4 copy-start.17
  42.4 1.2 copy-start.8
  47.0 11.7 %copy-start.13 = (bf16[24,1024]{1,0:T(8,128)(2,1)S(1)}, bf16[24,1024]{1,0:T(8,128)(2,1)}, u32[]{:S(2)}) copy-start(bf16[24,1024]{1,0:T(8,128)(2,1)} %x_ref.2) | copy-start | bytes 147460
  47.1 206.8 %all-gather.2.cloned.1.call-start = ((), (), s32[]{:S(2)}) async-start(), calls=%async_computation.2 | async-start | bytes 3096576 | tf_op jit(solution)/shard_map/all_gather | solution.py:301
  78.4 2.9 copy-start.15
  81.5 3.8 %copy-start.16 = (s32[8,7]{1,0:T(8,128)S(1)}, s32[8,7]{1,0:T(8,128)}, u32[]{:S(2)}) copy-start(s32[8,7]{1,0:T(8,128)} %param.12) | copy-start | bytes 676
  85.5 1.9 copy-start.5
  87.4 1.2 copy-start.6
  87.4 1.8 copy-start.7
  87.6 4.7 %copy-start.10 = (bf16[2,4,4,24,1024]{4,3,2,1,0:T(8,128)(2,1)}, bf16[2,4,4,24,1024]{4,3,2,1,0:T(8,128)(2,1)S(1)}, u32[]{:S(2)}) copy-start(bf16[2,4,4,24,1024]{4,3,2,1,0:T(8,128)(2,1)S(1)} %pad_maximum_fusion.4) | copy-start | bytes 4718596
  131.7 2.2 copy-start
  136.5 20.3 %copy-start.4 = (f32[2,96,896]{2,1,0:T(8,128)S(1)}, f32[2,96,896]{2,1,0:T(8,128)}, u32[]{:S(2)}) copy-start(f32[2,96,896]{2,1,0:T(8,128)} %add.83.refs_0_) | copy-start | bytes 2064388
  181.1 2.9 copy-start.12
  184.5 10.6 %copy-start.11 = (bf16[768,896]{1,0:T(8,128)(2,1)}, bf16[768,896]{1,0:T(8,128)(2,1)S(1)}, u32[]{:S(2)}) copy-start(bf16[768,896]{1,0:T(8,128)(2,1)S(1)} %pad_maximum_fusion.5) | copy-start | bytes 4128772
  199.0 1.7 copy-start.3
  259.5 1.7 copy-start.2
  310.9 5.6 %copy-start.1 = (bf16[1024,896]{1,0:T(8,128)(2,1)S(1)}, bf16[1024,896]{1,0:T(8,128)(2,1)}, u32[]{:S(2)}) copy-start(bf16[1024,896]{1,0:T(8,128)(2,1)} %copy.20) | copy-start | bytes 5505028
Sparse Core Ops, SparseCore 0:
  47.2 42.6 reduce-scatter.1
  185.4 39.8 all-gather.1

commit v13 on v12

--- a/solution.py
+++ b/solution.py
@@ -152,15 +152,16 @@
 
 
 def seq_gather_2d(x, digits, ids):
+    half = x.shape[1] // 2
     if len(digits) != 2:
-        return seq_gather(x, digits, ids)
+        x = seq_gather(x, digits, ids)
+        return [x[:, :half], x[:, half:]]
     (ns, ss), (nf, sf) = digits
-    half = x.shape[1] // 2
     a, b = multi_gather([x[:, :half], x[:, half:]], "seq", [(ns, ss), (nf, sf)], ids.take())
     a, b = multi_gather([a, b], "seq", [(nf, sf), (ns, ss)], ids.take())
     a = jnp.swapaxes(a, 0, 1).reshape((-1, half))
     b = b.reshape((-1, b.shape[-1]))
-    return jnp.concatenate([a, b], axis=1)
+    return [a, b]
 
 
 def seq_sum_scatter_2d(x, digits, ids):
@@ -293,9 +294,11 @@
     gate, up, sig, act = gating(summed, width)
     hidden_part = (act * up).astype(jnp.bfloat16)
     hidden = seq_gather_2d(hidden_part, seq_digits, ids)
-    output = sum_scatter_rows(
-        jnp.dot(hidden, down_w, preferred_element_type=jnp.float32), "tensor", tensor_digits, ids
-    ).astype(jnp.bfloat16)
+    cut = hidden[0].shape[1]
+    output_part = jnp.dot(hidden[0], down_w[:cut], preferred_element_type=jnp.float32) + jnp.dot(
+        hidden[1], down_w[cut:], preferred_element_type=jnp.float32
+    )
+    output = sum_scatter_rows(output_part, "tensor", tensor_digits, ids).astype(jnp.bfloat16)
     grads_part = gate_up_grads(gate, up, sig, act, grad_hidden)
     grads_part, hidden = lax.optimization_barrier((grads_part, hidden))
     grads = lax.all_gather(grads_part, "seq", axis=0, tiled=True)
@@ -310,8 +313,11 @@
     )
     grad_gate = (weight_grad[:, :width] * gate_mask).astype(jnp.bfloat16)
     grad_up = (weight_grad[:, width:] * up_mask).astype(jnp.bfloat16)
-    down_grad = lax.dot_general(
-        hidden, cot_rows, contract_first, preferred_element_type=jnp.float32
+    down_grad = jnp.concatenate(
+        [
+            lax.dot_general(piece, cot_rows, contract_first, preferred_element_type=jnp.float32)
+            for piece in hidden
+        ]
     )
     grad_down = (down_grad * down_mask).astype(jnp.bfloat16)
     return (output, grad_tokens, grad_gate, grad_up, grad_down)

time: 327 us -> 320 us (0.979)
  matrix products: 26.6 us -> 21.9 us
  local copies, waits for them, and re-layouts: 35.5 us -> 31.9 us
    dot_general x2 -> x4, matrix products: 9.1 us -> 5.07 us  [the longest x1 2.31 us: per_device(): jnp.dot(hidden[0], down_w[:cut], preferred_element_type=jnp.float32)]
    unnamed x42 -> x66, local copies, waits for them, and re-layouts: 13.1 us -> 14.4 us
  transfers between devices with their start and end apart: 2 -> 2, of which waited for: 0 -> 0; matrix products, arithmetic and copies ran while one was open for 17% -> 16% of each run, Pallas kernels for 36% -> 37%
where the time goes in v13:
time: 320 us; the launch traced here: 319 us
  Pallas kernels  208 us (65%)
  other arithmetic  42.6 us (13%)
  local copies, waits for them, and re-layouts  31.9 us (10%)
  matrix products  21.9 us (7%)
  between operations  14.6 us (5%)
    pallas_call x12, Pallas kernels, exchange(): pl.pallas_call(functools.partial(exchange_kernel, axis, n, stride, gather...  135 us
    pallas_call x4, Pallas kernels, multi_call(): pl.pallas_call(functools.partial(multi_sum_kernel, axis, tuple(groups), g...  72.5 us
    unnamed x66, local copies, waits for them, and re-layouts  14.4 us
    add x4, other arithmetic, sum_scatter_rows(): x = x[0] + jnp.sum(exchange(x, axis, n, stride, False, ids.take()), axis=0)  10.2 us
    broadcast_in_dim x4, other arithmetic, gather_rows(): x[None]  7.34 us
  transfers between devices with their start and end apart: 2, of which 0 were waited for; matrix products, arithmetic and copies ran while one was open for 16% of the time, Pallas kernels for 37%

profile of v13, /device:TPU:1, one launch (start us, length us, event | category | flops | bytes accessed | tf_op | source)
XLA Modules:
  0.0 319.0 jit_solution(1680712354849751234)
XLA Ops:
  7.2 12.6 %shard_map.119 = bf16[3,24,1024]{2,1,0:T(8,128)(2,1)} custom-call(bf16[24,1024]{1,0:T(8,128)(2,1)} %x_ref.1), custom_call_target="tpu_custom_call" | custom-call | tf_op jit(solution)/shard_map/pallas_call | solution.py:194
  19.8 1.6 fusion.21
  21.4 13.1 %shard_map.120 = bf16[3,4,24,1024]{3,2,1,0:T(8,128)(2,1)} custom-call(bf16[4,24,1024]{2,1,0:T(8,128)(2,1)} %get-tuple-element.45.x_ref), custom_call_target="tpu_custom_call" | custom-call | tf_op jit(solution)/shard_map/pallas_call | solution.py:194
  34.5 2.1 fusion.23
  36.6 3.4 %shard_map.121 = bf16[1,4,4,24,1024]{4,3,2,1,0:T(8,128)(2,1)} custom-call(bf16[4,4,24,1024]{3,2,1,0:T(8,128)(2,1)} %get-tuple-element.41.x_ref), custom_call_target="tpu_custom_call" | custom-call | tf_op jit(solution)/shard_map/pallas_call | solution.py:194
  40.0 1.3 pad_maximum_fusion.3
  41.3 1.1 broadcast_in_dim.56
  42.4 0.9 copy-done.16
  43.7 1.2 copy-done.6
  44.9 3.4 %fusion.26 = f32[768,896]{1,0:T(8,128)} fusion(bf16[768,1024]{1,0:T(8,128)(2,1)S(1)} %bitcast.131, bf16[896,1024]{1,0:T(8,128)(2,1)S(1)} %bitcast_multiply_fusion), kind=kOutput, calls=%fused_computation.62 | convolution fusion | flops 1409286144 | bytes 6160384 | tf_op jit(solution)/shard_map/dot_general | solution.py:288
  48.6 11.5 %shard_map.122 = bf16[3,24,1024]{2,1,0:T(8,128)(2,1)} custom-call(bf16[24,1024]{1,0:T(8,128)(2,1)} %x_ref.2), custom_call_target="tpu_custom_call" | custom-call | tf_op jit(solution)/shard_map/pallas_call | solution.py:194
  60.1 1.6 fusion.20
  61.7 13.1 %shard_map.123 = bf16[3,4,24,1024]{3,2,1,0:T(8,128)(2,1)} custom-call(bf16[4,24,1024]{2,1,0:T(8,128)(2,1)} %get-tuple-element.43.x_ref), custom_call_target="tpu_custom_call" | custom-call | tf_op jit(solution)/shard_map/pallas_call | solution.py:194
  74.8 2.1 fusion.22
  76.9 2.8 shard_map.124
  79.7 2.9 copy.17
  82.8 3.8 %copy.15 = bf16[1024,896]{0,1:T(8,128)(2,1)} copy(bf16[1024,896]{1,0:T(8,128)(2,1)} %param.9) | data formatting | bytes 3670016 | tf_op args[1]
  86.8 1.8 bitcast_multiply_fusion.1
  88.8 1.0 copy-done.13
  90.5 3.1 fusion.4
  93.6 1.9 fusion.24
  95.5 1.7 copy.18
  97.2 34.0 %shard_map.125 = (f32[3,192,896]{2,1,0:T(8,128)}, f32[1,384,896]{2,1,0:T(8,128)}) custom-call(f32[4,192,896]{2,1,0:T(8,128)} %bitcast.111, f32[2,384,896]{2,1,0:T(8,128)} %bitcast.107), custom_call_target="tpu_custom_call" | custom-call | tf_op jit(solution)/shard_map/pallas_call | solution.py:127
  131.2 1.8 reduce_sum.80
  133.0 1.3 constant_dynamic-slice_fusion
  134.3 1.0 add.86.refs_0_
  135.3 2.6 dynamic-slice_add_fusion
  137.8 18.9 %shard_map.126 = (f32[1,96,896]{2,1,0:T(8,128)}, f32[3,96,896]{2,1,0:T(8,128)}) custom-call(f32[2,96,896]{2,1,0:T(8,128)} %add.86.refs_0_, f32[4,96,896]{2,1,0:T(8,128)} %bitcast.123), custom_call_target="tpu_custom_call" | custom-call | tf_op jit(solution)/shard_map/pallas_call | solution.py:127
  156.7 1.3 reduce_sum.82
  158.1 1.4 fusion.15
  160.2 7.4 %shard_map.127 = (bf16[2,96,448]{2,1,0:T(8,128)(2,1)}, bf16[4,96,448]{2,1,0:T(8,128)(2,1)}) custom-call(bf16[96,448]{1,0:T(8,128)(2,1)} %get-tuple-element.49.refs_0_, bf16[96,448]{1,0:T(8,128)(2,1)} %get-tuple-element.48.refs_1_), custom_call_target="tpu_custom_call" | custom-call | tf_op jit(solution)/shard_map/pallas_call | solution.py:127
  168.3 12.3 %shard_map.128 = (bf16[4,2,96,448]{3,2,1,0:T(8,128)(2,1)}, bf16[2,4,96,448]{3,2,1,0:T(8,128)(2,1)}) custom-call(bf16[2,96,448]{2,1,0:T(8,128)(2,1)} %get-tuple-element.47.refs_0_, bf16[4,96,448]{2,1,0:T(8,128)(2,1)} %get-tuple-element.46.refs_1_), custom_call_target="tpu_custom_call" | custom-call | tf_op jit(solution)/shard_map/pallas_call | solution.py:127
  180.6 1.7 bitcast_dynamic-update-slice_fusion.1
  182.3 1.2 copy.19
  183.6 0.8 pad_maximum_fusion.7
  184.9 2.5 copy.21
  187.6 2.5 copy.20
  190.1 2.3 fusion.6
  192.4 1.0 convolution_add_fusion
  193.4 1.3 slice.68
  194.8 0.8 copy-done
  195.6 5.6 %shard_map.129 = f32[1,384,1024]{2,1,0:T(8,128)} custom-call(f32[2,384,1024]{2,1,0:T(8,128)} %bitcast.106), custom_call_target="tpu_custom_call" | custom-call | tf_op jit(solution)/shard_map/pallas_call | solution.py:194
  201.1 3.4 %add.96.x_ref = f32[4,96,1024]{2,1,0:T(8,128)} add(f32[4,96,1024]{2,1,0:T(8,128)} %bitcast.114, f32[4,96,1024]{2,1,0:T(8,128)} %bitcast.115) | non-fusion elementwise | flops 393216 | bytes 4718592 | tf_op jit(solution)/shard_map/add | solution.py:216
  204.6 20.6 %shard_map.130 = f32[3,96,1024]{2,1,0:T(8,128)} custom-call(f32[4,96,1024]{2,1,0:T(8,128)} %add.96.x_ref), custom_call_target="tpu_custom_call" | custom-call | tf_op jit(solution)/shard_map/pallas_call | solution.py:194
  225.2 1.4 reduce_sum.85
  226.6 2.1 fusion.9
  228.7 12.5 %shard_map.131 = f32[3,24,1024]{2,1,0:T(8,128)} custom-call(f32[4,24,1024]{2,1,0:T(8,128)} %bitcast.130), custom_call_target="tpu_custom_call" | custom-call | tf_op jit(solution)/shard_map/pallas_call | solution.py:194
  241.1 1.0 reduce_sum.86
  242.1 1.5 fusion.17
  243.7 0.9 fusion.29
  244.8 0.9 fusion.28
  246.3 2.2 fusion.2
  248.5 5.3 %fusion.3 = f32[768,1024]{1,0:T(8,128)S(1)} fusion(bf16[768,1792]{1,0:T(8,128)(2,1)} %all-gather.2.cloned.1.call-done, bf16[1024,896]{0,1:T(8,128)(2,1)S(1)} %copy-done.14, bf16[1024,896]{0,1:T(8,128)(2,1)} %copy-done.15), kind=kOutput, calls=%fused_computation.7 | convolution fusion | flops 2825912320 | bytes 9568256 | tf_op jit(solution)/shard_map/dot_general | solution.py:306
  253.8 1.7 copy-done.8
  255.6 6.9 %shard_map.132 = f32[1,384,1024]{2,1,0:T(8,128)} custom-call(f32[2,384,1024]{2,1,0:T(8,128)} %bitcast.122), custom_call_target="tpu_custom_call" | custom-call | tf_op jit(solution)/shard_map/pallas_call | solution.py:194
  262.5 2.8 add.102.x_ref
  265.3 20.7 %shard_map.133 = f32[3,96,1024]{2,1,0:T(8,128)} custom-call(f32[4,96,1024]{2,1,0:T(8,128)} %add.102.x_ref), custom_call_target="tpu_custom_call" | custom-call | tf_op jit(solution)/shard_map/pallas_call | solution.py:194
  286.0 1.4 reduce_sum.89
  287.4 1.9 fusion.8
  289.3 12.5 %shard_map.134 = f32[3,24,1024]{2,1,0:T(8,128)} custom-call(f32[4,24,1024]{2,1,0:T(8,128)} %bitcast.129), custom_call_target="tpu_custom_call" | custom-call | tf_op jit(solution)/shard_map/pallas_call | solution.py:194
  301.8 1.0 reduce_sum.90
  302.8 1.5 fusion.16
  304.4 5.1 %fusion.27 = f32[1024,1792]{1,0:T(8,128)S(1)} fusion(bf16[768,1024]{1,0:T(8,128)(2,1)S(1)} %bitcast.135, bf16[768,1792]{1,0:T(8,128)(2,1)} %all-gather.2.cloned.1.call-done), kind=kOutput, calls=%fused_computation.63 | convolution fusion | flops 2818572288 | bytes 11665408 | tf_op jit(solution)/shard_map/dot_general | solution.py:311
  309.4 2.7 fusion
  (79 shorter events, 5.1 us)
Async XLA Ops:
  7.2 150.9 %reduce-scatter.2.cloned.1.call-start = ((), (), s32[]{:S(2)}) async-start(), calls=%async_computation.1 | async-start | bytes 3096576 | tf_op jit(solution)/shard_map/reduce_scatter | solution.py:290
  34.5 5.4 %copy-start.27 = (s32[7,8]{1,0:T(8,128)S(1)}, s32[7,8]{1,0:T(8,128)}, u32[]{:S(2)}) copy-start(s32[7,8]{1,0:T(8,128)} %param.14) | copy-start | bytes 676
  41.2 2.4 copy-start.17
  41.3 2.1 copy-start.16
  42.4 1.3 copy-start.2
  43.7 1.2 copy-start.6
  48.3 11.7 %copy-start.26 = (bf16[24,1024]{1,0:T(8,128)(2,1)S(1)}, bf16[24,1024]{1,0:T(8,128)(2,1)}, u32[]{:S(2)}) copy-start(bf16[24,1024]{1,0:T(8,128)(2,1)} %x_ref.2) | copy-start | bytes 147460
  48.3 200.1 %all-gather.2.cloned.1.call-start = ((), (), s32[]{:S(2)}) async-start(), calls=%async_computation.2 | async-start | bytes 3096576 | tf_op jit(solution)/shard_map/all_gather | solution.py:304
  79.6 2.9 copy-start.28
  82.8 3.8 %copy-start.29 = (s32[8,7]{1,0:T(8,128)S(1)}, s32[8,7]{1,0:T(8,128)}, u32[]{:S(2)}) copy-start(s32[8,7]{1,0:T(8,128)} %param.12) | copy-start | bytes 676
  86.8 1.9 copy-start.12
  88.6 1.2 copy-start.13
  88.7 1.9 copy-start.15
  88.8 4.8 %copy-start.19 = (bf16[2,4,4,24,1024]{4,3,2,1,0:T(8,128)(2,1)}, bf16[2,4,4,24,1024]{4,3,2,1,0:T(8,128)(2,1)S(1)}, u32[]{:S(2)}) copy-start(bf16[2,4,4,24,1024]{4,3,2,1,0:T(8,128)(2,1)S(1)} %pad_maximum_fusion.4) | copy-start | bytes 4718596
  133.0 2.3 copy-start.1
  137.8 20.2 %copy-start.11 = (f32[2,96,896]{2,1,0:T(8,128)S(1)}, f32[2,96,896]{2,1,0:T(8,128)}, u32[]{:S(2)}) copy-start(f32[2,96,896]{2,1,0:T(8,128)} %add.86.refs_0_) | copy-start | bytes 2064388
  168.3 15.2 %copy-start.21 = (bf16[4,96,448]{2,1,0:T(8,128)(2,1)S(1)}, bf16[4,96,448]{2,1,0:T(8,128)(2,1)}, u32[]{:S(2)}) copy-start(bf16[4,96,448]{2,1,0:T(8,128)(2,1)} %get-tuple-element.46.refs_1_) | copy-start | bytes 1032196
  180.6 2.9 copy-start.22
  183.5 6.6 %copy-start.9 = (bf16[2,4,96,448]{3,2,1,0:T(8,128)(2,1)}, bf16[2,4,96,448]{3,2,1,0:T(8,128)(2,1)S(1)}, u32[]{:S(2)}) copy-start(bf16[2,4,96,448]{3,2,1,0:T(8,128)(2,1)S(1)} %copy.19) | copy-start | bytes 2064388
  183.6 1.1 copy-start.23
  190.1 2.3 copy-start.7
  190.1 2.3 copy-start.24
  193.4 2.1 copy-start
  226.6 17.1 %copy-start.18 = (bf16[2,4,4,24,1024]{4,3,2,1,0:T(8,128)(2,1)S(1)}, bf16[2,4,4,24,1024]{4,3,2,1,0:T(8,128)(2,1)}, u32[]{:S(2)}) copy-start(bf16[2,4,4,24,1024]{4,3,2,1,0:T(8,128)(2,1)} %copy-done.17) | copy-start | bytes 4718596
  226.6 17.1 %copy-start.25 = (bf16[2,4,96,448]{3,2,1,0:T(8,128)(2,1)S(1)}, bf16[2,4,96,448]{3,2,1,0:T(8,128)(2,1)}, u32[]{:S(2)}) copy-start(bf16[2,4,96,448]{3,2,1,0:T(8,128)(2,1)} %copy-done.23) | copy-start | bytes 2064388
  243.7 1.1 copy-start.10
  244.8 1.5 copy-start.3
  246.3 2.2 copy-start.14
  253.8 1.7 copy-start.8
  287.4 16.9 %copy-start.20 = (bf16[2,4,4,24,1024]{4,3,2,1,0:T(8,128)(2,1)S(1)}, bf16[2,4,4,24,1024]{4,3,2,1,0:T(8,128)(2,1)}, u32[]{:S(2)}) copy-start(bf16[2,4,4,24,1024]{4,3,2,1,0:T(8,128)(2,1)} %copy-done.19) | copy-start | bytes 4718596
  304.3 5.1 %copy-start.4 = (bf16[1024,896]{1,0:T(8,128)(2,1)S(1)}, bf16[1024,896]{1,0:T(8,128)(2,1)}, u32[]{:S(2)}) copy-start(bf16[1024,896]{1,0:T(8,128)(2,1)} %copy.21) | copy-start | bytes 5505028
  304.3 5.1 %copy-start.5 = (bf16[1024,896]{1,0:T(8,128)(2,1)S(1)}, bf16[1024,896]{1,0:T(8,128)(2,1)}, u32[]{:S(2)}) copy-start(bf16[1024,896]{1,0:T(8,128)(2,1)} %copy.20) | copy-start | bytes 5505028
Sparse Core Ops, SparseCore 0:
  48.5 42.6 reduce-scatter.1
  184.8 39.8 all-gather.1
